TPU v7x, 32 devices: a whole 2x2x4 slice. The times are simulated.
32 devices in a mesh: rows: 8 (over z, x), cols: 4 (over y, core).
Axes of the slice: x: 2, y: 2, z: 4, core: 2. Of those that a mesh axis runs over, the one named last changes fastest.
Arguments:
- row_features: float32 [4096, 64], P('rows'), may hold values from -6 to 6, as said below
- col_features: float32 [16384, 64], P('cols'), may hold values from -6 to 6, as said below
- test_block: bfloat16 [16384, 256], P('cols'), may hold values from -0.046875 to 0.046875, as said below
Outputs:
- basis: float32 [4096, 256], P('rows', 'cols')
- projected: float32 [256, 16384], P('rows', 'cols')
Inputs may be any that keep to these rules, and one draw needn't show every extreme that they name: `row_features`: independent entries of mean zero and unit variance. `col_features`: independent entries of mean zero and unit variance. `test_block`: independent entries of mean zero and variance 1 / 16384.
All inputs are finite; a program needn't handle non-finite values.
Results may differ from a plain program's by a relative error of at most 0.0095.
Values may be sent and summed in bfloat16 or wider, within the bound.
No kernel may reach another device: no remote copies, remote signals or barrier semaphores. Data moves between devices by JAX's collectives and lax.ppermute only.
A program may use at most 64 MiB of HBM per device.

v0:
```python
import math

import jax
import jax.numpy as jnp
from jax import lax
from jax.experimental import pallas as pl
from jax.experimental.pallas import tpu as pltpu
from jax.sharding import PartitionSpec as P


F32 = jnp.float32
BF16 = jnp.bfloat16
NN = ((1,), (0,))
NT = ((1,), (1,))
TN = ((0,), (0,))


def mm(a, b, dims, precision=None):
    return lax.dot_general(
        a, b, (dims, ((), ())), precision=precision, preferred_element_type=F32
    )


def split(a):
    high = a.astype(BF16)
    return high, (a - high.astype(F32)).astype(BF16)


def cube(inner):
    shifted = inner + 1.0
    return (shifted * shifted * shifted).astype(BF16)


def factor_inverse(rows, n):
    blocks = n // 8
    lane = lax.broadcasted_iota(jnp.int32, (8, n), 1)
    sub = lax.broadcasted_iota(jnp.int32, (8, n), 0)
    rows = list(rows)
    done = []

    def row_of(a, t):
        return jnp.broadcast_to(a[t : t + 1, :], (8, n))

    for g in range(blocks):
        first = 8 * g
        inside = (lane >= first) & (lane < first + 8)
        pivot = jnp.where(inside, jnp.where(lane == sub + first, 1.0, 0.0), rows[g])
        column = [
            [jnp.broadcast_to(rows[v][:, first + k : first + k + 1], (8, n)) for k in range(8)]
            for v in range(g, blocks)
        ]
        factor = [[None] * 8 for _ in range(g, blocks)]
        diagonal = jnp.zeros((8, n), F32)
        for t in range(8):
            d = row_of(column[0][t], t)
            diagonal = jnp.where(sub == t, d, diagonal)
            r = 1.0 / d
            own = jnp.where(sub > t, column[0][t] * r, 0.0)
            for v in range(1, blocks - g):
                factor[v][t] = column[v][t] * r
            for k in range(t + 1, 8):
                e = row_of(column[0][k], t)
                column[0][k] = column[0][k] - own * e
                for v in range(1, blocks - g):
                    column[v][k] = column[v][k] - factor[v][t] * e
            pivot = pivot - own * row_of(pivot, t)
        pivots = [row_of(pivot, t) for t in range(8)]
        for v in range(1, blocks - g):
            m = jnp.where(inside, 0.0, rows[g + v])
            for t in range(8):
                m = m - factor[v][t] * pivots[t]
            rows[g + v] = m
        done.append(jnp.where(lane <= sub + first, pivot, 0.0) * lax.rsqrt(diagonal))
    return jnp.concatenate(done, axis=0)


def inverse_factor(gram, base=128):
    n = gram.shape[0]
    if n <= base:
        return factor_inverse([gram[8 * i : 8 * i + 8, :] for i in range(n // 8)], n)
    k = n // 2
    high = lax.Precision.HIGHEST
    w11 = inverse_factor(gram[:k, :k], base)
    l21 = mm(gram[k:, :k], w11, NT, high)
    w22 = inverse_factor(gram[k:, k:] - mm(l21, l21, NT, high), base)
    w21 = -mm(w22, mm(l21, w11, NN, high), NN, high)
    top = jnp.concatenate([w11, jnp.zeros((k, n - k), F32)], axis=1)
    return jnp.concatenate([top, jnp.concatenate([w21, w22], axis=1)], axis=0)


def sketch_kernel(scale, x_ref, y_ref, t_ref, mine_ref, given_ref, pairs_ref, x4, total):
    step = pl.program_id(0)

    @pl.when(step == 0)
    def _():
        pairs = jnp.concatenate(split(x_ref[...] * scale), axis=0).T
        x4[...] = jnp.concatenate([pairs, pairs], axis=1)
        pairs_ref[...] = pairs

    high, low = split(y_ref[...])
    y4 = jnp.concatenate([high, high, low, low], axis=0)
    part = mm(cube(mm(x4[...], y4, NN)), t_ref[...], NN)

    @pl.when(step == 0)
    def _():
        total[...] = part

    @pl.when(step > 0)
    def _():
        total[...] += part

    @pl.when(step == pl.num_programs(0) - 1)
    def _():
        half = mine_ref.shape[0]
        core = lax.axis_index("cols") % 2
        mine_ref[...] = total[pl.ds(pl.multiple_of(core * half, half), half), :]
        given_ref[...] = total[pl.ds(pl.multiple_of((1 - core) * half, half), half), :]


def sketch_call(x_t, y_t, test, scale):
    width, rows = x_t.shape
    cols, columns = test.shape
    tile = 1024
    whole = lambda shape: pl.BlockSpec(shape, lambda j: (0, 0))
    return pl.pallas_call(
        lambda *refs: sketch_kernel(scale, *refs),
        grid=(cols // tile,),
        in_specs=[
            whole((width, rows)),
            pl.BlockSpec((width, tile), lambda j: (0, j)),
            pl.BlockSpec((tile, columns), lambda j: (j, 0)),
        ],
        out_specs=[
            whole((rows // 2, columns)),
            whole((rows // 2, columns)),
            whole((rows, 2 * width)),
        ],
        out_shape=[
            jax.ShapeDtypeStruct((rows // 2, columns), F32),
            jax.ShapeDtypeStruct((rows // 2, columns), F32),
            jax.ShapeDtypeStruct((rows, 2 * width), BF16),
        ],
        scratch_shapes=[pltpu.VMEM((rows, 4 * width), BF16), pltpu.VMEM((rows, columns), F32)],
        name="sketch_tile",
    )(x_t, y_t, test)


def product_kernel(columns, count, first, *refs):
    pieces, refs = refs[:count], refs[count:]
    y_ref, refs = refs[0], refs[1:]
    (z_in, g_in), (z_ref, g_ref) = ((None, None), refs) if first else (refs[:2], refs[2:])
    m = pl.program_id(0)
    tile = z_ref.shape[0]
    start = (lax.axis_index("rows") % 2) * (y_ref.shape[1] // 2) + m * tile
    high, low = split(y_ref[:, pl.ds(pl.multiple_of(start, tile), tile)])
    y4 = jnp.concatenate([high, high, low, low], axis=0).T
    total = None if first else z_in[...]
    for piece in pieces:
        pairs = piece[:, columns:]
        k = cube(mm(y4, jnp.concatenate([pairs, pairs], axis=1), NT))
        part = mm(k, piece[:, :columns], NN)
        total = part if total is None else total + part
    z_ref[...] = total

    @pl.when(m == 0)
    def _():
        gram = None if first else g_in[...]
        for piece in pieces:
            s = piece[:, :columns]
            part = mm(s, s, TN)
            gram = part if gram is None else gram + part
        g_ref[...] = gram


def product_call(pieces, y_t, columns, carry=None):
    cols = y_t.shape[1] // 2
    tile = 1024
    first = carry is None
    whole = lambda shape: pl.BlockSpec(shape, lambda m: (0, 0))
    z_spec = pl.BlockSpec((tile, columns), lambda m: (m, 0))
    g_spec = whole((columns, columns))
    return pl.pallas_call(
        lambda *refs: product_kernel(columns, len(pieces), first, *refs),
        grid=(cols // tile,),
        in_specs=[whole(a.shape) for a in pieces]
        + [whole(y_t.shape)]
        + ([] if first else [z_spec, g_spec]),
        out_specs=[z_spec, g_spec],
        out_shape=[
            jax.ShapeDtypeStruct((cols, columns), F32),
            jax.ShapeDtypeStruct((columns, columns), F32),
        ],
        cost_estimate=pl.CostEstimate(
            flops=2 * cols * sum(a.shape[0] for a in pieces) * (columns + 4 * y_t.shape[0]),
            bytes_accessed=4 * (2 * cols * columns + y_t.size) + 2 * sum(a.size for a in pieces),
            transcendentals=0,
        ),
        name="kernel_times_sketch",
    )(*pieces, y_t, *(() if first else carry))


def final_kernel(places, g_ref, z_ref, *refs):
    pieces, (basis_ref, projected_ref, given_ref, w, s) = refs[: len(places)], refs[len(places) :]
    quarter = pieces[0].shape[0]
    for place, piece in zip(places, pieces):
        s[pl.ds(pl.multiple_of(place() * quarter, quarter), quarter), :] = piece[...]
    w[...] = inverse_factor(g_ref[...])
    own_r, own_c = projected_ref.shape[0], basis_ref.shape[0]
    ir, ic = lax.axis_index("rows"), lax.axis_index("cols")

    def rows_of(i, n):
        return split(w[pl.ds(pl.multiple_of(i * n, n), n), :])

    both = mm(jnp.concatenate(rows_of(ic, own_c), axis=0), s[...], NT)
    basis_ref[...] = both[:own_c] + both[own_c:]
    mine, given = rows_of(ir, own_r), rows_of(ir ^ 1, own_r)
    tall = jnp.concatenate([mine[0], given[0], mine[1], given[1]], axis=0)
    cols = z_ref.shape[0]
    start = (ir % 2) * cols
    tile = 512
    for j in range(cols // tile):
        high, low = split(z_ref[tile * j : tile * (j + 1), :])
        both = mm(tall, high, NT)
        both = both[: 2 * own_r] + both[2 * own_r :] + mm(tall[: 2 * own_r], low, NT)
        there = pl.ds(pl.multiple_of(start + tile * j, tile), tile)
        projected_ref[:, there] = both[:own_r]
        given_ref[:, tile * j : tile * (j + 1)] = both[own_r:].astype(BF16)


def final_call(gram, z, pieces, places, quarter, own_r, own_c):
    columns = gram.shape[0]
    whole = lambda shape: pl.BlockSpec(shape, lambda i: (0, 0))
    height = quarter * len(pieces)
    cols = z.shape[0]
    return pl.pallas_call(
        lambda *refs: final_kernel(places, *refs),
        grid=(1,),
        in_specs=[whole(gram.shape), whole(z.shape)] + [whole((quarter, columns)) for _ in pieces],
        out_specs=[whole((own_c, height)), whole((own_r, 2 * cols)), whole((own_r, cols))],
        out_shape=[
            jax.ShapeDtypeStruct((own_c, height), F32),
            jax.ShapeDtypeStruct((own_r, 2 * cols), F32),
            jax.ShapeDtypeStruct((own_r, cols), BF16),
        ],
        scratch_shapes=[pltpu.VMEM((columns, columns), F32), pltpu.VMEM((height, columns), BF16)],
        name="factor_and_project",
    )(gram, z, *pieces)


def swap(a, axis, bits):
    return lax.ppermute(a, axis, [(i, i ^ bits) for i in range(lax.axis_size(axis))])


def local(row_features, col_features, test_block):
    cols = lax.axis_size("cols")
    rows = lax.axis_size("rows")
    chips_y, chips_z = cols // 2, rows // 2
    ir, ic = lax.axis_index("rows"), lax.axis_index("cols")
    core, iy = ic % 2, ic // 2
    height, width = row_features.shape
    scale = 1.0 / math.sqrt(width)
    columns = test_block.shape[1]
    half = height // 2
    quarter = half // chips_y

    x_t, y_t = row_features.T, col_features.T
    mine, given, pairs = sketch_call(x_t, y_t, test_block, scale)
    mine = mine + swap(given, "cols", 1)
    s_own = lax.dynamic_slice_in_dim(mine, iy * quarter, quarter, 0)
    for d in range(1, chips_y):
        given = lax.dynamic_slice_in_dim(mine, (iy ^ d) * quarter, quarter, 0)
        s_own = s_own + swap(given, "cols", 2 * d)
    pairs = lax.dynamic_slice_in_dim(pairs, core * half + iy * quarter, quarter, 0)
    piece = jnp.concatenate([s_own.astype(BF16), pairs], axis=1)

    own = jnp.concatenate([piece] + [swap(piece, "rows", 2 * d) for d in range(1, chips_z)], 0)
    near_x = swap(own, "rows", 1)
    near_y = [swap(own, "cols", 2 * d) for d in range(1, chips_y)]
    own_core = swap(own, "cols", 1)
    carry = product_call([own, own_core], y_t, columns)
    cut = own.shape[0] // 2
    far = []
    for d in range(1, chips_y):
        far.append(swap(near_y[d - 1][:cut], "rows", 1))
        far.append(swap(near_x[cut:], "cols", 2 * d))
    near = [near_x] + near_y
    near_core = [swap(a, "cols", 1) for a in near]
    carry = product_call(near + near_core, y_t, columns, carry)
    far_core = [swap(a, "cols", 1) for a in far]
    z, gram = product_call(far + far_core, y_t, columns, carry)

    pieces, places = [], []
    for k, group in enumerate(([own] + near_y, [own_core] + near_core[1:])):
        for d, a in enumerate(group):
            pieces.append(a)

            def place(k=k, d=d):
                c = lax.axis_index("cols")
                return ((c % 2) ^ k) * chips_y + ((c // 2) ^ d)

            places.append(place)
    basis_t, projected, given = final_call(
        gram, z, pieces, places, quarter, columns // rows, columns // cols
    )
    there = swap(given, "rows", 1).astype(F32)
    projected = lax.dynamic_update_slice_in_dim(
        projected, there, (1 - ir % 2) * there.shape[1], 1
    )
    return (basis_t.T, projected)


def solution(mesh):
    in_specs = (P("rows", None), P("cols", None), P("cols", None))
    out_specs = (P("rows", "cols"), P("rows", "cols"))
    return jax.shard_map(local, mesh=mesh, in_specs=in_specs, out_specs=out_specs, check_vma=False)
```

profile of v0, /device:TPU:0, one launch (start us, length us, event | category | flops | bytes accessed | tf_op | source)
XLA Modules:
  0.0 83.8 jit_solution(775766083842622489)
XLA Ops:
  0.6 5.9 %sketch_tile.1 = (f32[256,256]{1,0:T(8,128)}, f32[256,256]{1,0:T(8,128)}, bf16[512,128]{1,0:T(8,128)(2,1)}) custom-call(f32[64,512]{1,0:T(8,128)} %bitcast.7, f32[64,4096]{1,0:T(8,128)} %bitcast.3, bf16[4096,256]{1,0:T(8,128)(2,1)} %refs_2_.1), custom_call_target="tpu_custom_call" | custom-call | tf_op jit(solution)/shard_map/sketch_tile/pallas_call | solution.py:125
  6.6 0.5 collective-permute-start
  7.1 1.4 %collective-permute-done = f32[256,256]{1,0:T(8,128)S(1)} collective-permute-done((f32[256,256]{1,0:T(8,128)}, f32[256,256]{1,0:T(8,128)S(1)}, u32[]{:S(2)}, u32[]{:S(2)}) %collective-permute-start) | collective-permute-done | bytes 262176 | tf_op jit(solution)/shard_map/ppermute | solution.py:251
  8.4 1.0 %add.29 = f32[256,256]{1,0:T(8,128)S(1)} add(f32[256,256]{1,0:T(8,128)} %get-tuple-element.14, f32[256,256]{1,0:T(8,128)S(1)} %collective-permute-done) | non-fusion elementwise | flops 65536 | bytes 786432 | tf_op jit(solution)/shard_map/add | solution.py:268
  9.4 2.9 %collective-permute-start.1 = (f32[128,256]{1,0:T(8,128)S(1)}, f32[128,256]{1,0:T(8,128)S(1)}, u32[]{:S(2)}, u32[]{:S(2)}) collective-permute-start(f32[128,256]{1,0:T(8,128)S(1)} %constant_dynamic-slice_fusion.1), channel_id=1, source_target_pairs={{0,2},{1,3},{2,0},{3,1},{4,6},{5,7},{6,4},{7,5},{8,10},{9,11},{10,... | collective-permute-start | bytes 393224 | tf_op jit(solution)/shard_map/ppermute | solution.py:251
  12.4 0.8 constant_dynamic-slice_fusion
  13.1 3.0 %collective-permute-done.1 = f32[128,256]{1,0:T(8,128)S(1)} collective-permute-done((f32[128,256]{1,0:T(8,128)S(1)}, f32[128,256]{1,0:T(8,128)S(1)}, u32[]{:S(2)}, u32[]{:S(2)}) %collective-permute-start.1) | collective-permute-done | bytes 131104 | tf_op jit(solution)/shard_map/ppermute | solution.py:251
  16.2 1.9 %collective-permute-start.2 = (bf16[128,384]{1,0:T(8,128)(2,1)S(1)}, bf16[128,384]{1,0:T(8,128)(2,1)S(1)}, u32[]{:S(2)}, u32[]{:S(2)}) collective-permute-start(bf16[128,384]{1,0:T(8,128)(2,1)S(1)} %pad_maximum_fusion.1), channel_id=1, source_target_pairs={{0,8},{4,12},{8,0},{12,4},{16,24},{20,28},{24,16},{28,20},{1,9},{5... | collective-permute-start | bytes 294920 | tf_op jit(solution)/shard_map/ppermute | solution.py:251
  18.1 2.6 %collective-permute-start.3 = (bf16[128,384]{1,0:T(8,128)(2,1)S(1)}, bf16[128,384]{1,0:T(8,128)(2,1)S(1)}, u32[]{:S(2)}, u32[]{:S(2)}) collective-permute-start(bf16[128,384]{1,0:T(8,128)(2,1)S(1)} %pad_maximum_fusion.1), channel_id=1, source_target_pairs={{0,16},{4,20},{8,24},{12,28},{16,0},{20,4},{24,8},{28,12},{1,17},{... | collective-permute-start | bytes 294920 | tf_op jit(solution)/shard_map/ppermute | solution.py:251
  20.7 0.0 collective-permute-start.4
  20.7 1.2 %collective-permute-done.2 = bf16[128,384]{1,0:T(8,128)(2,1)S(1)} collective-permute-done((bf16[128,384]{1,0:T(8,128)(2,1)S(1)}, bf16[128,384]{1,0:T(8,128)(2,1)S(1)}, u32[]{:S(2)}, u32[]{:S(2)}) %collective-permute-start.2) | collective-permute-done | bytes 98336 | tf_op jit(solution)/shard_map/ppermute | solution.py:251
  21.9 6.1 %collective-permute-done.3 = bf16[128,384]{1,0:T(8,128)(2,1)S(1)} collective-permute-done((bf16[128,384]{1,0:T(8,128)(2,1)S(1)}, bf16[128,384]{1,0:T(8,128)(2,1)S(1)}, u32[]{:S(2)}, u32[]{:S(2)}) %collective-permute-start.3) | collective-permute-done | bytes 98336 | tf_op jit(solution)/shard_map/ppermute | solution.py:251
  27.9 0.0 collective-permute-done.4
  28.0 0.0 copy-start
  28.0 1.6 %collective-permute-start.7 = (bf16[512,384]{1,0:T(8,128)(2,1)S(1)}, bf16[512,384]{1,0:T(8,128)(2,1)S(1)}, u32[]{:S(2)}, u32[]{:S(2)}) collective-permute-start(bf16[512,384]{1,0:T(8,128)(2,1)S(1)} %pad_maximum_fusion.refs_0_.refs_2_), channel_id=1, source_target_pairs={{0,4},{4,0},{8,12},{12,8},{16,20},{20,16},{24,28},{28,24},{1,5},{5... | collective-permute-start | bytes 1179656 | tf_op jit(solution)/shard_map/ppermute | solution.py:251
  29.6 1.5 %collective-permute-start.5 = (bf16[512,384]{1,0:T(8,128)(2,1)S(1)}, bf16[512,384]{1,0:T(8,128)(2,1)S(1)}, u32[]{:S(2)}, u32[]{:S(2)}) collective-permute-start(bf16[512,384]{1,0:T(8,128)(2,1)S(1)} %pad_maximum_fusion.refs_0_.refs_2_), channel_id=1, source_target_pairs={{0,2},{1,3},{2,0},{3,1},{4,6},{5,7},{6,4},{7,5},{8,10},{9,11},{10,... | collective-permute-start | bytes 1179656 | tf_op jit(solution)/shard_map/ppermute | solution.py:251
  31.1 0.0 collective-permute-start.13
  31.1 5.6 %collective-permute-done.7.refs_0_ = bf16[512,384]{1,0:T(8,128)(2,1)S(1)} collective-permute-done((bf16[512,384]{1,0:T(8,128)(2,1)S(1)}, bf16[512,384]{1,0:T(8,128)(2,1)S(1)}, u32[]{:S(2)}, u32[]{:S(2)}) %collective-permute-start.7) | collective-permute-done | bytes 393248 | tf_op jit(solution)/shard_map/ppermute | solution.py:251
  36.7 0.0 collective-permute-start.11
  36.7 1.2 %collective-permute-done.5.refs_1_.refs_3_ = bf16[512,384]{1,0:T(8,128)(2,1)S(1)} collective-permute-done((bf16[512,384]{1,0:T(8,128)(2,1)S(1)}, bf16[512,384]{1,0:T(8,128)(2,1)S(1)}, u32[]{:S(2)}, u32[]{:S(2)}) %collective-permute-start.5) | collective-permute-done | bytes 393248 | tf_op jit(solution)/shard_map/ppermute | solution.py:251
  37.9 0.0 collective-permute-start.12
  38.0 1.6 %collective-permute-start.8 = (bf16[256,384]{1,0:T(8,128)(2,1)S(1)}, bf16[256,384]{1,0:T(8,128)(2,1)S(1)}, u32[]{:S(2)}, u32[]{:S(2)}) collective-permute-start(bf16[256,384]{1,0:T(8,128)(2,1)S(1)} %slice.9), channel_id=1, source_target_pairs={{0,2},{1,3},{2,0},{3,1},{4,6},{5,7},{6,4},{7,5},{8,10},{9,11},{10,... | collective-permute-start | bytes 589832 | tf_op jit(solution)/shard_map/ppermute | solution.py:251
  39.6 0.9 %collective-permute-start.6 = (bf16[256,384]{1,0:T(8,128)(2,1)S(1)}, bf16[256,384]{1,0:T(8,128)(2,1)S(1)}, u32[]{:S(2)}, u32[]{:S(2)}) collective-permute-start(bf16[256,384]{1,0:T(8,128)(2,1)S(1)} %slice.8), channel_id=1, source_target_pairs={{0,4},{4,0},{8,12},{12,8},{16,20},{20,16},{24,28},{28,24},{1,5},{5... | collective-permute-start | bytes 589832 | tf_op jit(solution)/shard_map/ppermute | solution.py:251
  40.4 0.0 collective-permute-done.13.refs_1_.refs_4_
  40.5 0.0 copy-done
  40.5 0.8 copy-done.2
  41.2 6.8 %kernel_times_sketch.3 = (f32[2048,256]{1,0:T(8,128)}, f32[256,256]{1,0:T(8,128)}) custom-call(bf16[512,384]{1,0:T(8,128)(2,1)} %copy-done, bf16[512,384]{1,0:T(8,128)(2,1)} %copy-done.2, f32[64,4096]{1,0:T(8,128)} %bitcast.4), custom_call_target="tpu_custom_call" | custom-call | flops 2147483648 | bytes 6029312 | tf_op jit(solution)/shard_map/kernel_times_sketch/pallas_call | solution.py:182
  48.0 0.0 copy-done.1
  48.0 0.0 collective-permute-done.8.refs_1_
  48.0 0.1 collective-permute-start.10
  48.1 0.0 collective-permute-done.6.refs_0_
  48.1 0.5 collective-permute-start.9
  48.6 0.0 collective-permute-done.11.refs_2_
  48.6 0.0 collective-permute-done.12.refs_3_.refs_5_
  48.6 0.7 copy-done.5
  49.4 0.1 copy-done.3
  49.5 8.6 %kernel_times_sketch.4 = (f32[2048,256]{1,0:T(8,128)}, f32[256,256]{1,0:T(8,128)}) custom-call(bf16[512,384]{1,0:T(8,128)(2,1)} %copy-done.4, bf16[512,384]{1,0:T(8,128)(2,1)} %copy-done.1, bf16[512,384]{1,0:T(8,128)(2,1)} %copy-done.5, bf16[512,384]{1,0:T(8,128)(2,1)} %copy-done.3, f32[64,4096]{1,0:T(8,128)} %bitcast.5, ...), custom_call_target="tpu_custom_call" | custom-call | flops 4294967296 | bytes 6815744 | tf_op jit(solution)/shard_map/kernel_times_sketch/pallas_call | solution.py:182
  58.1 0.0 copy-done.7
  58.1 0.0 collective-permute-done.10.refs_3_
  58.1 0.0 collective-permute-done.9.refs_2_
  58.1 0.0 copy-start.9
  58.1 0.7 copy-done.8
  58.8 0.0 copy-done.9
  58.8 6.1 %kernel_times_sketch.5 = (f32[2048,256]{1,0:T(8,128)}, f32[256,256]{1,0:T(8,128)}) custom-call(bf16[256,384]{1,0:T(8,128)(2,1)} %copy-done.7, bf16[256,384]{1,0:T(8,128)(2,1)} %copy-done.6, bf16[256,384]{1,0:T(8,128)(2,1)} %copy-done.9, bf16[256,384]{1,0:T(8,128)(2,1)} %copy-done.8, f32[64,4096]{1,0:T(8,128)} %bitcast.6, ...), custom_call_target="tpu_custom_call" | custom-call | flops 2147483648 | bytes 6029312 | tf_op jit(solution)/shard_map/kernel_times_sketch/pallas_call | solution.py:182
  64.9 12.4 %factor_and_project.1 = (f32[64,512]{1,0:T(8,128)}, f32[32,4096]{1,0:T(8,128)}, bf16[32,2048]{1,0:T(8,128)(2,1)}) custom-call(f32[256,256]{1,0:T(8,128)} %get-tuple-element.21.refs_0_, f32[2048,256]{1,0:T(8,128)} %get-tuple-element.22.refs_1_, bf16[512,384]{1,0:T(8,128)(2,1)} %copy-done, bf16[512,384]{1,0:T(8,128)(2,1)} %copy-done.1, ...), custom_call_target="tpu_custom_call" | custom-call | tf_op jit(solution)/shard_map/factor_and_project/pallas_call | solution.py:235
  77.4 1.2 %collective-permute-start.14 = (bf16[32,2048]{1,0:T(8,128)(2,1)}, bf16[32,2048]{1,0:T(8,128)(2,1)S(1)}, u32[]{:S(2)}, u32[]{:S(2)}) collective-permute-start(bf16[32,2048]{1,0:T(8,128)(2,1)} %get-tuple-element.25), channel_id=1, source_target_pairs={{0,4},{4,0},{8,12},{12,8},{16,20},{20,16},{24,28},{28,24},{1,5},{5... | collective-permute-start | bytes 393224 | tf_op jit(solution)/shard_map/ppermute | solution.py:251
  78.6 4.5 %collective-permute-done.14 = bf16[32,2048]{1,0:T(8,128)(2,1)S(1)} collective-permute-done((bf16[32,2048]{1,0:T(8,128)(2,1)}, bf16[32,2048]{1,0:T(8,128)(2,1)S(1)}, u32[]{:S(2)}, u32[]{:S(2)}) %collective-permute-start.14) | collective-permute-done | bytes 131104 | tf_op jit(solution)/shard_map/ppermute | solution.py:251
  83.1 0.7 convert_dynamic-update-slice_fusion
  (16 shorter events, 0.1 us)
Async XLA Ops:
  6.6 1.9 %collective-permute-start = (f32[256,256]{1,0:T(8,128)}, f32[256,256]{1,0:T(8,128)S(1)}, u32[]{:S(2)}, u32[]{:S(2)}) collective-permute-start(f32[256,256]{1,0:T(8,128)} %get-tuple-element.15), channel_id=1, source_target_pairs={{0,1},{1,0},{2,3},{3,2},{4,5},{5,4},{6,7},{7,6},{8,9},{9,8},{10,11... | collective-permute-start | bytes 786440 | tf_op jit(solution)/shard_map/ppermute | solution.py:251
  9.4 6.7 %collective-permute-start.1 = (f32[128,256]{1,0:T(8,128)S(1)}, f32[128,256]{1,0:T(8,128)S(1)}, u32[]{:S(2)}, u32[]{:S(2)}) collective-permute-start(f32[128,256]{1,0:T(8,128)S(1)} %constant_dynamic-slice_fusion.1), channel_id=1, source_target_pairs={{0,2},{1,3},{2,0},{3,1},{4,6},{5,7},{6,4},{7,5},{8,10},{9,11},{10,... | collective-permute-start | bytes 393224 | tf_op jit(solution)/shard_map/ppermute | solution.py:251
  16.2 5.7 %collective-permute-start.2 = (bf16[128,384]{1,0:T(8,128)(2,1)S(1)}, bf16[128,384]{1,0:T(8,128)(2,1)S(1)}, u32[]{:S(2)}, u32[]{:S(2)}) collective-permute-start(bf16[128,384]{1,0:T(8,128)(2,1)S(1)} %pad_maximum_fusion.1), channel_id=1, source_target_pairs={{0,8},{4,12},{8,0},{12,4},{16,24},{20,28},{24,16},{28,20},{1,9},{5... | collective-permute-start | bytes 294920 | tf_op jit(solution)/shard_map/ppermute | solution.py:251
  18.1 9.9 %collective-permute-start.3 = (bf16[128,384]{1,0:T(8,128)(2,1)S(1)}, bf16[128,384]{1,0:T(8,128)(2,1)S(1)}, u32[]{:S(2)}, u32[]{:S(2)}) collective-permute-start(bf16[128,384]{1,0:T(8,128)(2,1)S(1)} %pad_maximum_fusion.1), channel_id=1, source_target_pairs={{0,16},{4,20},{8,24},{12,28},{16,0},{20,4},{24,8},{28,12},{1,17},{... | collective-permute-start | bytes 294920 | tf_op jit(solution)/shard_map/ppermute | solution.py:251
  20.7 7.3 %collective-permute-start.4 = (bf16[128,384]{1,0:T(8,128)(2,1)S(1)}, bf16[128,384]{1,0:T(8,128)(2,1)S(1)}, u32[]{:S(2)}, u32[]{:S(2)}) collective-permute-start(bf16[128,384]{1,0:T(8,128)(2,1)S(1)} %pad_maximum_fusion.1), channel_id=1, source_target_pairs={{0,24},{4,28},{8,16},{12,20},{16,8},{20,12},{24,0},{28,4},{1,25},{... | collective-permute-start | bytes 294920 | tf_op jit(solution)/shard_map/ppermute | solution.py:251
  28.0 12.5 %copy-start = (bf16[512,384]{1,0:T(8,128)(2,1)}, bf16[512,384]{1,0:T(8,128)(2,1)S(1)}, u32[]{:S(2)}) copy-start(bf16[512,384]{1,0:T(8,128)(2,1)S(1)} %pad_maximum_fusion.refs_0_.refs_2_) | copy-start | bytes 1179652
  28.0 8.7 %collective-permute-start.7 = (bf16[512,384]{1,0:T(8,128)(2,1)S(1)}, bf16[512,384]{1,0:T(8,128)(2,1)S(1)}, u32[]{:S(2)}, u32[]{:S(2)}) collective-permute-start(bf16[512,384]{1,0:T(8,128)(2,1)S(1)} %pad_maximum_fusion.refs_0_.refs_2_), channel_id=1, source_target_pairs={{0,4},{4,0},{8,12},{12,8},{16,20},{20,16},{24,28},{28,24},{1,5},{5... | collective-permute-start | bytes 1179656 | tf_op jit(solution)/shard_map/ppermute | solution.py:251
  29.6 8.4 %collective-permute-start.5 = (bf16[512,384]{1,0:T(8,128)(2,1)S(1)}, bf16[512,384]{1,0:T(8,128)(2,1)S(1)}, u32[]{:S(2)}, u32[]{:S(2)}) collective-permute-start(bf16[512,384]{1,0:T(8,128)(2,1)S(1)} %pad_maximum_fusion.refs_0_.refs_2_), channel_id=1, source_target_pairs={{0,2},{1,3},{2,0},{3,1},{4,6},{5,7},{6,4},{7,5},{8,10},{9,11},{10,... | collective-permute-start | bytes 1179656 | tf_op jit(solution)/shard_map/ppermute | solution.py:251
  31.1 9.4 %collective-permute-start.13 = (bf16[512,384]{1,0:T(8,128)(2,1)S(1)}, bf16[512,384]{1,0:T(8,128)(2,1)S(1)}, u32[]{:S(2)}, u32[]{:S(2)}) collective-permute-start(bf16[512,384]{1,0:T(8,128)(2,1)S(1)} %pad_maximum_fusion.refs_0_.refs_2_), channel_id=1, source_target_pairs={{0,1},{1,0},{2,3},{3,2},{4,5},{5,4},{6,7},{7,6},{8,9},{9,8},{10,11... | collective-permute-start | bytes 1179656 | tf_op jit(solution)/shard_map/ppermute | solution.py:251
  36.7 11.9 %copy-start.4 = (bf16[512,384]{1,0:T(8,128)(2,1)}, bf16[512,384]{1,0:T(8,128)(2,1)S(1)}, u32[]{:S(2)}) copy-start(bf16[512,384]{1,0:T(8,128)(2,1)S(1)} %collective-permute-done.7.refs_0_) | copy-start | bytes 1179652
  36.7 11.8 %collective-permute-start.11 = (bf16[512,384]{1,0:T(8,128)(2,1)S(1)}, bf16[512,384]{1,0:T(8,128)(2,1)S(1)}, u32[]{:S(2)}, u32[]{:S(2)}) collective-permute-start(bf16[512,384]{1,0:T(8,128)(2,1)S(1)} %collective-permute-done.7.refs_0_), channel_id=1, source_target_pairs={{0,1},{1,0},{2,3},{3,2},{4,5},{5,4},{6,7},{7,6},{8,9},{9,8},{10,11... | collective-permute-start | bytes 1179656 | tf_op jit(solution)/shard_map/ppermute | solution.py:251
  37.9 10.0 %copy-start.1 = (bf16[512,384]{1,0:T(8,128)(2,1)}, bf16[512,384]{1,0:T(8,128)(2,1)S(1)}, u32[]{:S(2)}) copy-start(bf16[512,384]{1,0:T(8,128)(2,1)S(1)} %collective-permute-done.5.refs_1_.refs_3_) | copy-start | bytes 1179652
  37.9 10.6 %collective-permute-start.12 = (bf16[512,384]{1,0:T(8,128)(2,1)S(1)}, bf16[512,384]{1,0:T(8,128)(2,1)S(1)}, u32[]{:S(2)}, u32[]{:S(2)}) collective-permute-start(bf16[512,384]{1,0:T(8,128)(2,1)S(1)} %collective-permute-done.5.refs_1_.refs_3_), channel_id=1, source_target_pairs={{0,1},{1,0},{2,3},{3,2},{4,5},{5,4},{6,7},{7,6},{8,9},{9,8},{10,11... | collective-permute-start | bytes 1179656 | tf_op jit(solution)/shard_map/ppermute | solution.py:251
  38.0 10.0 %collective-permute-start.8 = (bf16[256,384]{1,0:T(8,128)(2,1)S(1)}, bf16[256,384]{1,0:T(8,128)(2,1)S(1)}, u32[]{:S(2)}, u32[]{:S(2)}) collective-permute-start(bf16[256,384]{1,0:T(8,128)(2,1)S(1)} %slice.9), channel_id=1, source_target_pairs={{0,2},{1,3},{2,0},{3,1},{4,6},{5,7},{6,4},{7,5},{8,10},{9,11},{10,... | collective-permute-start | bytes 589832 | tf_op jit(solution)/shard_map/ppermute | solution.py:251
  39.6 8.5 %collective-permute-start.6 = (bf16[256,384]{1,0:T(8,128)(2,1)S(1)}, bf16[256,384]{1,0:T(8,128)(2,1)S(1)}, u32[]{:S(2)}, u32[]{:S(2)}) collective-permute-start(bf16[256,384]{1,0:T(8,128)(2,1)S(1)} %slice.8), channel_id=1, source_target_pairs={{0,4},{4,0},{8,12},{12,8},{16,20},{20,16},{24,28},{28,24},{1,5},{5... | collective-permute-start | bytes 589832 | tf_op jit(solution)/shard_map/ppermute | solution.py:251
  40.5 0.8 copy-start.2
  48.0 10.1 %copy-start.6 = (bf16[256,384]{1,0:T(8,128)(2,1)}, bf16[256,384]{1,0:T(8,128)(2,1)S(1)}, u32[]{:S(2)}) copy-start(bf16[256,384]{1,0:T(8,128)(2,1)S(1)} %collective-permute-done.8.refs_1_) | copy-start | bytes 589828
  48.0 10.1 %collective-permute-start.10 = (bf16[256,384]{1,0:T(8,128)(2,1)S(1)}, bf16[256,384]{1,0:T(8,128)(2,1)S(1)}, u32[]{:S(2)}, u32[]{:S(2)}) collective-permute-start(bf16[256,384]{1,0:T(8,128)(2,1)S(1)} %collective-permute-done.8.refs_1_), channel_id=1, source_target_pairs={{0,1},{1,0},{2,3},{3,2},{4,5},{5,4},{6,7},{7,6},{8,9},{9,8},{10,11... | collective-permute-start | bytes 589832 | tf_op jit(solution)/shard_map/ppermute | solution.py:251
  48.1 10.0 %copy-start.7 = (bf16[256,384]{1,0:T(8,128)(2,1)}, bf16[256,384]{1,0:T(8,128)(2,1)S(1)}, u32[]{:S(2)}) copy-start(bf16[256,384]{1,0:T(8,128)(2,1)S(1)} %collective-permute-done.6.refs_0_) | copy-start | bytes 589828
  48.1 10.0 %collective-permute-start.9 = (bf16[256,384]{1,0:T(8,128)(2,1)S(1)}, bf16[256,384]{1,0:T(8,128)(2,1)S(1)}, u32[]{:S(2)}, u32[]{:S(2)}) collective-permute-start(bf16[256,384]{1,0:T(8,128)(2,1)S(1)} %collective-permute-done.6.refs_0_), channel_id=1, source_target_pairs={{0,1},{1,0},{2,3},{3,2},{4,5},{5,4},{6,7},{7,6},{8,9},{9,8},{10,11... | collective-permute-start | bytes 589832 | tf_op jit(solution)/shard_map/ppermute | solution.py:251
  48.6 0.8 copy-start.5
  48.6 0.9 %copy-start.3 = (bf16[512,384]{1,0:T(8,128)(2,1)}, bf16[512,384]{1,0:T(8,128)(2,1)S(1)}, u32[]{:S(2)}) copy-start(bf16[512,384]{1,0:T(8,128)(2,1)S(1)} %collective-permute-done.12.refs_3_.refs_5_) | copy-start | bytes 1179652
  58.1 0.7 copy-start.8
  58.1 0.7 copy-start.9
  77.4 5.7 %collective-permute-start.14 = (bf16[32,2048]{1,0:T(8,128)(2,1)}, bf16[32,2048]{1,0:T(8,128)(2,1)S(1)}, u32[]{:S(2)}, u32[]{:S(2)}) collective-permute-start(bf16[32,2048]{1,0:T(8,128)(2,1)} %get-tuple-element.25), channel_id=1, source_target_pairs={{0,4},{4,0},{8,12},{12,8},{16,20},{20,16},{24,28},{28,24},{1,5},{5... | collective-permute-start | bytes 393224 | tf_op jit(solution)/shard_map/ppermute | solution.py:251
where the time goes:
time: 84.1 us; the launch traced here: 83.8 us
  Pallas kernels  39.8 us (47%)
  waiting for transfers between devices  23 us (27%)
  starting transfers between devices  15.2 us (18%)
  local copies, waits for them, and re-layouts  3.19 us (4%)
  other arithmetic  1.77 us (2%)
    ppermute x15, waiting for transfers between devices, swap(): lax.ppermute(a, axis, [(i, i ^ bits) for i in range(lax.axis_size(axis))])  23 us
    pallas_call x3, Pallas kernels, product_call(): pl.pallas_call(lambda *refs: product_kernel(columns, len(pieces), first,...  21.4 us
    ppermute x15, starting transfers between devices, swap(): lax.ppermute(a, axis, [(i, i ^ bits) for i in range(lax.axis_size(axis))])  15.2 us
    pallas_call x1, Pallas kernels, final_call(): pl.pallas_call(lambda *refs: final_kernel(places, *refs), grid=(1,), in_s...  12.4 us
    pallas_call x1, Pallas kernels, sketch_call(): pl.pallas_call(lambda *refs: sketch_kernel(scale, *refs), grid=(cols // t...  5.93 us
    unnamed x20, local copies, waits for them, and re-layouts  2.37 us
  transfers between devices with their start and end apart: 15, of which 7 were waited for; matrix products, arithmetic and copies ran while one was open for 1% of the time, Pallas kernels for 18%

commit v1 on v0

--- a/solution.py
+++ b/solution.py
@@ -31,7 +31,14 @@
     return (shifted * shifted * shifted).astype(BF16)
 
 
-def factor_inverse(rows, n):
+def three(a):
+    high = a.astype(BF16).astype(F32)
+    rest = a - high
+    middle = rest.astype(BF16).astype(F32)
+    return high, middle, rest - middle
+
+
+def factor_inverse(rows, n, jobs):
     blocks = n // 8
     lane = lax.broadcasted_iota(jnp.int32, (8, n), 1)
     sub = lax.broadcasted_iota(jnp.int32, (8, n), 0)
@@ -45,44 +52,53 @@
         first = 8 * g
         inside = (lane >= first) & (lane < first + 8)
         pivot = jnp.where(inside, jnp.where(lane == sub + first, 1.0, 0.0), rows[g])
+        near = min(g + 2, blocks) - g
         column = [
-            [jnp.broadcast_to(rows[v][:, first + k : first + k + 1], (8, n)) for k in range(8)]
-            for v in range(g, blocks)
+            [jnp.broadcast_to(rows[g + v][:, first + k : first + k + 1], (8, n)) for k in range(8)]
+            for v in range(near)
         ]
-        factor = [[None] * 8 for _ in range(g, blocks)]
+        factor = [None] * 8
         diagonal = jnp.zeros((8, n), F32)
+        if jobs:
+            jobs.pop(0)()
         for t in range(8):
-            d = row_of(column[0][t], t)
-            diagonal = jnp.where(sub == t, d, diagonal)
-            r = 1.0 / d
+            diagonal = jnp.where(sub == t, column[0][t], diagonal)
+            r = row_of(1.0 / column[0][t], t)
             own = jnp.where(sub > t, column[0][t] * r, 0.0)
-            for v in range(1, blocks - g):
-                factor[v][t] = column[v][t] * r
+            if near > 1:
+                factor[t] = column[1][t] * r
             for k in range(t + 1, 8):
                 e = row_of(column[0][k], t)
                 column[0][k] = column[0][k] - own * e
-                for v in range(1, blocks - g):
-                    column[v][k] = column[v][k] - factor[v][t] * e
+                if near > 1:
+                    column[1][k] = column[1][k] - factor[t] * e
             pivot = pivot - own * row_of(pivot, t)
-        pivots = [row_of(pivot, t) for t in range(8)]
-        for v in range(1, blocks - g):
-            m = jnp.where(inside, 0.0, rows[g + v])
+        if g + 2 < blocks:
+            a1, a2, a3 = three(pivot * (1.0 / diagonal))
+            b1, b2, b3 = three(pivot)
+            left = jnp.concatenate([a1, a1, a2, a2, a1, a3], axis=0).astype(BF16)
+            right = jnp.concatenate([b1, b2, b1, b2, b3, b1], axis=0).astype(BF16)
+            update = mm(left, right, TN)
+            for v in range(g + 2, blocks):
+                rows[v] = jnp.where(inside, 0.0, rows[v]) - update[8 * v : 8 * v + 8, :]
+        if near > 1:
+            m = jnp.where(inside, 0.0, rows[g + 1])
             for t in range(8):
-                m = m - factor[v][t] * pivots[t]
-            rows[g + v] = m
+                m = m - factor[t] * row_of(pivot, t)
+            rows[g + 1] = m
         done.append(jnp.where(lane <= sub + first, pivot, 0.0) * lax.rsqrt(diagonal))
     return jnp.concatenate(done, axis=0)
 
 
-def inverse_factor(gram, base=128):
+def inverse_factor(gram, jobs, base=128):
     n = gram.shape[0]
     if n <= base:
-        return factor_inverse([gram[8 * i : 8 * i + 8, :] for i in range(n // 8)], n)
+        return factor_inverse([gram[8 * i : 8 * i + 8, :] for i in range(n // 8)], n, jobs)
     k = n // 2
     high = lax.Precision.HIGHEST
-    w11 = inverse_factor(gram[:k, :k], base)
+    w11 = inverse_factor(gram[:k, :k], jobs, base)
     l21 = mm(gram[k:, :k], w11, NT, high)
-    w22 = inverse_factor(gram[k:, k:] - mm(l21, l21, NT, high), base)
+    w22 = inverse_factor(gram[k:, k:] - mm(l21, l21, NT, high), jobs, base)
     w21 = -mm(w22, mm(l21, w11, NN, high), NN, high)
     top = jnp.concatenate([w11, jnp.zeros((k, n - k), F32)], axis=1)
     return jnp.concatenate([top, jnp.concatenate([w21, w22], axis=1)], axis=0)
@@ -145,35 +161,59 @@
     )(x_t, y_t, test)
 
 
+def columns_kernel(y_ref, y4_ref):
+    cols = y4_ref.shape[0]
+    start = (lax.axis_index("rows") % 2) * cols
+    high, low = split(y_ref[:, pl.ds(pl.multiple_of(start, cols), cols)])
+    y4_ref[...] = jnp.concatenate([high, high, low, low], axis=0).T
+
+
+def columns_call(y_t):
+    width, cols = y_t.shape
+    return pl.pallas_call(
+        columns_kernel,
+        out_shape=jax.ShapeDtypeStruct((cols // 2, 4 * width), BF16),
+        cost_estimate=pl.CostEstimate(
+            flops=0, bytes_accessed=4 * y_t.size + 4 * width * cols, transcendentals=0
+        ),
+        name="column_pieces",
+    )(y_t)
+
+
+def rows_of_kernel(y4, piece, columns):
+    pairs = piece[:, columns:]
+    k = cube(mm(y4, jnp.concatenate([pairs, pairs], axis=1), NT))
+    return mm(k, piece[:, :columns], NN)
+
+
+def gram_of(pieces, columns, total=None):
+    for piece in pieces:
+        s = piece[:, :columns]
+        part = mm(s, s, TN)
+        total = part if total is None else total + part
+    return total
+
+
 def product_kernel(columns, count, first, *refs):
     pieces, refs = refs[:count], refs[count:]
-    y_ref, refs = refs[0], refs[1:]
+    y4_ref, refs = refs[0], refs[1:]
     (z_in, g_in), (z_ref, g_ref) = ((None, None), refs) if first else (refs[:2], refs[2:])
-    m = pl.program_id(0)
-    tile = z_ref.shape[0]
-    start = (lax.axis_index("rows") % 2) * (y_ref.shape[1] // 2) + m * tile
-    high, low = split(y_ref[:, pl.ds(pl.multiple_of(start, tile), tile)])
-    y4 = jnp.concatenate([high, high, low, low], axis=0).T
-    total = None if first else z_in[...]
-    for piece in pieces:
-        pairs = piece[:, columns:]
-        k = cube(mm(y4, jnp.concatenate([pairs, pairs], axis=1), NT))
-        part = mm(k, piece[:, :columns], NN)
-        total = part if total is None else total + part
-    z_ref[...] = total
-
-    @pl.when(m == 0)
-    def _():
-        gram = None if first else g_in[...]
+    sub = 256
+    for i in range(z_ref.shape[0] // sub):
+        there = slice(i * sub, (i + 1) * sub)
+        total = None if first else z_in[there, :]
         for piece in pieces:
-            s = piece[:, :columns]
-            part = mm(s, s, TN)
-            gram = part if gram is None else gram + part
-        g_ref[...] = gram
-
-
-def product_call(pieces, y_t, columns, carry=None):
-    cols = y_t.shape[1] // 2
+            part = rows_of_kernel(y4_ref[there, :], piece, columns)
+            total = part if total is None else total + part
+        z_ref[there, :] = total
+
+    @pl.when(pl.program_id(0) == 0)
+    def _():
+        g_ref[...] = gram_of(pieces, columns, None if first else g_in[...])
+
+
+def product_call(pieces, y4, columns, carry=None):
+    cols, depth = y4.shape
     tile = 1024
     first = carry is None
     whole = lambda shape: pl.BlockSpec(shape, lambda m: (0, 0))
@@ -183,7 +223,7 @@
         lambda *refs: product_kernel(columns, len(pieces), first, *refs),
         grid=(cols // tile,),
         in_specs=[whole(a.shape) for a in pieces]
-        + [whole(y_t.shape)]
+        + [pl.BlockSpec((tile, depth), lambda m: (m, 0))]
         + ([] if first else [z_spec, g_spec]),
         out_specs=[z_spec, g_spec],
         out_shape=[
@@ -191,60 +231,91 @@
             jax.ShapeDtypeStruct((columns, columns), F32),
         ],
         cost_estimate=pl.CostEstimate(
-            flops=2 * cols * sum(a.shape[0] for a in pieces) * (columns + 4 * y_t.shape[0]),
-            bytes_accessed=4 * (2 * cols * columns + y_t.size) + 2 * sum(a.size for a in pieces),
+            flops=2 * cols * sum(a.shape[0] for a in pieces) * (columns + depth),
+            bytes_accessed=8 * cols * columns + 2 * y4.size + 2 * sum(a.size for a in pieces),
             transcendentals=0,
         ),
         name="kernel_times_sketch",
-    )(*pieces, y_t, *(() if first else carry))
-
-
-def final_kernel(places, g_ref, z_ref, *refs):
-    pieces, (basis_ref, projected_ref, given_ref, w, s) = refs[: len(places)], refs[len(places) :]
+    )(*pieces, y4, *(() if first else carry))
+
+
+def final_kernel(places, count, *refs):
+    late, refs = refs[:count], refs[count:]
+    (y4_ref, g_ref, z_hbm), refs = refs[:3], refs[3:]
+    pieces, refs = refs[: len(places)], refs[len(places) :]
+    basis_ref, projected_ref, given_ref, w, s, z, arrived = refs
+    columns = g_ref.shape[0]
+    cols = z.shape[0]
+    copy = pltpu.make_async_copy(z_hbm, z, arrived)
+    copy.start()
     quarter = pieces[0].shape[0]
     for place, piece in zip(places, pieces):
         s[pl.ds(pl.multiple_of(place() * quarter, quarter), quarter), :] = piece[...]
-    w[...] = inverse_factor(g_ref[...])
+    gram = gram_of(late, columns, g_ref[...])
+    copy.wait()
+
+    sub = 256
+    work = [(i, piece) for i in range(cols // sub) for piece in late]
+    slots = columns // 8
+
+    def job(part):
+        def run():
+            for i, piece in part:
+                there = slice(i * sub, (i + 1) * sub)
+                z[there, :] += rows_of_kernel(y4_ref[there, :], piece, columns)
+
+        return run
+
+    bounds = [len(work) * i // slots for i in range(slots + 1)]
+    jobs = [job(work[i:j]) for i, j in zip(bounds, bounds[1:])]
+    w[...] = inverse_factor(gram, jobs)
+
     own_r, own_c = projected_ref.shape[0], basis_ref.shape[0]
     ir, ic = lax.axis_index("rows"), lax.axis_index("cols")
 
     def rows_of(i, n):
         return split(w[pl.ds(pl.multiple_of(i * n, n), n), :])
 
-    both = mm(jnp.concatenate(rows_of(ic, own_c), axis=0), s[...], NT)
-    basis_ref[...] = both[:own_c] + both[own_c:]
     mine, given = rows_of(ir, own_r), rows_of(ir ^ 1, own_r)
     tall = jnp.concatenate([mine[0], given[0], mine[1], given[1]], axis=0)
-    cols = z_ref.shape[0]
     start = (ir % 2) * cols
     tile = 512
     for j in range(cols // tile):
-        high, low = split(z_ref[tile * j : tile * (j + 1), :])
+        high, low = split(z[tile * j : tile * (j + 1), :])
         both = mm(tall, high, NT)
         both = both[: 2 * own_r] + both[2 * own_r :] + mm(tall[: 2 * own_r], low, NT)
         there = pl.ds(pl.multiple_of(start + tile * j, tile), tile)
         projected_ref[:, there] = both[:own_r]
         given_ref[:, tile * j : tile * (j + 1)] = both[own_r:].astype(BF16)
-
-
-def final_call(gram, z, pieces, places, quarter, own_r, own_c):
+    both = mm(jnp.concatenate(rows_of(ic, own_c), axis=0), s[...], NT)
+    basis_ref[...] = both[:own_c] + both[own_c:]
+
+
+def final_call(late, y4, gram, z, pieces, places, quarter, own_r, own_c):
     columns = gram.shape[0]
     whole = lambda shape: pl.BlockSpec(shape, lambda i: (0, 0))
     height = quarter * len(pieces)
     cols = z.shape[0]
     return pl.pallas_call(
-        lambda *refs: final_kernel(places, *refs),
+        lambda *refs: final_kernel(places, len(late), *refs),
         grid=(1,),
-        in_specs=[whole(gram.shape), whole(z.shape)] + [whole((quarter, columns)) for _ in pieces],
+        in_specs=[whole(a.shape) for a in late]
+        + [whole(y4.shape), whole(gram.shape), pl.BlockSpec(memory_space=pl.ANY)]
+        + [whole((quarter, columns)) for _ in pieces],
         out_specs=[whole((own_c, height)), whole((own_r, 2 * cols)), whole((own_r, cols))],
         out_shape=[
             jax.ShapeDtypeStruct((own_c, height), F32),
             jax.ShapeDtypeStruct((own_r, 2 * cols), F32),
             jax.ShapeDtypeStruct((own_r, cols), BF16),
         ],
-        scratch_shapes=[pltpu.VMEM((columns, columns), F32), pltpu.VMEM((height, columns), BF16)],
+        scratch_shapes=[
+            pltpu.VMEM((columns, columns), F32),
+            pltpu.VMEM((height, columns), BF16),
+            pltpu.VMEM((cols, columns), F32),
+            pltpu.SemaphoreType.DMA,
+        ],
         name="factor_and_project",
-    )(gram, z, *pieces)
+    )(*late, y4, gram, z, *pieces)
 
 
 def swap(a, axis, bits):
@@ -265,6 +336,7 @@
 
     x_t, y_t = row_features.T, col_features.T
     mine, given, pairs = sketch_call(x_t, y_t, test_block, scale)
+    y4 = columns_call(y_t)
     mine = mine + swap(given, "cols", 1)
     s_own = lax.dynamic_slice_in_dim(mine, iy * quarter, quarter, 0)
     for d in range(1, chips_y):
@@ -277,7 +349,7 @@
     near_x = swap(own, "rows", 1)
     near_y = [swap(own, "cols", 2 * d) for d in range(1, chips_y)]
     own_core = swap(own, "cols", 1)
-    carry = product_call([own, own_core], y_t, columns)
+    carry = product_call([own, own_core], y4, columns)
     cut = own.shape[0] // 2
     far = []
     for d in range(1, chips_y):
@@ -285,9 +357,8 @@
         far.append(swap(near_x[cut:], "cols", 2 * d))
     near = [near_x] + near_y
     near_core = [swap(a, "cols", 1) for a in near]
-    carry = product_call(near + near_core, y_t, columns, carry)
-    far_core = [swap(a, "cols", 1) for a in far]
-    z, gram = product_call(far + far_core, y_t, columns, carry)
+    z, gram = product_call(near, y4, columns, carry)
+    late = near_core + far + [swap(a, "cols", 1) for a in far]
 
     pieces, places = [], []
     for k, group in enumerate(([own] + near_y, [own_core] + near_core[1:])):
@@ -300,7 +371,7 @@
 
             places.append(place)
     basis_t, projected, given = final_call(
-        gram, z, pieces, places, quarter, columns // rows, columns // cols
+        late, y4, gram, z, pieces, places, quarter, columns // rows, columns // cols
     )
     there = swap(given, "rows", 1).astype(F32)
     projected = lax.dynamic_update_slice_in_dim(

time: 84.1 us -> 76.2 us (0.906)
  Pallas kernels: 39.8 us -> 34.7 us
  waiting for transfers between devices: 23 us -> 20 us
    pallas_call x3 -> x2, Pallas kernels: 21.4 us -> 11.7 us  [product_call(): pl.pallas_call(lambda *refs: product_kernel(columns, len(pieces), first,...]
    pallas_call x1 -> x2, Pallas kernels: 12.4 us -> 17.1 us  [the longest x1 14.6 us: final_call(): pl.pallas_call(lambda *refs: final_kernel(places, len(late), *refs), grid...]
    ppermute x15, waiting for transfers between devices: 23 us -> 20 us  [swap(): lax.ppermute(a, axis, [(i, i ^ bits) for i in range(lax.axis_size(axis))])]
  transfers between devices with their start and end apart: 15 -> 15, of which waited for: 7 -> 7; matrix products, arithmetic and copies ran while one was open for 1% -> 1% of each run, Pallas kernels for 18% -> 19%
where the time goes in v1:
time: 76.2 us; the launch traced here: 75.8 us
  Pallas kernels  34.7 us (46%)
  waiting for transfers between devices  20 us (26%)
  starting transfers between devices  16 us (21%)
  local copies, waits for them, and re-layouts  2.58 us (3%)
  other arithmetic  1.77 us (2%)
  between operations  0.82 us (1%)
    ppermute x15, waiting for transfers between devices, swap(): lax.ppermute(a, axis, [(i, i ^ bits) for i in range(lax.axis_size(axis))])  20 us
    ppermute x15, starting transfers between devices, swap(): lax.ppermute(a, axis, [(i, i ^ bits) for i in range(lax.axis_size(axis))])  16 us
    pallas_call x1, Pallas kernels, final_call(): pl.pallas_call(lambda *refs: final_kernel(places, len(late), *refs), grid...  14.6 us
    pallas_call x2, Pallas kernels, product_call(): pl.pallas_call(lambda *refs: product_kernel(columns, len(pieces), first,...  11.7 us
    pallas_call x1, Pallas kernels, sketch_call(): pl.pallas_call(lambda *refs: sketch_kernel(scale, *refs), grid=(cols // t...  5.93 us
    pallas_call x1, Pallas kernels, columns_call(): pl.pallas_call(columns_kernel, out_shape=jax.ShapeDtypeStruct((cols // 2,...  2.56 us
    unnamed x20, local copies, waits for them, and re-layouts  1.76 us
  transfers between devices with their start and end apart: 15, of which 7 were waited for; matrix products, arithmetic and copies ran while one was open for 1% of the time, Pallas kernels for 19%

profile of v1, /device:TPU:0, one launch (start us, length us, event | category | flops | bytes accessed | tf_op | source)
XLA Modules:
  0.0 75.8 jit_solution(14224542540825592880)
XLA Ops:
  0.6 5.9 %sketch_tile.1 = (f32[256,256]{1,0:T(8,128)}, f32[256,256]{1,0:T(8,128)}, bf16[512,128]{1,0:T(8,128)(2,1)}) custom-call(f32[64,512]{1,0:T(8,128)} %bitcast.5, f32[64,4096]{1,0:T(8,128)} %bitcast.3, bf16[4096,256]{1,0:T(8,128)(2,1)} %refs_2_.1), custom_call_target="tpu_custom_call" | custom-call | tf_op jit(solution)/shard_map/sketch_tile/pallas_call | solution.py:141
  6.6 0.5 collective-permute-start
  7.1 1.4 %collective-permute-done = f32[256,256]{1,0:T(8,128)S(1)} collective-permute-done((f32[256,256]{1,0:T(8,128)}, f32[256,256]{1,0:T(8,128)S(1)}, u32[]{:S(2)}, u32[]{:S(2)}) %collective-permute-start) | collective-permute-done | bytes 262176 | tf_op jit(solution)/shard_map/ppermute | solution.py:322
  8.4 1.0 %add.29 = f32[256,256]{1,0:T(8,128)S(1)} add(f32[256,256]{1,0:T(8,128)} %get-tuple-element.12, f32[256,256]{1,0:T(8,128)S(1)} %collective-permute-done) | non-fusion elementwise | flops 65536 | bytes 786432 | tf_op jit(solution)/shard_map/add | solution.py:340
  9.4 2.9 %collective-permute-start.1 = (f32[128,256]{1,0:T(8,128)S(1)}, f32[128,256]{1,0:T(8,128)S(1)}, u32[]{:S(2)}, u32[]{:S(2)}) collective-permute-start(f32[128,256]{1,0:T(8,128)S(1)} %constant_dynamic-slice_fusion.1), channel_id=1, source_target_pairs={{0,2},{1,3},{2,0},{3,1},{4,6},{5,7},{6,4},{7,5},{8,10},{9,11},{10,... | collective-permute-start | bytes 393224 | tf_op jit(solution)/shard_map/ppermute | solution.py:322
  12.4 0.8 %constant_dynamic-slice_fusion = bf16[128,128]{1,0:T(8,128)(2,1)S(1)} fusion(bf16[512,128]{1,0:T(8,128)(2,1)} %get-tuple-element.14, s32[]{:T(128)S(6)} %select_n.31), kind=kLoop, calls=%fused_computation.4 | loop fusion | bytes 65540 | tf_op jit(solution)/shard_map/dynamic_slice | solution.py:345
  13.1 3.0 %collective-permute-done.1 = f32[128,256]{1,0:T(8,128)S(1)} collective-permute-done((f32[128,256]{1,0:T(8,128)S(1)}, f32[128,256]{1,0:T(8,128)S(1)}, u32[]{:S(2)}, u32[]{:S(2)}) %collective-permute-start.1) | collective-permute-done | bytes 131104 | tf_op jit(solution)/shard_map/ppermute | solution.py:322
  16.2 1.9 %collective-permute-start.2 = (bf16[128,384]{1,0:T(8,128)(2,1)S(1)}, bf16[128,384]{1,0:T(8,128)(2,1)S(1)}, u32[]{:S(2)}, u32[]{:S(2)}) collective-permute-start(bf16[128,384]{1,0:T(8,128)(2,1)S(1)} %pad_maximum_fusion.1), channel_id=1, source_target_pairs={{0,8},{4,12},{8,0},{12,4},{16,24},{20,28},{24,16},{28,20},{1,9},{5... | collective-permute-start | bytes 294920 | tf_op jit(solution)/shard_map/ppermute | solution.py:322
  18.1 2.6 %collective-permute-start.3 = (bf16[128,384]{1,0:T(8,128)(2,1)S(1)}, bf16[128,384]{1,0:T(8,128)(2,1)S(1)}, u32[]{:S(2)}, u32[]{:S(2)}) collective-permute-start(bf16[128,384]{1,0:T(8,128)(2,1)S(1)} %pad_maximum_fusion.1), channel_id=1, source_target_pairs={{0,16},{4,20},{8,24},{12,28},{16,0},{20,4},{24,8},{28,12},{1,17},{... | collective-permute-start | bytes 294920 | tf_op jit(solution)/shard_map/ppermute | solution.py:322
  20.7 0.0 collective-permute-start.4
  20.7 1.2 %collective-permute-done.2 = bf16[128,384]{1,0:T(8,128)(2,1)S(1)} collective-permute-done((bf16[128,384]{1,0:T(8,128)(2,1)S(1)}, bf16[128,384]{1,0:T(8,128)(2,1)S(1)}, u32[]{:S(2)}, u32[]{:S(2)}) %collective-permute-start.2) | collective-permute-done | bytes 98336 | tf_op jit(solution)/shard_map/ppermute | solution.py:322
  21.9 6.1 %collective-permute-done.3 = bf16[128,384]{1,0:T(8,128)(2,1)S(1)} collective-permute-done((bf16[128,384]{1,0:T(8,128)(2,1)S(1)}, bf16[128,384]{1,0:T(8,128)(2,1)S(1)}, u32[]{:S(2)}, u32[]{:S(2)}) %collective-permute-start.3) | collective-permute-done | bytes 98336 | tf_op jit(solution)/shard_map/ppermute | solution.py:322
  27.9 0.0 collective-permute-done.4
  28.0 0.0 copy-start.1
  28.0 1.6 %collective-permute-start.7 = (bf16[512,384]{1,0:T(8,128)(2,1)S(1)}, bf16[512,384]{1,0:T(8,128)(2,1)S(1)}, u32[]{:S(2)}, u32[]{:S(2)}) collective-permute-start(bf16[512,384]{1,0:T(8,128)(2,1)S(1)} %pad_maximum_fusion.refs_0_.refs_9_), channel_id=1, source_target_pairs={{0,2},{1,3},{2,0},{3,1},{4,6},{5,7},{6,4},{7,5},{8,10},{9,11},{10,... | collective-permute-start | bytes 1179656 | tf_op jit(solution)/shard_map/ppermute | solution.py:322
  29.6 1.5 %collective-permute-start.5 = (bf16[512,384]{1,0:T(8,128)(2,1)S(1)}, bf16[512,384]{1,0:T(8,128)(2,1)S(1)}, u32[]{:S(2)}, u32[]{:S(2)}) collective-permute-start(bf16[512,384]{1,0:T(8,128)(2,1)S(1)} %pad_maximum_fusion.refs_0_.refs_9_), channel_id=1, source_target_pairs={{0,4},{4,0},{8,12},{12,8},{16,20},{20,16},{24,28},{28,24},{1,5},{5... | collective-permute-start | bytes 1179656 | tf_op jit(solution)/shard_map/ppermute | solution.py:322
  31.1 0.0 collective-permute-start.13
  31.1 2.6 %column_pieces.1.refs_2_.refs_6_ = bf16[2048,256]{1,0:T(8,128)(2,1)} custom-call(f32[64,4096]{1,0:T(8,128)} %bitcast.4), custom_call_target="tpu_custom_call" | custom-call | bytes 2097152 | tf_op jit(solution)/shard_map/column_pieces/pallas_call | solution.py:173
  33.7 3.1 %collective-permute-done.7.refs_1_.refs_10_ = bf16[512,384]{1,0:T(8,128)(2,1)S(1)} collective-permute-done((bf16[512,384]{1,0:T(8,128)(2,1)S(1)}, bf16[512,384]{1,0:T(8,128)(2,1)S(1)}, u32[]{:S(2)}, u32[]{:S(2)}) %collective-permute-start.7) | collective-permute-done | bytes 393248 | tf_op jit(solution)/shard_map/ppermute | solution.py:322
  36.8 1.6 %collective-permute-start.9 = (bf16[256,384]{1,0:T(8,128)(2,1)S(1)}, bf16[256,384]{1,0:T(8,128)(2,1)S(1)}, u32[]{:S(2)}, u32[]{:S(2)}) collective-permute-start(bf16[256,384]{1,0:T(8,128)(2,1)S(1)} %slice.8), channel_id=1, source_target_pairs={{0,4},{4,0},{8,12},{12,8},{16,20},{20,16},{24,28},{28,24},{1,5},{5... | collective-permute-start | bytes 589832 | tf_op jit(solution)/shard_map/ppermute | solution.py:322
  38.3 0.8 %collective-permute-done.5.refs_0_ = bf16[512,384]{1,0:T(8,128)(2,1)S(1)} collective-permute-done((bf16[512,384]{1,0:T(8,128)(2,1)S(1)}, bf16[512,384]{1,0:T(8,128)(2,1)S(1)}, u32[]{:S(2)}, u32[]{:S(2)}) %collective-permute-start.5) | collective-permute-done | bytes 393248 | tf_op jit(solution)/shard_map/ppermute | solution.py:322
  39.1 1.0 %collective-permute-start.10 = (bf16[256,384]{1,0:T(8,128)(2,1)S(1)}, bf16[256,384]{1,0:T(8,128)(2,1)S(1)}, u32[]{:S(2)}, u32[]{:S(2)}) collective-permute-start(bf16[256,384]{1,0:T(8,128)(2,1)S(1)} %slice.9), channel_id=1, source_target_pairs={{0,2},{1,3},{2,0},{3,1},{4,6},{5,7},{6,4},{7,5},{8,10},{9,11},{10,... | collective-permute-start | bytes 589832 | tf_op jit(solution)/shard_map/ppermute | solution.py:322
  40.1 0.0 collective-permute-start.6
  40.1 0.5 collective-permute-start.8
  40.6 0.0 collective-permute-done.13.refs_1_.refs_11_
  40.6 0.0 copy-done.1
  40.6 0.8 %copy-done.3 = bf16[512,384]{1,0:T(8,128)(2,1)} copy-done((bf16[512,384]{1,0:T(8,128)(2,1)}, bf16[512,384]{1,0:T(8,128)(2,1)S(1)}, u32[]{:S(2)}) %copy-start.3) | copy-done | bytes 393240
  41.4 5.8 %kernel_times_sketch.2 = (f32[2048,256]{1,0:T(8,128)}, f32[256,256]{1,0:T(8,128)}) custom-call(bf16[512,384]{1,0:T(8,128)(2,1)} %copy-done.1, bf16[512,384]{1,0:T(8,128)(2,1)} %copy-done.3, bf16[2048,256]{1,0:T(8,128)(2,1)} %column_pieces.1.refs_2_.refs_6_), custom_call_target="tpu_custom_call" | custom-call | flops 2147483648 | bytes 6029312 | tf_op jit(solution)/shard_map/kernel_times_sketch/pallas_call | solution.py:222
  47.2 0.0 copy-done.2
  47.2 0.0 collective-permute-done.9.refs_2_
  47.2 0.1 collective-permute-start.11
  47.3 0.0 collective-permute-done.10.refs_3_
  47.3 0.5 collective-permute-start.12
  47.8 5.9 %kernel_times_sketch.3 = (f32[2048,256]{1,0:T(8,128)}, f32[256,256]{1,0:T(8,128)}) custom-call(bf16[512,384]{1,0:T(8,128)(2,1)} %copy-done.9, bf16[512,384]{1,0:T(8,128)(2,1)} %copy-done.2, bf16[2048,256]{1,0:T(8,128)(2,1)} %column_pieces.1.refs_2_.refs_6_, f32[2048,256]{1,0:T(8,128)} %get-tuple-element.15.refs_3_, f32[256,256]{1,0:T(8,128)} %get-tuple-element.16.refs_4_), custom_call_target="tpu_custom_call" | custom-call | flops 2147483648 | bytes 6029312 | tf_op jit(solution)/shard_map/kernel_times_sketch/pallas_call | solution.py:222
  53.7 0.0 copy-done.6
  53.7 0.0 collective-permute-done.11.refs_4_
  53.7 0.0 collective-permute-done.12.refs_5_
  53.7 0.0 collective-permute-done.6.refs_0_
  53.8 0.0 copy-start.4
  53.8 0.0 collective-permute-done.8.refs_1_.refs_12_
  53.8 0.6 copy-done.7
  54.4 0.1 copy-done.8
  54.5 0.1 copy-done.4
  54.6 0.1 copy-done
  54.7 14.6 %factor_and_project.1 = (f32[64,512]{1,0:T(8,128)}, f32[32,4096]{1,0:T(8,128)}, bf16[32,2048]{1,0:T(8,128)(2,1)}) custom-call(bf16[512,384]{1,0:T(8,128)(2,1)} %copy-done.4, bf16[512,384]{1,0:T(8,128)(2,1)} %copy-done, bf16[256,384]{1,0:T(8,128)(2,1)} %copy-done.5, bf16[256,384]{1,0:T(8,128)(2,1)} %copy-done.6, bf16[256,384]{1,0:T(8,128)(2,1)} %copy-done.7, ...), custom_call_target="tpu_custom_call" | custom-call | tf_op jit(solution)/shard_map/factor_and_project/pallas_call | solution.py:299
  69.3 1.4 %collective-permute-start.14 = (bf16[32,2048]{1,0:T(8,128)(2,1)}, bf16[32,2048]{1,0:T(8,128)(2,1)S(1)}, u32[]{:S(2)}, u32[]{:S(2)}) collective-permute-start(bf16[32,2048]{1,0:T(8,128)(2,1)} %get-tuple-element.21), channel_id=1, source_target_pairs={{0,4},{4,0},{8,12},{12,8},{16,20},{20,16},{24,28},{28,24},{1,5},{5... | collective-permute-start | bytes 393224 | tf_op jit(solution)/shard_map/ppermute | solution.py:322
  70.7 4.4 %collective-permute-done.14 = bf16[32,2048]{1,0:T(8,128)(2,1)S(1)} collective-permute-done((bf16[32,2048]{1,0:T(8,128)(2,1)}, bf16[32,2048]{1,0:T(8,128)(2,1)S(1)}, u32[]{:S(2)}, u32[]{:S(2)}) %collective-permute-start.14) | collective-permute-done | bytes 131104 | tf_op jit(solution)/shard_map/ppermute | solution.py:322
  75.1 0.7 convert_dynamic-update-slice_fusion
  (16 shorter events, 0.1 us)
Async XLA Ops:
  6.6 1.9 %collective-permute-start = (f32[256,256]{1,0:T(8,128)}, f32[256,256]{1,0:T(8,128)S(1)}, u32[]{:S(2)}, u32[]{:S(2)}) collective-permute-start(f32[256,256]{1,0:T(8,128)} %get-tuple-element.13), channel_id=1, source_target_pairs={{0,1},{1,0},{2,3},{3,2},{4,5},{5,4},{6,7},{7,6},{8,9},{9,8},{10,11... | collective-permute-start | bytes 786440 | tf_op jit(solution)/shard_map/ppermute | solution.py:322
  9.4 6.7 %collective-permute-start.1 = (f32[128,256]{1,0:T(8,128)S(1)}, f32[128,256]{1,0:T(8,128)S(1)}, u32[]{:S(2)}, u32[]{:S(2)}) collective-permute-start(f32[128,256]{1,0:T(8,128)S(1)} %constant_dynamic-slice_fusion.1), channel_id=1, source_target_pairs={{0,2},{1,3},{2,0},{3,1},{4,6},{5,7},{6,4},{7,5},{8,10},{9,11},{10,... | collective-permute-start | bytes 393224 | tf_op jit(solution)/shard_map/ppermute | solution.py:322
  16.2 5.7 %collective-permute-start.2 = (bf16[128,384]{1,0:T(8,128)(2,1)S(1)}, bf16[128,384]{1,0:T(8,128)(2,1)S(1)}, u32[]{:S(2)}, u32[]{:S(2)}) collective-permute-start(bf16[128,384]{1,0:T(8,128)(2,1)S(1)} %pad_maximum_fusion.1), channel_id=1, source_target_pairs={{0,8},{4,12},{8,0},{12,4},{16,24},{20,28},{24,16},{28,20},{1,9},{5... | collective-permute-start | bytes 294920 | tf_op jit(solution)/shard_map/ppermute | solution.py:322
  18.1 9.9 %collective-permute-start.3 = (bf16[128,384]{1,0:T(8,128)(2,1)S(1)}, bf16[128,384]{1,0:T(8,128)(2,1)S(1)}, u32[]{:S(2)}, u32[]{:S(2)}) collective-permute-start(bf16[128,384]{1,0:T(8,128)(2,1)S(1)} %pad_maximum_fusion.1), channel_id=1, source_target_pairs={{0,16},{4,20},{8,24},{12,28},{16,0},{20,4},{24,8},{28,12},{1,17},{... | collective-permute-start | bytes 294920 | tf_op jit(solution)/shard_map/ppermute | solution.py:322
  20.7 7.3 %collective-permute-start.4 = (bf16[128,384]{1,0:T(8,128)(2,1)S(1)}, bf16[128,384]{1,0:T(8,128)(2,1)S(1)}, u32[]{:S(2)}, u32[]{:S(2)}) collective-permute-start(bf16[128,384]{1,0:T(8,128)(2,1)S(1)} %pad_maximum_fusion.1), channel_id=1, source_target_pairs={{0,24},{4,28},{8,16},{12,20},{16,8},{20,12},{24,0},{28,4},{1,25},{... | collective-permute-start | bytes 294920 | tf_op jit(solution)/shard_map/ppermute | solution.py:322
  28.0 12.6 %copy-start.1 = (bf16[512,384]{1,0:T(8,128)(2,1)}, bf16[512,384]{1,0:T(8,128)(2,1)S(1)}, u32[]{:S(2)}) copy-start(bf16[512,384]{1,0:T(8,128)(2,1)S(1)} %pad_maximum_fusion.refs_0_.refs_9_) | copy-start | bytes 1179652
  28.0 8.7 %collective-permute-start.7 = (bf16[512,384]{1,0:T(8,128)(2,1)S(1)}, bf16[512,384]{1,0:T(8,128)(2,1)S(1)}, u32[]{:S(2)}, u32[]{:S(2)}) collective-permute-start(bf16[512,384]{1,0:T(8,128)(2,1)S(1)} %pad_maximum_fusion.refs_0_.refs_9_), channel_id=1, source_target_pairs={{0,2},{1,3},{2,0},{3,1},{4,6},{5,7},{6,4},{7,5},{8,10},{9,11},{10,... | collective-permute-start | bytes 1179656 | tf_op jit(solution)/shard_map/ppermute | solution.py:322
  29.6 9.5 %collective-permute-start.5 = (bf16[512,384]{1,0:T(8,128)(2,1)S(1)}, bf16[512,384]{1,0:T(8,128)(2,1)S(1)}, u32[]{:S(2)}, u32[]{:S(2)}) collective-permute-start(bf16[512,384]{1,0:T(8,128)(2,1)S(1)} %pad_maximum_fusion.refs_0_.refs_9_), channel_id=1, source_target_pairs={{0,4},{4,0},{8,12},{12,8},{16,20},{20,16},{24,28},{28,24},{1,5},{5... | collective-permute-start | bytes 1179656 | tf_op jit(solution)/shard_map/ppermute | solution.py:322
  31.1 9.6 %collective-permute-start.13 = (bf16[512,384]{1,0:T(8,128)(2,1)S(1)}, bf16[512,384]{1,0:T(8,128)(2,1)S(1)}, u32[]{:S(2)}, u32[]{:S(2)}) collective-permute-start(bf16[512,384]{1,0:T(8,128)(2,1)S(1)} %pad_maximum_fusion.refs_0_.refs_9_), channel_id=1, source_target_pairs={{0,1},{1,0},{2,3},{3,2},{4,5},{5,4},{6,7},{7,6},{8,9},{9,8},{10,11... | collective-permute-start | bytes 1179656 | tf_op jit(solution)/shard_map/ppermute | solution.py:322
  36.7 10.4 %copy-start.2 = (bf16[512,384]{1,0:T(8,128)(2,1)}, bf16[512,384]{1,0:T(8,128)(2,1)S(1)}, u32[]{:S(2)}) copy-start(bf16[512,384]{1,0:T(8,128)(2,1)S(1)} %collective-permute-done.7.refs_1_.refs_10_) | copy-start | bytes 1179652
  36.8 10.4 %collective-permute-start.9 = (bf16[256,384]{1,0:T(8,128)(2,1)S(1)}, bf16[256,384]{1,0:T(8,128)(2,1)S(1)}, u32[]{:S(2)}, u32[]{:S(2)}) collective-permute-start(bf16[256,384]{1,0:T(8,128)(2,1)S(1)} %slice.8), channel_id=1, source_target_pairs={{0,4},{4,0},{8,12},{12,8},{16,20},{20,16},{24,28},{28,24},{1,5},{5... | collective-permute-start | bytes 589832 | tf_op jit(solution)/shard_map/ppermute | solution.py:322
  39.1 8.1 %copy-start.9 = (bf16[512,384]{1,0:T(8,128)(2,1)}, bf16[512,384]{1,0:T(8,128)(2,1)S(1)}, u32[]{:S(2)}) copy-start(bf16[512,384]{1,0:T(8,128)(2,1)S(1)} %collective-permute-done.5.refs_0_) | copy-start | bytes 1179652
  39.1 8.2 %collective-permute-start.10 = (bf16[256,384]{1,0:T(8,128)(2,1)S(1)}, bf16[256,384]{1,0:T(8,128)(2,1)S(1)}, u32[]{:S(2)}, u32[]{:S(2)}) collective-permute-start(bf16[256,384]{1,0:T(8,128)(2,1)S(1)} %slice.9), channel_id=1, source_target_pairs={{0,2},{1,3},{2,0},{3,1},{4,6},{5,7},{6,4},{7,5},{8,10},{9,11},{10,... | collective-permute-start | bytes 589832 | tf_op jit(solution)/shard_map/ppermute | solution.py:322
  40.1 13.6 %collective-permute-start.6 = (bf16[512,384]{1,0:T(8,128)(2,1)S(1)}, bf16[512,384]{1,0:T(8,128)(2,1)S(1)}, u32[]{:S(2)}, u32[]{:S(2)}) collective-permute-start(bf16[512,384]{1,0:T(8,128)(2,1)S(1)} %collective-permute-done.5.refs_0_), channel_id=1, source_target_pairs={{0,1},{1,0},{2,3},{3,2},{4,5},{5,4},{6,7},{7,6},{8,9},{9,8},{10,11... | collective-permute-start | bytes 1179656 | tf_op jit(solution)/shard_map/ppermute | solution.py:322
  40.1 13.6 %collective-permute-start.8 = (bf16[512,384]{1,0:T(8,128)(2,1)S(1)}, bf16[512,384]{1,0:T(8,128)(2,1)S(1)}, u32[]{:S(2)}, u32[]{:S(2)}) collective-permute-start(bf16[512,384]{1,0:T(8,128)(2,1)S(1)} %collective-permute-done.7.refs_1_.refs_10_), channel_id=1, source_target_pairs={{0,1},{1,0},{2,3},{3,2},{4,5},{5,4},{6,7},{7,6},{8,9},{9,8},{10,11... | collective-permute-start | bytes 1179656 | tf_op jit(solution)/shard_map/ppermute | solution.py:322
  40.6 0.8 %copy-start.3 = (bf16[512,384]{1,0:T(8,128)(2,1)}, bf16[512,384]{1,0:T(8,128)(2,1)S(1)}, u32[]{:S(2)}) copy-start(bf16[512,384]{1,0:T(8,128)(2,1)S(1)} %collective-permute-done.13.refs_1_.refs_11_) | copy-start | bytes 1179652
  47.2 6.5 %copy-start.5 = (bf16[256,384]{1,0:T(8,128)(2,1)}, bf16[256,384]{1,0:T(8,128)(2,1)S(1)}, u32[]{:S(2)}) copy-start(bf16[256,384]{1,0:T(8,128)(2,1)S(1)} %collective-permute-done.9.refs_2_) | copy-start | bytes 589828
  47.2 6.5 %collective-permute-start.11 = (bf16[256,384]{1,0:T(8,128)(2,1)S(1)}, bf16[256,384]{1,0:T(8,128)(2,1)S(1)}, u32[]{:S(2)}, u32[]{:S(2)}) collective-permute-start(bf16[256,384]{1,0:T(8,128)(2,1)S(1)} %collective-permute-done.9.refs_2_), channel_id=1, source_target_pairs={{0,1},{1,0},{2,3},{3,2},{4,5},{5,4},{6,7},{7,6},{8,9},{9,8},{10,11... | collective-permute-start | bytes 589832 | tf_op jit(solution)/shard_map/ppermute | solution.py:322
  47.3 6.4 %copy-start.6 = (bf16[256,384]{1,0:T(8,128)(2,1)}, bf16[256,384]{1,0:T(8,128)(2,1)S(1)}, u32[]{:S(2)}) copy-start(bf16[256,384]{1,0:T(8,128)(2,1)S(1)} %collective-permute-done.10.refs_3_) | copy-start | bytes 589828
  47.3 6.4 %collective-permute-start.12 = (bf16[256,384]{1,0:T(8,128)(2,1)S(1)}, bf16[256,384]{1,0:T(8,128)(2,1)S(1)}, u32[]{:S(2)}, u32[]{:S(2)}) collective-permute-start(bf16[256,384]{1,0:T(8,128)(2,1)S(1)} %collective-permute-done.10.refs_3_), channel_id=1, source_target_pairs={{0,1},{1,0},{2,3},{3,2},{4,5},{5,4},{6,7},{7,6},{8,9},{9,8},{10,11... | collective-permute-start | bytes 589832 | tf_op jit(solution)/shard_map/ppermute | solution.py:322
  53.7 0.7 copy-start.7
  53.7 0.7 copy-start.8
  53.8 0.9 %copy-start.4 = (bf16[512,384]{1,0:T(8,128)(2,1)}, bf16[512,384]{1,0:T(8,128)(2,1)S(1)}, u32[]{:S(2)}) copy-start(bf16[512,384]{1,0:T(8,128)(2,1)S(1)} %collective-permute-done.6.refs_0_) | copy-start | bytes 1179652
  53.8 1.0 %copy-start = (bf16[512,384]{1,0:T(8,128)(2,1)}, bf16[512,384]{1,0:T(8,128)(2,1)S(1)}, u32[]{:S(2)}) copy-start(bf16[512,384]{1,0:T(8,128)(2,1)S(1)} %collective-permute-done.8.refs_1_.refs_12_) | copy-start | bytes 1179652
  69.3 5.8 %collective-permute-start.14 = (bf16[32,2048]{1,0:T(8,128)(2,1)}, bf16[32,2048]{1,0:T(8,128)(2,1)S(1)}, u32[]{:S(2)}, u32[]{:S(2)}) collective-permute-start(bf16[32,2048]{1,0:T(8,128)(2,1)} %get-tuple-element.21), channel_id=1, source_target_pairs={{0,4},{4,0},{8,12},{12,8},{16,20},{20,16},{24,28},{28,24},{1,5},{5... | collective-permute-start | bytes 393224 | tf_op jit(solution)/shard_map/ppermute | solution.py:322

commit v2 on v1

--- a/solution.py
+++ b/solution.py
@@ -112,18 +112,14 @@
         pairs = jnp.concatenate(split(x_ref[...] * scale), axis=0).T
         x4[...] = jnp.concatenate([pairs, pairs], axis=1)
         pairs_ref[...] = pairs
+        total[...] = jnp.zeros_like(total)
 
     high, low = split(y_ref[...])
     y4 = jnp.concatenate([high, high, low, low], axis=0)
-    part = mm(cube(mm(x4[...], y4, NN)), t_ref[...], NN)
-
-    @pl.when(step == 0)
-    def _():
-        total[...] = part
-
-    @pl.when(step > 0)
-    def _():
-        total[...] += part
+    sub = 256
+    for i in range(total.shape[0] // sub):
+        there = slice(i * sub, (i + 1) * sub)
+        total[there, :] += mm(cube(mm(x4[there, :], y4, NN)), t_ref[...], NN)
 
     @pl.when(step == pl.num_programs(0) - 1)
     def _():
@@ -136,7 +132,7 @@
 def sketch_call(x_t, y_t, test, scale):
     width, rows = x_t.shape
     cols, columns = test.shape
-    tile = 1024
+    tile = 2048
     whole = lambda shape: pl.BlockSpec(shape, lambda j: (0, 0))
     return pl.pallas_call(
         lambda *refs: sketch_kernel(scale, *refs),
@@ -159,6 +155,19 @@
         scratch_shapes=[pltpu.VMEM((rows, 4 * width), BF16), pltpu.VMEM((rows, columns), F32)],
         name="sketch_tile",
     )(x_t, y_t, test)
+
+
+def pieces_kernel(mine_ref, there_ref, *out_refs):
+    quarter = out_refs[0].shape[0]
+    iy = lax.axis_index("cols") // 2
+    for d, out_ref in enumerate(out_refs):
+        rows = pl.ds(pl.multiple_of((iy ^ d) * quarter, quarter), quarter)
+        out_ref[...] = mine_ref[rows, :] + there_ref[rows, :]
+
+
+def pieces_call(mine, there, count):
+    shape = jax.ShapeDtypeStruct((mine.shape[0] // count, mine.shape[1]), F32)
+    return pl.pallas_call(pieces_kernel, out_shape=[shape] * count, name="chip_sums")(mine, there)
 
 
 def columns_kernel(y_ref, y4_ref):
@@ -194,75 +203,47 @@
     return total
 
 
-def product_kernel(columns, count, first, *refs):
-    pieces, refs = refs[:count], refs[count:]
-    y4_ref, refs = refs[0], refs[1:]
-    (z_in, g_in), (z_ref, g_ref) = ((None, None), refs) if first else (refs[:2], refs[2:])
-    sub = 256
-    for i in range(z_ref.shape[0] // sub):
-        there = slice(i * sub, (i + 1) * sub)
-        total = None if first else z_in[there, :]
-        for piece in pieces:
-            part = rows_of_kernel(y4_ref[there, :], piece, columns)
-            total = part if total is None else total + part
-        z_ref[there, :] = total
-
-    @pl.when(pl.program_id(0) == 0)
-    def _():
-        g_ref[...] = gram_of(pieces, columns, None if first else g_in[...])
-
-
-def product_call(pieces, y4, columns, carry=None):
-    cols, depth = y4.shape
-    tile = 1024
+def gram_kernel(columns, count, first, *refs):
+    refs, g_ref = refs[:-1], refs[-1]
+    g_ref[...] = gram_of(refs[:count], columns, None if first else refs[count][...])
+
+
+def gram_call(pieces, columns, carry=None):
     first = carry is None
-    whole = lambda shape: pl.BlockSpec(shape, lambda m: (0, 0))
-    z_spec = pl.BlockSpec((tile, columns), lambda m: (m, 0))
-    g_spec = whole((columns, columns))
     return pl.pallas_call(
-        lambda *refs: product_kernel(columns, len(pieces), first, *refs),
-        grid=(cols // tile,),
-        in_specs=[whole(a.shape) for a in pieces]
-        + [pl.BlockSpec((tile, depth), lambda m: (m, 0))]
-        + ([] if first else [z_spec, g_spec]),
-        out_specs=[z_spec, g_spec],
-        out_shape=[
-            jax.ShapeDtypeStruct((cols, columns), F32),
-            jax.ShapeDtypeStruct((columns, columns), F32),
-        ],
+        lambda *refs: gram_kernel(columns, len(pieces), first, *refs),
+        out_shape=jax.ShapeDtypeStruct((columns, columns), F32),
         cost_estimate=pl.CostEstimate(
-            flops=2 * cols * sum(a.shape[0] for a in pieces) * (columns + depth),
-            bytes_accessed=8 * cols * columns + 2 * y4.size + 2 * sum(a.size for a in pieces),
+            flops=2 * columns * columns * sum(a.shape[0] for a in pieces),
+            bytes_accessed=2 * sum(a.size for a in pieces) + 8 * columns * columns,
             transcendentals=0,
         ),
-        name="kernel_times_sketch",
-    )(*pieces, y4, *(() if first else carry))
-
-
-def final_kernel(places, count, *refs):
-    late, refs = refs[:count], refs[count:]
-    (y4_ref, g_ref, z_hbm), refs = refs[:3], refs[3:]
-    pieces, refs = refs[: len(places)], refs[len(places) :]
-    basis_ref, projected_ref, given_ref, w, s, z, arrived = refs
+        name="sketch_gram",
+    )(*pieces, *(() if first else (carry,)))
+
+
+def final_kernel(places, early, count, *refs):
+    parts, refs = refs[:count], refs[count:]
+    (y4_ref, g_ref), refs = refs[:2], refs[2:]
+    basis_ref, projected_ref, given_ref, w, s, z = refs
     columns = g_ref.shape[0]
     cols = z.shape[0]
-    copy = pltpu.make_async_copy(z_hbm, z, arrived)
-    copy.start()
-    quarter = pieces[0].shape[0]
-    for place, piece in zip(places, pieces):
-        s[pl.ds(pl.multiple_of(place() * quarter, quarter), quarter), :] = piece[...]
-    gram = gram_of(late, columns, g_ref[...])
-    copy.wait()
+    quarter = s.shape[0] // len(places)
+    for place, piece in places:
+        rows = pl.ds(pl.multiple_of(place() * quarter, quarter), quarter)
+        s[rows, :] = parts[piece][:quarter, :columns]
+    gram = gram_of(parts[early:], columns, g_ref[...])
 
     sub = 256
-    work = [(i, piece) for i in range(cols // sub) for piece in late]
+    work = [(i, n) for i in range(cols // sub) for n in range(count)]
     slots = columns // 8
 
     def job(part):
         def run():
-            for i, piece in part:
+            for i, n in part:
                 there = slice(i * sub, (i + 1) * sub)
-                z[there, :] += rows_of_kernel(y4_ref[there, :], piece, columns)
+                term = rows_of_kernel(y4_ref[there, :], parts[n], columns)
+                z[there, :] = term if n == 0 else z[there, :] + term
 
         return run
 
@@ -291,17 +272,15 @@
     basis_ref[...] = both[:own_c] + both[own_c:]
 
 
-def final_call(late, y4, gram, z, pieces, places, quarter, own_r, own_c):
+def final_call(parts, early, y4, gram, places, quarter, own_r, own_c):
     columns = gram.shape[0]
     whole = lambda shape: pl.BlockSpec(shape, lambda i: (0, 0))
-    height = quarter * len(pieces)
-    cols = z.shape[0]
+    height = quarter * len(places)
+    cols = y4.shape[0]
     return pl.pallas_call(
-        lambda *refs: final_kernel(places, len(late), *refs),
+        lambda *refs: final_kernel(places, early, len(parts), *refs),
         grid=(1,),
-        in_specs=[whole(a.shape) for a in late]
-        + [whole(y4.shape), whole(gram.shape), pl.BlockSpec(memory_space=pl.ANY)]
-        + [whole((quarter, columns)) for _ in pieces],
+        in_specs=[whole(a.shape) for a in parts] + [whole(y4.shape), whole(gram.shape)],
         out_specs=[whole((own_c, height)), whole((own_r, 2 * cols)), whole((own_r, cols))],
         out_shape=[
             jax.ShapeDtypeStruct((own_c, height), F32),
@@ -312,10 +291,9 @@
             pltpu.VMEM((columns, columns), F32),
             pltpu.VMEM((height, columns), BF16),
             pltpu.VMEM((cols, columns), F32),
-            pltpu.SemaphoreType.DMA,
         ],
         name="factor_and_project",
-    )(*late, y4, gram, z, *pieces)
+    )(*parts, y4, gram)
 
 
 def swap(a, axis, bits):
@@ -337,19 +315,20 @@
     x_t, y_t = row_features.T, col_features.T
     mine, given, pairs = sketch_call(x_t, y_t, test_block, scale)
     y4 = columns_call(y_t)
-    mine = mine + swap(given, "cols", 1)
-    s_own = lax.dynamic_slice_in_dim(mine, iy * quarter, quarter, 0)
+    s_own, *given = pieces_call(mine, swap(given, "cols", 1), chips_y)
     for d in range(1, chips_y):
-        given = lax.dynamic_slice_in_dim(mine, (iy ^ d) * quarter, quarter, 0)
-        s_own = s_own + swap(given, "cols", 2 * d)
+        s_own = s_own + swap(given[d - 1], "cols", 2 * d)
     pairs = lax.dynamic_slice_in_dim(pairs, core * half + iy * quarter, quarter, 0)
     piece = jnp.concatenate([s_own.astype(BF16), pairs], axis=1)
 
-    own = jnp.concatenate([piece] + [swap(piece, "rows", 2 * d) for d in range(1, chips_z)], 0)
+    along_z = {0: piece}
+    for d in range(1, chips_z):
+        along_z[d] = swap(piece, "rows", 2 * d)
+    own = jnp.concatenate([along_z[d] for d in range(chips_z)], 0)
     near_x = swap(own, "rows", 1)
     near_y = [swap(own, "cols", 2 * d) for d in range(1, chips_y)]
     own_core = swap(own, "cols", 1)
-    carry = product_call([own, own_core], y4, columns)
+    gram = gram_call([own, own_core], columns)
     cut = own.shape[0] // 2
     far = []
     for d in range(1, chips_y):
@@ -357,21 +336,22 @@
         far.append(swap(near_x[cut:], "cols", 2 * d))
     near = [near_x] + near_y
     near_core = [swap(a, "cols", 1) for a in near]
-    z, gram = product_call(near, y4, columns, carry)
-    late = near_core + far + [swap(a, "cols", 1) for a in far]
-
-    pieces, places = [], []
-    for k, group in enumerate(([own] + near_y, [own_core] + near_core[1:])):
-        for d, a in enumerate(group):
-            pieces.append(a)
+    gram = gram_call(near, columns, gram)
+    parts = [own, own_core] + near
+    early = len(parts)
+    parts += near_core + far + [swap(a, "cols", 1) for a in far]
+
+    places = []
+    for k, group in enumerate(([0] + list(range(3, early)), [1] + list(range(early + 1, 2 * early - 2)))):
+        for d, n in enumerate(group):
 
             def place(k=k, d=d):
                 c = lax.axis_index("cols")
                 return ((c % 2) ^ k) * chips_y + ((c // 2) ^ d)
 
-            places.append(place)
+            places.append((place, n))
     basis_t, projected, given = final_call(
-        late, y4, gram, z, pieces, places, quarter, columns // rows, columns // cols
+        parts, early, y4, gram, places, quarter, columns // rows, columns // cols
     )
     there = swap(given, "rows", 1).astype(F32)
     projected = lax.dynamic_update_slice_in_dim(

time: 76.2 us -> 80 us (1.050)
  waiting for transfers between devices: 20 us -> 27.2 us
  Pallas kernels: 34.7 us -> 30.2 us
  local copies, waits for them, and re-layouts: 2.58 us -> 3.9 us
    ppermute x15, waiting for transfers between devices: 20 us -> 27.2 us  [swap(): lax.ppermute(a, axis, [(i, i ^ bits) for i in range(lax.axis_size(axis))])]
    pallas_call x3 -> x4, Pallas kernels: 26.2 us -> 22.4 us  [the longest x1 16.3 us: final_call(): pl.pallas_call(lambda *refs: final_kernel(places, early, len(parts), *ref...]
    unnamed x20 -> x22, local copies, waits for them, and re-layouts: 1.76 us -> 3.1 us
    add x1 -> x0, other arithmetic: 0.98 us -> none  [local(): mine = mine + swap(given, 'cols', 1)]
    convert_element_type x1, other arithmetic: 0.02 us -> 0.92 us  [local(): piece = jnp.concatenate([s_own.astype(BF16), pairs], axis=1)]
    pallas_call x1, Pallas kernels: 5.93 us -> 5.13 us  [sketch_call(): pl.pallas_call(lambda *refs: sketch_kernel(scale, *refs), grid=(cols // t...]
  transfers between devices with their start and end apart: 15 -> 15, of which waited for: 7 -> 8; matrix products, arithmetic and copies ran while one was open for 1% -> 1% of each run, Pallas kernels for 19% -> 9%
where the time goes in v2:
time: 80 us; the launch traced here: 79.7 us
  Pallas kernels  30.2 us (38%)
  waiting for transfers between devices  27.2 us (34%)
  starting transfers between devices  16 us (20%)
  local copies, waits for them, and re-layouts  3.9 us (5%)
  other arithmetic  1.69 us (2%)
    ppermute x15, waiting for transfers between devices, swap(): lax.ppermute(a, axis, [(i, i ^ bits) for i in range(lax.axis_size(axis))])  27.2 us
    pallas_call x1, Pallas kernels, final_call(): pl.pallas_call(lambda *refs: final_kernel(places, early, len(parts), *ref...  16.3 us
    ppermute x15, starting transfers between devices, swap(): lax.ppermute(a, axis, [(i, i ^ bits) for i in range(lax.axis_size(axis))])  16 us
    pallas_call x1, Pallas kernels, sketch_call(): pl.pallas_call(lambda *refs: sketch_kernel(scale, *refs), grid=(cols // t...  5.13 us
    pallas_call x2, Pallas kernels, gram_call(): pl.pallas_call(lambda *refs: gram_kernel(columns, len(pieces), first, *re...  4.41 us
    unnamed x22, local copies, waits for them, and re-layouts  3.1 us
    pallas_call x1, Pallas kernels, columns_call(): pl.pallas_call(columns_kernel, out_shape=jax.ShapeDtypeStruct((cols // 2,...  2.63 us
    pallas_call x1, Pallas kernels, pieces_call(): pl.pallas_call(pieces_kernel, out_shape=[shape] * count, name='chip_sums')  1.75 us
  transfers between devices with their start and end apart: 15, of which 8 were waited for; matrix products, arithmetic and copies ran while one was open for 1% of the time, Pallas kernels for 9%

profile of v2, /device:TPU:0, one launch (start us, length us, event | category | flops | bytes accessed | tf_op | source)
XLA Modules:
  0.0 79.7 jit_solution(11535989526673147329)
XLA Ops:
  0.6 5.1 %sketch_tile.1 = (f32[256,256]{1,0:T(8,128)}, f32[256,256]{1,0:T(8,128)}, bf16[512,128]{1,0:T(8,128)(2,1)}) custom-call(f32[64,512]{1,0:T(8,128)} %bitcast.5, f32[64,4096]{1,0:T(8,128)} %bitcast.3, bf16[4096,256]{1,0:T(8,128)(2,1)} %refs_2_.1), custom_call_target="tpu_custom_call" | custom-call | tf_op jit(solution)/shard_map/sketch_tile/pallas_call | solution.py:137
  5.8 0.5 collective-permute-start
  6.3 1.4 %collective-permute-done.there_ref = f32[256,256]{1,0:T(8,128)S(1)} collective-permute-done((f32[256,256]{1,0:T(8,128)}, f32[256,256]{1,0:T(8,128)S(1)}, u32[]{:S(2)}, u32[]{:S(2)}) %collective-permute-start) | collective-permute-done | bytes 262176 | tf_op jit(solution)/shard_map/ppermute | solution.py:300
  7.6 0.7 copy-done.6
  8.3 1.7 %chip_sums.1 = (f32[128,256]{1,0:T(8,128)}, f32[128,256]{1,0:T(8,128)}) custom-call(f32[256,256]{1,0:T(8,128)} %get-tuple-element.10.mine_ref, f32[256,256]{1,0:T(8,128)} %copy-done.6), custom_call_target="tpu_custom_call" | custom-call | tf_op jit(solution)/shard_map/chip_sums/pallas_call | solution.py:170
  10.1 2.9 %collective-permute-start.1 = (f32[128,256]{1,0:T(8,128)}, f32[128,256]{1,0:T(8,128)S(1)}, u32[]{:S(2)}, u32[]{:S(2)}) collective-permute-start(f32[128,256]{1,0:T(8,128)} %get-tuple-element.13), channel_id=1, source_target_pairs={{0,2},{1,3},{2,0},{3,1},{4,6},{5,7},{6,4},{7,5},{8,10},{9,11},{10,... | collective-permute-start | bytes 393224 | tf_op jit(solution)/shard_map/ppermute | solution.py:300
  13.0 0.8 constant_dynamic-slice_fusion
  13.7 3.2 %collective-permute-done.1 = f32[128,256]{1,0:T(8,128)S(1)} collective-permute-done((f32[128,256]{1,0:T(8,128)}, f32[128,256]{1,0:T(8,128)S(1)}, u32[]{:S(2)}, u32[]{:S(2)}) %collective-permute-start.1) | collective-permute-done | bytes 131104 | tf_op jit(solution)/shard_map/ppermute | solution.py:300
  17.0 0.9 %add_convert_fusion = bf16[128,256]{1,0:T(8,128)(2,1)S(1)} fusion(f32[128,256]{1,0:T(8,128)} %get-tuple-element.12, f32[128,256]{1,0:T(8,128)S(1)} %collective-permute-done.1), kind=kLoop, calls=%fused_computation.2 | loop fusion | flops 65536 | bytes 327680 | tf_op jit(solution)/shard_map/convert_element_type | solution.py:322
  17.9 3.9 %collective-permute-start.4 = (bf16[128,384]{1,0:T(8,128)(2,1)S(1)}, bf16[128,384]{1,0:T(8,128)(2,1)S(1)}, u32[]{:S(2)}, u32[]{:S(2)}) collective-permute-start(bf16[128,384]{1,0:T(8,128)(2,1)S(1)} %pad_maximum_fusion.1), channel_id=1, source_target_pairs={{0,24},{4,28},{8,16},{12,20},{16,8},{20,12},{24,0},{28,4},{1,25},{... | collective-permute-start | bytes 294920 | tf_op jit(solution)/shard_map/ppermute | solution.py:300
  21.8 0.0 collective-permute-start.3
  21.8 0.6 collective-permute-start.2
  22.4 3.0 %collective-permute-done.4 = bf16[128,384]{1,0:T(8,128)(2,1)S(1)} collective-permute-done((bf16[128,384]{1,0:T(8,128)(2,1)S(1)}, bf16[128,384]{1,0:T(8,128)(2,1)S(1)}, u32[]{:S(2)}, u32[]{:S(2)}) %collective-permute-start.4) | collective-permute-done | bytes 98336 | tf_op jit(solution)/shard_map/ppermute | solution.py:300
  25.5 4.0 %collective-permute-done.3 = bf16[128,384]{1,0:T(8,128)(2,1)S(1)} collective-permute-done((bf16[128,384]{1,0:T(8,128)(2,1)S(1)}, bf16[128,384]{1,0:T(8,128)(2,1)S(1)}, u32[]{:S(2)}, u32[]{:S(2)}) %collective-permute-start.3) | collective-permute-done | bytes 98336 | tf_op jit(solution)/shard_map/ppermute | solution.py:300
  29.5 0.0 collective-permute-done.2
  29.6 0.0 copy-start
  29.6 1.6 %collective-permute-start.7 = (bf16[512,384]{1,0:T(8,128)(2,1)S(1)}, bf16[512,384]{1,0:T(8,128)(2,1)S(1)}, u32[]{:S(2)}, u32[]{:S(2)}) collective-permute-start(bf16[512,384]{1,0:T(8,128)(2,1)S(1)} %pad_maximum_fusion.refs_0_), channel_id=1, source_target_pairs={{0,2},{1,3},{2,0},{3,1},{4,6},{5,7},{6,4},{7,5},{8,10},{9,11},{10,... | collective-permute-start | bytes 1179656 | tf_op jit(solution)/shard_map/ppermute | solution.py:300
  31.2 1.5 %collective-permute-start.6 = (bf16[512,384]{1,0:T(8,128)(2,1)S(1)}, bf16[512,384]{1,0:T(8,128)(2,1)S(1)}, u32[]{:S(2)}, u32[]{:S(2)}) collective-permute-start(bf16[512,384]{1,0:T(8,128)(2,1)S(1)} %pad_maximum_fusion.refs_0_), channel_id=1, source_target_pairs={{0,4},{4,0},{8,12},{12,8},{16,20},{20,16},{24,28},{28,24},{1,5},{5... | collective-permute-start | bytes 1179656 | tf_op jit(solution)/shard_map/ppermute | solution.py:300
  32.6 0.0 collective-permute-start.5
  32.7 7.2 %collective-permute-done.7.refs_1_.refs_3_ = bf16[512,384]{1,0:T(8,128)(2,1)S(1)} collective-permute-done((bf16[512,384]{1,0:T(8,128)(2,1)S(1)}, bf16[512,384]{1,0:T(8,128)(2,1)S(1)}, u32[]{:S(2)}, u32[]{:S(2)}) %collective-permute-start.7) | collective-permute-done | bytes 393248 | tf_op jit(solution)/shard_map/ppermute | solution.py:300
  39.9 1.6 %collective-permute-start.10 = (bf16[256,384]{1,0:T(8,128)(2,1)S(1)}, bf16[256,384]{1,0:T(8,128)(2,1)S(1)}, u32[]{:S(2)}, u32[]{:S(2)}) collective-permute-start(bf16[256,384]{1,0:T(8,128)(2,1)S(1)} %slice.8), channel_id=1, source_target_pairs={{0,4},{4,0},{8,12},{12,8},{16,20},{20,16},{24,28},{28,24},{1,5},{5... | collective-permute-start | bytes 589832 | tf_op jit(solution)/shard_map/ppermute | solution.py:300
  41.4 0.0 collective-permute-done.6.refs_0_.refs_2_
  41.4 1.6 %collective-permute-start.11 = (bf16[256,384]{1,0:T(8,128)(2,1)S(1)}, bf16[256,384]{1,0:T(8,128)(2,1)S(1)}, u32[]{:S(2)}, u32[]{:S(2)}) collective-permute-start(bf16[256,384]{1,0:T(8,128)(2,1)S(1)} %slice.9), channel_id=1, source_target_pairs={{0,2},{1,3},{2,0},{3,1},{4,6},{5,7},{6,4},{7,5},{8,10},{9,11},{10,... | collective-permute-start | bytes 589832 | tf_op jit(solution)/shard_map/ppermute | solution.py:300
  43.0 0.0 collective-permute-start.9
  43.0 0.5 collective-permute-start.8
  43.5 2.1 %collective-permute-done.10.refs_6_ = bf16[256,384]{1,0:T(8,128)(2,1)S(1)} collective-permute-done((bf16[256,384]{1,0:T(8,128)(2,1)S(1)}, bf16[256,384]{1,0:T(8,128)(2,1)S(1)}, u32[]{:S(2)}, u32[]{:S(2)}) %collective-permute-start.10) | collective-permute-done | bytes 196640 | tf_op jit(solution)/shard_map/ppermute | solution.py:300
  45.6 0.0 collective-permute-start.12
  45.6 1.6 %collective-permute-done.11.refs_7_ = bf16[256,384]{1,0:T(8,128)(2,1)S(1)} collective-permute-done((bf16[256,384]{1,0:T(8,128)(2,1)S(1)}, bf16[256,384]{1,0:T(8,128)(2,1)S(1)}, u32[]{:S(2)}, u32[]{:S(2)}) %collective-permute-start.11) | collective-permute-done | bytes 196640 | tf_op jit(solution)/shard_map/ppermute | solution.py:300
  47.2 0.0 collective-permute-start.13
  47.2 2.6 %column_pieces.1.refs_10_ = bf16[2048,256]{1,0:T(8,128)(2,1)} custom-call(f32[64,4096]{1,0:T(8,128)} %bitcast.4), custom_call_target="tpu_custom_call" | custom-call | bytes 2097152 | tf_op jit(solution)/shard_map/column_pieces/pallas_call | solution.py:182
  49.8 0.0 collective-permute-done.5.refs_1_
  49.8 0.8 copy-done.3
  50.6 2.2 %sketch_gram.2.refs_2_ = f32[256,256]{1,0:T(8,128)} custom-call(bf16[512,384]{1,0:T(8,128)(2,1)} %copy-done, bf16[512,384]{1,0:T(8,128)(2,1)} %copy-done.3), custom_call_target="tpu_custom_call" | custom-call | flops 134217728 | bytes 1310720 | tf_op jit(solution)/shard_map/sketch_gram/pallas_call | solution.py:213
  52.8 0.0 copy-done.1
  52.8 2.2 %sketch_gram.3.refs_11_ = f32[256,256]{1,0:T(8,128)} custom-call(bf16[512,384]{1,0:T(8,128)(2,1)} %copy-done.2, bf16[512,384]{1,0:T(8,128)(2,1)} %copy-done.1, f32[256,256]{1,0:T(8,128)} %sketch_gram.2.refs_2_), custom_call_target="tpu_custom_call" | custom-call | flops 134217728 | bytes 1310720 | tf_op jit(solution)/shard_map/sketch_gram/pallas_call | solution.py:213
  55.0 0.0 collective-permute-done.12.refs_8_
  55.0 0.0 collective-permute-done.9.refs_5_
  55.0 0.0 collective-permute-done.13.refs_9_
  55.1 0.0 copy-start.10
  55.1 0.0 collective-permute-done.8.refs_4_
  55.1 0.6 copy-done.9
  55.7 0.2 copy-done.4
  55.9 0.1 copy-done.10
  55.9 0.8 copy-done.5
  56.7 16.3 %factor_and_project.1 = (f32[64,512]{1,0:T(8,128)}, f32[32,4096]{1,0:T(8,128)}, bf16[32,2048]{1,0:T(8,128)(2,1)}) custom-call(bf16[512,384]{1,0:T(8,128)(2,1)} %copy-done, bf16[512,384]{1,0:T(8,128)(2,1)} %copy-done.3, bf16[512,384]{1,0:T(8,128)(2,1)} %copy-done.2, bf16[512,384]{1,0:T(8,128)(2,1)} %copy-done.1, bf16[512,384]{1,0:T(8,128)(2,1)} %copy-done.5, ...), custom_call_target="tpu_custom_call" | custom-call | tf_op jit(solution)/shard_map/factor_and_project/pallas_call | solution.py:280
  73.0 1.4 %collective-permute-start.14 = (bf16[32,2048]{1,0:T(8,128)(2,1)}, bf16[32,2048]{1,0:T(8,128)(2,1)S(1)}, u32[]{:S(2)}, u32[]{:S(2)}) collective-permute-start(bf16[32,2048]{1,0:T(8,128)(2,1)} %get-tuple-element.17), channel_id=1, source_target_pairs={{0,4},{4,0},{8,12},{12,8},{16,20},{20,16},{24,28},{28,24},{1,5},{5... | collective-permute-start | bytes 393224 | tf_op jit(solution)/shard_map/ppermute | solution.py:300
  74.3 4.7 %collective-permute-done.14 = bf16[32,2048]{1,0:T(8,128)(2,1)S(1)} collective-permute-done((bf16[32,2048]{1,0:T(8,128)(2,1)}, bf16[32,2048]{1,0:T(8,128)(2,1)S(1)}, u32[]{:S(2)}, u32[]{:S(2)}) %collective-permute-start.14) | collective-permute-done | bytes 131104 | tf_op jit(solution)/shard_map/ppermute | solution.py:300
  79.0 0.7 convert_dynamic-update-slice_fusion
  (17 shorter events, 0.1 us)
Async XLA Ops:
  5.8 1.9 %collective-permute-start = (f32[256,256]{1,0:T(8,128)}, f32[256,256]{1,0:T(8,128)S(1)}, u32[]{:S(2)}, u32[]{:S(2)}) collective-permute-start(f32[256,256]{1,0:T(8,128)} %get-tuple-element.11), channel_id=1, source_target_pairs={{0,1},{1,0},{2,3},{3,2},{4,5},{5,4},{6,7},{7,6},{8,9},{9,8},{10,11... | collective-permute-start | bytes 786440 | tf_op jit(solution)/shard_map/ppermute | solution.py:300
  7.6 0.7 copy-start.6
  10.1 6.9 %collective-permute-start.1 = (f32[128,256]{1,0:T(8,128)}, f32[128,256]{1,0:T(8,128)S(1)}, u32[]{:S(2)}, u32[]{:S(2)}) collective-permute-start(f32[128,256]{1,0:T(8,128)} %get-tuple-element.13), channel_id=1, source_target_pairs={{0,2},{1,3},{2,0},{3,1},{4,6},{5,7},{6,4},{7,5},{8,10},{9,11},{10,... | collective-permute-start | bytes 393224 | tf_op jit(solution)/shard_map/ppermute | solution.py:300
  17.9 7.6 %collective-permute-start.4 = (bf16[128,384]{1,0:T(8,128)(2,1)S(1)}, bf16[128,384]{1,0:T(8,128)(2,1)S(1)}, u32[]{:S(2)}, u32[]{:S(2)}) collective-permute-start(bf16[128,384]{1,0:T(8,128)(2,1)S(1)} %pad_maximum_fusion.1), channel_id=1, source_target_pairs={{0,24},{4,28},{8,16},{12,20},{16,8},{20,12},{24,0},{28,4},{1,25},{... | collective-permute-start | bytes 294920 | tf_op jit(solution)/shard_map/ppermute | solution.py:300
  21.8 7.7 %collective-permute-start.3 = (bf16[128,384]{1,0:T(8,128)(2,1)S(1)}, bf16[128,384]{1,0:T(8,128)(2,1)S(1)}, u32[]{:S(2)}, u32[]{:S(2)}) collective-permute-start(bf16[128,384]{1,0:T(8,128)(2,1)S(1)} %pad_maximum_fusion.1), channel_id=1, source_target_pairs={{0,16},{4,20},{8,24},{12,28},{16,0},{20,4},{24,8},{28,12},{1,17},{... | collective-permute-start | bytes 294920 | tf_op jit(solution)/shard_map/ppermute | solution.py:300
  21.8 7.7 %collective-permute-start.2 = (bf16[128,384]{1,0:T(8,128)(2,1)S(1)}, bf16[128,384]{1,0:T(8,128)(2,1)S(1)}, u32[]{:S(2)}, u32[]{:S(2)}) collective-permute-start(bf16[128,384]{1,0:T(8,128)(2,1)S(1)} %pad_maximum_fusion.1), channel_id=1, source_target_pairs={{0,8},{4,12},{8,0},{12,4},{16,24},{20,28},{24,16},{28,20},{1,9},{5... | collective-permute-start | bytes 294920 | tf_op jit(solution)/shard_map/ppermute | solution.py:300
  29.6 20.3 %copy-start = (bf16[512,384]{1,0:T(8,128)(2,1)}, bf16[512,384]{1,0:T(8,128)(2,1)S(1)}, u32[]{:S(2)}) copy-start(bf16[512,384]{1,0:T(8,128)(2,1)S(1)} %pad_maximum_fusion.refs_0_) | copy-start | bytes 1179652
  29.6 10.3 %collective-permute-start.7 = (bf16[512,384]{1,0:T(8,128)(2,1)S(1)}, bf16[512,384]{1,0:T(8,128)(2,1)S(1)}, u32[]{:S(2)}, u32[]{:S(2)}) collective-permute-start(bf16[512,384]{1,0:T(8,128)(2,1)S(1)} %pad_maximum_fusion.refs_0_), channel_id=1, source_target_pairs={{0,2},{1,3},{2,0},{3,1},{4,6},{5,7},{6,4},{7,5},{8,10},{9,11},{10,... | collective-permute-start | bytes 1179656 | tf_op jit(solution)/shard_map/ppermute | solution.py:300
  31.2 10.3 %collective-permute-start.6 = (bf16[512,384]{1,0:T(8,128)(2,1)S(1)}, bf16[512,384]{1,0:T(8,128)(2,1)S(1)}, u32[]{:S(2)}, u32[]{:S(2)}) collective-permute-start(bf16[512,384]{1,0:T(8,128)(2,1)S(1)} %pad_maximum_fusion.refs_0_), channel_id=1, source_target_pairs={{0,4},{4,0},{8,12},{12,8},{16,20},{20,16},{24,28},{28,24},{1,5},{5... | collective-permute-start | bytes 1179656 | tf_op jit(solution)/shard_map/ppermute | solution.py:300
  32.6 17.2 %collective-permute-start.5 = (bf16[512,384]{1,0:T(8,128)(2,1)S(1)}, bf16[512,384]{1,0:T(8,128)(2,1)S(1)}, u32[]{:S(2)}, u32[]{:S(2)}) collective-permute-start(bf16[512,384]{1,0:T(8,128)(2,1)S(1)} %pad_maximum_fusion.refs_0_), channel_id=1, source_target_pairs={{0,1},{1,0},{2,3},{3,2},{4,5},{5,4},{6,7},{7,6},{8,9},{9,8},{10,11... | collective-permute-start | bytes 1179656 | tf_op jit(solution)/shard_map/ppermute | solution.py:300
  39.8 12.9 %copy-start.1 = (bf16[512,384]{1,0:T(8,128)(2,1)}, bf16[512,384]{1,0:T(8,128)(2,1)S(1)}, u32[]{:S(2)}) copy-start(bf16[512,384]{1,0:T(8,128)(2,1)S(1)} %collective-permute-done.7.refs_1_.refs_3_) | copy-start | bytes 1179652
  39.9 5.7 %collective-permute-start.10 = (bf16[256,384]{1,0:T(8,128)(2,1)S(1)}, bf16[256,384]{1,0:T(8,128)(2,1)S(1)}, u32[]{:S(2)}, u32[]{:S(2)}) collective-permute-start(bf16[256,384]{1,0:T(8,128)(2,1)S(1)} %slice.8), channel_id=1, source_target_pairs={{0,4},{4,0},{8,12},{12,8},{16,20},{20,16},{24,28},{28,24},{1,5},{5... | collective-permute-start | bytes 589832 | tf_op jit(solution)/shard_map/ppermute | solution.py:300
  41.4 11.3 %copy-start.2 = (bf16[512,384]{1,0:T(8,128)(2,1)}, bf16[512,384]{1,0:T(8,128)(2,1)S(1)}, u32[]{:S(2)}) copy-start(bf16[512,384]{1,0:T(8,128)(2,1)S(1)} %collective-permute-done.6.refs_0_.refs_2_) | copy-start | bytes 1179652
  41.4 5.7 %collective-permute-start.11 = (bf16[256,384]{1,0:T(8,128)(2,1)S(1)}, bf16[256,384]{1,0:T(8,128)(2,1)S(1)}, u32[]{:S(2)}, u32[]{:S(2)}) collective-permute-start(bf16[256,384]{1,0:T(8,128)(2,1)S(1)} %slice.9), channel_id=1, source_target_pairs={{0,2},{1,3},{2,0},{3,1},{4,6},{5,7},{6,4},{7,5},{8,10},{9,11},{10,... | collective-permute-start | bytes 589832 | tf_op jit(solution)/shard_map/ppermute | solution.py:300
  43.0 12.0 %collective-permute-start.9 = (bf16[512,384]{1,0:T(8,128)(2,1)S(1)}, bf16[512,384]{1,0:T(8,128)(2,1)S(1)}, u32[]{:S(2)}, u32[]{:S(2)}) collective-permute-start(bf16[512,384]{1,0:T(8,128)(2,1)S(1)} %collective-permute-done.7.refs_1_.refs_3_), channel_id=1, source_target_pairs={{0,1},{1,0},{2,3},{3,2},{4,5},{5,4},{6,7},{7,6},{8,9},{9,8},{10,11... | collective-permute-start | bytes 1179656 | tf_op jit(solution)/shard_map/ppermute | solution.py:300
  43.0 12.0 %collective-permute-start.8 = (bf16[512,384]{1,0:T(8,128)(2,1)S(1)}, bf16[512,384]{1,0:T(8,128)(2,1)S(1)}, u32[]{:S(2)}, u32[]{:S(2)}) collective-permute-start(bf16[512,384]{1,0:T(8,128)(2,1)S(1)} %collective-permute-done.6.refs_0_.refs_2_), channel_id=1, source_target_pairs={{0,1},{1,0},{2,3},{3,2},{4,5},{5,4},{6,7},{7,6},{8,9},{9,8},{10,11... | collective-permute-start | bytes 1179656 | tf_op jit(solution)/shard_map/ppermute | solution.py:300
  45.6 9.4 %copy-start.7 = (bf16[256,384]{1,0:T(8,128)(2,1)}, bf16[256,384]{1,0:T(8,128)(2,1)S(1)}, u32[]{:S(2)}) copy-start(bf16[256,384]{1,0:T(8,128)(2,1)S(1)} %collective-permute-done.10.refs_6_) | copy-start | bytes 589828
  45.6 9.4 %collective-permute-start.12 = (bf16[256,384]{1,0:T(8,128)(2,1)S(1)}, bf16[256,384]{1,0:T(8,128)(2,1)S(1)}, u32[]{:S(2)}, u32[]{:S(2)}) collective-permute-start(bf16[256,384]{1,0:T(8,128)(2,1)S(1)} %collective-permute-done.10.refs_6_), channel_id=1, source_target_pairs={{0,1},{1,0},{2,3},{3,2},{4,5},{5,4},{6,7},{7,6},{8,9},{9,8},{10,11... | collective-permute-start | bytes 589832 | tf_op jit(solution)/shard_map/ppermute | solution.py:300
  47.2 7.8 %copy-start.8 = (bf16[256,384]{1,0:T(8,128)(2,1)}, bf16[256,384]{1,0:T(8,128)(2,1)S(1)}, u32[]{:S(2)}) copy-start(bf16[256,384]{1,0:T(8,128)(2,1)S(1)} %collective-permute-done.11.refs_7_) | copy-start | bytes 589828
  47.2 7.9 %collective-permute-start.13 = (bf16[256,384]{1,0:T(8,128)(2,1)S(1)}, bf16[256,384]{1,0:T(8,128)(2,1)S(1)}, u32[]{:S(2)}, u32[]{:S(2)}) collective-permute-start(bf16[256,384]{1,0:T(8,128)(2,1)S(1)} %collective-permute-done.11.refs_7_), channel_id=1, source_target_pairs={{0,1},{1,0},{2,3},{3,2},{4,5},{5,4},{6,7},{7,6},{8,9},{9,8},{10,11... | collective-permute-start | bytes 589832 | tf_op jit(solution)/shard_map/ppermute | solution.py:300
  49.8 0.8 copy-start.3
  55.0 0.7 copy-start.9
  55.0 0.8 %copy-start.4 = (bf16[512,384]{1,0:T(8,128)(2,1)}, bf16[512,384]{1,0:T(8,128)(2,1)S(1)}, u32[]{:S(2)}) copy-start(bf16[512,384]{1,0:T(8,128)(2,1)S(1)} %collective-permute-done.9.refs_5_) | copy-start | bytes 1179652
  55.1 0.9 %copy-start.10 = (bf16[256,384]{1,0:T(8,128)(2,1)}, bf16[256,384]{1,0:T(8,128)(2,1)S(1)}, u32[]{:S(2)}) copy-start(bf16[256,384]{1,0:T(8,128)(2,1)S(1)} %collective-permute-done.13.refs_9_) | copy-start | bytes 589828
  55.9 0.8 copy-start.5
  73.0 6.0 %collective-permute-start.14 = (bf16[32,2048]{1,0:T(8,128)(2,1)}, bf16[32,2048]{1,0:T(8,128)(2,1)S(1)}, u32[]{:S(2)}, u32[]{:S(2)}) collective-permute-start(bf16[32,2048]{1,0:T(8,128)(2,1)} %get-tuple-element.17), channel_id=1, source_target_pairs={{0,4},{4,0},{8,12},{12,8},{16,20},{20,16},{24,28},{28,24},{1,5},{5... | collective-permute-start | bytes 393224 | tf_op jit(solution)/shard_map/ppermute | solution.py:300

commit v3 on v2

--- a/solution.py
+++ b/solution.py
@@ -104,14 +104,25 @@
     return jnp.concatenate([top, jnp.concatenate([w21, w22], axis=1)], axis=0)
 
 
-def sketch_kernel(scale, x_ref, y_ref, t_ref, mine_ref, given_ref, pairs_ref, x4, total):
+def sketch_kernel(scale, quarter, x_ref, y_ref, t_ref, mine_ref, given_ref, own_ref, x4, total):
     step = pl.program_id(0)
 
     @pl.when(step == 0)
     def _():
         pairs = jnp.concatenate(split(x_ref[...] * scale), axis=0).T
         x4[...] = jnp.concatenate([pairs, pairs], axis=1)
-        pairs_ref[...] = pairs
+        depth, columns = own_ref.shape
+        width = x_ref.shape[0]
+        c = lax.axis_index("cols")
+        start = (c % 2) * (total.shape[0] // 2) + (c // 2) * quarter
+        packed = []
+        for b in range(columns // width):
+            if b * depth < quarter:
+                rows = pl.ds(pl.multiple_of(start + b * depth, depth), depth)
+                packed.append(x4[rows, :][:, :width])
+            else:
+                packed.append(jnp.zeros((depth, width), BF16))
+        own_ref[...] = jnp.concatenate(packed, axis=1)
         total[...] = jnp.zeros_like(total)
 
     high, low = split(y_ref[...])
@@ -129,13 +140,13 @@
         given_ref[...] = total[pl.ds(pl.multiple_of((1 - core) * half, half), half), :]
 
 
-def sketch_call(x_t, y_t, test, scale):
+def sketch_call(x_t, y_t, test, scale, quarter, depth):
     width, rows = x_t.shape
     cols, columns = test.shape
     tile = 2048
     whole = lambda shape: pl.BlockSpec(shape, lambda j: (0, 0))
     return pl.pallas_call(
-        lambda *refs: sketch_kernel(scale, *refs),
+        lambda *refs: sketch_kernel(scale, quarter, *refs),
         grid=(cols // tile,),
         in_specs=[
             whole((width, rows)),
@@ -145,43 +156,30 @@
         out_specs=[
             whole((rows // 2, columns)),
             whole((rows // 2, columns)),
-            whole((rows, 2 * width)),
+            whole((depth, columns)),
         ],
         out_shape=[
             jax.ShapeDtypeStruct((rows // 2, columns), F32),
             jax.ShapeDtypeStruct((rows // 2, columns), F32),
-            jax.ShapeDtypeStruct((rows, 2 * width), BF16),
+            jax.ShapeDtypeStruct((depth, columns), BF16),
         ],
         scratch_shapes=[pltpu.VMEM((rows, 4 * width), BF16), pltpu.VMEM((rows, columns), F32)],
         name="sketch_tile",
     )(x_t, y_t, test)
 
 
-def pieces_kernel(mine_ref, there_ref, *out_refs):
-    quarter = out_refs[0].shape[0]
-    iy = lax.axis_index("cols") // 2
-    for d, out_ref in enumerate(out_refs):
-        rows = pl.ds(pl.multiple_of((iy ^ d) * quarter, quarter), quarter)
-        out_ref[...] = mine_ref[rows, :] + there_ref[rows, :]
-
-
-def pieces_call(mine, there, count):
-    shape = jax.ShapeDtypeStruct((mine.shape[0] // count, mine.shape[1]), F32)
-    return pl.pallas_call(pieces_kernel, out_shape=[shape] * count, name="chip_sums")(mine, there)
-
-
-def columns_kernel(y_ref, y4_ref):
-    cols = y4_ref.shape[0]
+def columns_kernel(y_ref, y2_ref):
+    cols = y2_ref.shape[0]
     start = (lax.axis_index("rows") % 2) * cols
     high, low = split(y_ref[:, pl.ds(pl.multiple_of(start, cols), cols)])
-    y4_ref[...] = jnp.concatenate([high, high, low, low], axis=0).T
+    y2_ref[...] = jnp.concatenate([high, low], axis=0).T
 
 
 def columns_call(y_t):
     width, cols = y_t.shape
     return pl.pallas_call(
         columns_kernel,
-        out_shape=jax.ShapeDtypeStruct((cols // 2, 4 * width), BF16),
+        out_shape=jax.ShapeDtypeStruct((cols // 2, 2 * width), BF16),
         cost_estimate=pl.CostEstimate(
             flops=0, bytes_accessed=4 * y_t.size + 4 * width * cols, transcendentals=0
         ),
@@ -189,29 +187,30 @@
     )(y_t)
 
 
-def rows_of_kernel(y4, piece, columns):
-    pairs = piece[:, columns:]
-    k = cube(mm(y4, jnp.concatenate([pairs, pairs], axis=1), NT))
-    return mm(k, piece[:, :columns], NN)
-
-
-def gram_of(pieces, columns, total=None):
-    for piece in pieces:
-        s = piece[:, :columns]
+def sketch_rows(parts, quarter, depth):
+    return jnp.concatenate(
+        [a[j : j + quarter, :] for a in parts for j in range(0, a.shape[0], quarter + depth)], axis=0
+    )
+
+
+def gram_of(sketches, total=None):
+    for s in sketches:
         part = mm(s, s, TN)
         total = part if total is None else total + part
     return total
 
 
-def gram_kernel(columns, count, first, *refs):
+def gram_kernel(quarter, depth, count, first, *refs):
     refs, g_ref = refs[:-1], refs[-1]
-    g_ref[...] = gram_of(refs[:count], columns, None if first else refs[count][...])
-
-
-def gram_call(pieces, columns, carry=None):
+    sketches = [sketch_rows([a], quarter, depth) for a in refs[:count]]
+    g_ref[...] = gram_of(sketches, None if first else refs[count][...])
+
+
+def gram_call(pieces, quarter, depth, carry=None):
+    columns = pieces[0].shape[1]
     first = carry is None
     return pl.pallas_call(
-        lambda *refs: gram_kernel(columns, len(pieces), first, *refs),
+        lambda *refs: gram_kernel(quarter, depth, len(pieces), first, *refs),
         out_shape=jax.ShapeDtypeStruct((columns, columns), F32),
         cost_estimate=pl.CostEstimate(
             flops=2 * columns * columns * sum(a.shape[0] for a in pieces),
@@ -222,27 +221,49 @@
     )(*pieces, *(() if first else (carry,)))
 
 
-def final_kernel(places, early, count, *refs):
+def final_kernel(places, depth, early, groups, *refs):
+    count = sum(groups)
     parts, refs = refs[:count], refs[count:]
-    (y4_ref, g_ref), refs = refs[:2], refs[2:]
-    basis_ref, projected_ref, given_ref, w, s, z = refs
+    (y2_ref, g_ref), refs = refs[:2], refs[2:]
+    basis_ref, projected_ref, given_ref, w, s, z, x2 = refs
     columns = g_ref.shape[0]
     cols = z.shape[0]
+    width = y2_ref.shape[1] // 2
     quarter = s.shape[0] // len(places)
     for place, piece in places:
         rows = pl.ds(pl.multiple_of(place() * quarter, quarter), quarter)
-        s[rows, :] = parts[piece][:quarter, :columns]
-    gram = gram_of(parts[early:], columns, g_ref[...])
+        s[rows, :] = parts[piece][:quarter, :]
+    sources, first = [], 0
+    for n in groups:
+        sources.append(parts[first : first + n])
+        first += n
+
+    def sketch(n):
+        return sketch_rows(sources[n], quarter, depth)
+
+    def features(n):
+        rows = []
+        for part in sources[n]:
+            for j in range(quarter, part.shape[0], quarter + depth):
+                packed = part[j : j + depth, :]
+                for b in range(quarter // depth):
+                    a = packed[:, b * width : (b + 1) * width]
+                    rows.append(jnp.concatenate([a, a], axis=1))
+        return jnp.concatenate(rows, axis=0)
+
+    gram = gram_of([sketch(n) for n in range(early, len(groups))], g_ref[...])
 
     sub = 256
-    work = [(i, n) for i in range(cols // sub) for n in range(count)]
+    work = [(i, n) for i in range(cols // sub) for n in range(len(groups))]
     slots = columns // 8
 
     def job(part):
         def run():
             for i, n in part:
                 there = slice(i * sub, (i + 1) * sub)
-                term = rows_of_kernel(y4_ref[there, :], parts[n], columns)
+                if i == 0:
+                    x2[n] = features(n)
+                term = mm(cube(mm(y2_ref[there, :], x2[n], NT)), sketch(n), NN)
                 z[there, :] = term if n == 0 else z[there, :] + term
 
         return run
@@ -272,15 +293,17 @@
     basis_ref[...] = both[:own_c] + both[own_c:]
 
 
-def final_call(parts, early, y4, gram, places, quarter, own_r, own_c):
+def final_call(groups, early, y2, gram, places, quarter, depth, own_r, own_c):
     columns = gram.shape[0]
+    parts = [a for group in groups for a in group]
+    counts = [len(group) for group in groups]
     whole = lambda shape: pl.BlockSpec(shape, lambda i: (0, 0))
     height = quarter * len(places)
-    cols = y4.shape[0]
+    cols = y2.shape[0]
     return pl.pallas_call(
-        lambda *refs: final_kernel(places, early, len(parts), *refs),
+        lambda *refs: final_kernel(places, depth, early, counts, *refs),
         grid=(1,),
-        in_specs=[whole(a.shape) for a in parts] + [whole(y4.shape), whole(gram.shape)],
+        in_specs=[whole(a.shape) for a in parts] + [whole(y2.shape), whole(gram.shape)],
         out_specs=[whole((own_c, height)), whole((own_r, 2 * cols)), whole((own_r, cols))],
         out_shape=[
             jax.ShapeDtypeStruct((own_c, height), F32),
@@ -291,9 +314,10 @@
             pltpu.VMEM((columns, columns), F32),
             pltpu.VMEM((height, columns), BF16),
             pltpu.VMEM((cols, columns), F32),
+            pltpu.VMEM((len(groups), sum(a.shape[0] for a in groups[0]) // (quarter + depth) * quarter, y2.shape[1]), BF16),
         ],
         name="factor_and_project",
-    )(*parts, y4, gram)
+    )(*parts, y2, gram)
 
 
 def swap(a, axis, bits):
@@ -305,7 +329,7 @@
     rows = lax.axis_size("rows")
     chips_y, chips_z = cols // 2, rows // 2
     ir, ic = lax.axis_index("rows"), lax.axis_index("cols")
-    core, iy = ic % 2, ic // 2
+    iy = ic // 2
     height, width = row_features.shape
     scale = 1.0 / math.sqrt(width)
     columns = test_block.shape[1]
@@ -313,13 +337,15 @@
     quarter = half // chips_y
 
     x_t, y_t = row_features.T, col_features.T
-    mine, given, pairs = sketch_call(x_t, y_t, test_block, scale)
-    y4 = columns_call(y_t)
-    s_own, *given = pieces_call(mine, swap(given, "cols", 1), chips_y)
+    depth = max(16, quarter * width // columns)
+    mine, given, x_own = sketch_call(x_t, y_t, test_block, scale, quarter, depth)
+    y2 = columns_call(y_t)
+    mine = mine + swap(given, "cols", 1)
+    s_own = lax.dynamic_slice_in_dim(mine, iy * quarter, quarter, 0)
     for d in range(1, chips_y):
-        s_own = s_own + swap(given[d - 1], "cols", 2 * d)
-    pairs = lax.dynamic_slice_in_dim(pairs, core * half + iy * quarter, quarter, 0)
-    piece = jnp.concatenate([s_own.astype(BF16), pairs], axis=1)
+        given = lax.dynamic_slice_in_dim(mine, (iy ^ d) * quarter, quarter, 0)
+        s_own = s_own + swap(given, "cols", 2 * d)
+    piece = jnp.concatenate([s_own.astype(BF16), x_own], axis=0)
 
     along_z = {0: piece}
     for d in range(1, chips_z):
@@ -328,21 +354,27 @@
     near_x = swap(own, "rows", 1)
     near_y = [swap(own, "cols", 2 * d) for d in range(1, chips_y)]
     own_core = swap(own, "cols", 1)
-    gram = gram_call([own, own_core], columns)
+    gram = gram_call([own, own_core], quarter, depth)
     cut = own.shape[0] // 2
     far = []
     for d in range(1, chips_y):
-        far.append(swap(near_y[d - 1][:cut], "rows", 1))
-        far.append(swap(near_x[cut:], "cols", 2 * d))
+        low = swap(near_y[d - 1][:cut], "rows", 1)
+        far.append([low, swap(near_x[cut:], "cols", 2 * d)])
     near = [near_x] + near_y
     near_core = [swap(a, "cols", 1) for a in near]
-    gram = gram_call(near, columns, gram)
-    parts = [own, own_core] + near
-    early = len(parts)
-    parts += near_core + far + [swap(a, "cols", 1) for a in far]
+    gram = gram_call(near + near_core, quarter, depth, gram)
+    singles = [own, own_core] + near + near_core
+    early = len(singles)
+    groups = [[a] for a in singles] + far + [[swap(a, "cols", 1) for a in pair] for pair in far]
 
     places = []
-    for k, group in enumerate(([0] + list(range(3, early)), [1] + list(range(early + 1, 2 * early - 2)))):
+    with_y = len(near)
+    for k, group in enumerate(
+        (
+            [0] + list(range(3, 2 + with_y)),
+            [1] + list(range(3 + with_y, 2 + 2 * with_y)),
+        )
+    ):
         for d, n in enumerate(group):
 
             def place(k=k, d=d):
@@ -351,7 +383,7 @@
 
             places.append((place, n))
     basis_t, projected, given = final_call(
-        parts, early, y4, gram, places, quarter, columns // rows, columns // cols
+        groups, early, y2, gram, places, quarter, depth, columns // rows, columns // cols
     )
     there = swap(given, "rows", 1).astype(F32)
     projected = lax.dynamic_update_slice_in_dim(

time: 80 us -> 77.7 us (0.971)
  Pallas kernels: 30.2 us -> 27.3 us
  starting transfers between devices: 16 us -> 14.1 us
  waiting for transfers between devices: 27.2 us -> 28.6 us
    pallas_call x5 -> x4, Pallas kernels: 27.6 us -> 25 us  [the longest x1 15.2 us: final_call(): pl.pallas_call(lambda *refs: final_kernel(places, depth, early, counts, *...]
    ppermute x15, starting transfers between devices: 16 us -> 14.1 us  [swap(): lax.ppermute(a, axis, [(i, i ^ bits) for i in range(lax.axis_size(axis))])]
    ppermute x15, waiting for transfers between devices: 27.2 us -> 28.6 us  [swap(): lax.ppermute(a, axis, [(i, i ^ bits) for i in range(lax.axis_size(axis))])]
    unnamed x22 -> x23, local copies, waits for them, and re-layouts: 3.1 us -> 4.21 us
    add x0 -> x1, other arithmetic: none -> 0.98 us  [local(): mine = mine + swap(given, 'cols', 1)]
    convert_element_type x1 -> x0, other arithmetic: 0.92 us -> none  [local(): piece = jnp.concatenate([s_own.astype(BF16), pairs], axis=1)]
  transfers between devices with their start and end apart: 15 -> 15, of which waited for: 8 -> 9; matrix products, arithmetic and copies ran while one was open for 1% -> 1% of each run, Pallas kernels for 9% -> 9%
where the time goes in v3:
time: 77.7 us; the launch traced here: 77.4 us
  waiting for transfers between devices  28.6 us (37%)
  Pallas kernels  27.3 us (35%)
  starting transfers between devices  14.1 us (18%)
  local copies, waits for them, and re-layouts  4.26 us (5%)
  other arithmetic  2.45 us (3%)
    ppermute x15, waiting for transfers between devices, swap(): lax.ppermute(a, axis, [(i, i ^ bits) for i in range(lax.axis_size(axis))])  28.6 us
    pallas_call x1, Pallas kernels, final_call(): pl.pallas_call(lambda *refs: final_kernel(places, depth, early, counts, *...  15.2 us
    ppermute x15, starting transfers between devices, swap(): lax.ppermute(a, axis, [(i, i ^ bits) for i in range(lax.axis_size(axis))])  14.1 us
    pallas_call x1, Pallas kernels, sketch_call(): pl.pallas_call(lambda *refs: sketch_kernel(scale, quarter, *refs), grid=(...  5.17 us
    pallas_call x2, Pallas kernels, gram_call(): pl.pallas_call(lambda *refs: gram_kernel(quarter, depth, len(pieces), fir...  4.67 us
    unnamed x23, local copies, waits for them, and re-layouts  4.21 us
    pallas_call x1, Pallas kernels, columns_call(): pl.pallas_call(columns_kernel, out_shape=jax.ShapeDtypeStruct((cols // 2,...  2.29 us
  transfers between devices with their start and end apart: 15, of which 9 were waited for; matrix products, arithmetic and copies ran while one was open for 1% of the time, Pallas kernels for 9%

profile of v3, /device:TPU:0, one launch (start us, length us, event | category | flops | bytes accessed | tf_op | source)
XLA Modules:
  0.0 77.4 jit_solution(622531614281679247)
XLA Ops:
  0.6 5.2 %sketch_tile.1 = (f32[256,256]{1,0:T(8,128)}, f32[256,256]{1,0:T(8,128)}, bf16[32,256]{1,0:T(8,128)(2,1)}) custom-call(f32[64,512]{1,0:T(8,128)} %bitcast.5, f32[64,4096]{1,0:T(8,128)} %bitcast.3, bf16[4096,256]{1,0:T(8,128)(2,1)} %refs_2_.1), custom_call_target="tpu_custom_call" | custom-call | tf_op jit(solution)/shard_map/sketch_tile/pallas_call | solution.py:148
  5.8 0.5 collective-permute-start
  6.3 1.4 %collective-permute-done = f32[256,256]{1,0:T(8,128)S(1)} collective-permute-done((f32[256,256]{1,0:T(8,128)}, f32[256,256]{1,0:T(8,128)S(1)}, u32[]{:S(2)}, u32[]{:S(2)}) %collective-permute-start) | collective-permute-done | bytes 262176 | tf_op jit(solution)/shard_map/ppermute | solution.py:324
  7.7 1.0 %add.20 = f32[256,256]{1,0:T(8,128)S(1)} add(f32[256,256]{1,0:T(8,128)} %get-tuple-element.8, f32[256,256]{1,0:T(8,128)S(1)} %collective-permute-done) | non-fusion elementwise | flops 65536 | bytes 786432 | tf_op jit(solution)/shard_map/add | solution.py:343
  8.7 2.9 %collective-permute-start.1 = (f32[128,256]{1,0:T(8,128)S(1)}, f32[128,256]{1,0:T(8,128)S(1)}, u32[]{:S(2)}, u32[]{:S(2)}) collective-permute-start(f32[128,256]{1,0:T(8,128)S(1)} %constant_dynamic-slice_fusion), channel_id=1, source_target_pairs={{0,2},{1,3},{2,0},{3,1},{4,6},{5,7},{6,4},{7,5},{8,10},{9,11},{10,... | collective-permute-start | bytes 393224 | tf_op jit(solution)/shard_map/ppermute | solution.py:324
  11.6 3.8 %collective-permute-done.1 = f32[128,256]{1,0:T(8,128)S(1)} collective-permute-done((f32[128,256]{1,0:T(8,128)S(1)}, f32[128,256]{1,0:T(8,128)S(1)}, u32[]{:S(2)}, u32[]{:S(2)}) %collective-permute-start.1) | collective-permute-done | bytes 131104 | tf_op jit(solution)/shard_map/ppermute | solution.py:324
  15.4 0.7 pad_maximum_fusion
  16.2 3.8 %collective-permute-start.4 = (bf16[160,256]{1,0:T(8,128)(2,1)S(1)}, bf16[160,256]{1,0:T(8,128)(2,1)S(1)}, u32[]{:S(2)}, u32[]{:S(2)}) collective-permute-start(bf16[160,256]{1,0:T(8,128)(2,1)S(1)} %pad_maximum_fusion), channel_id=1, source_target_pairs={{0,24},{4,28},{8,16},{12,20},{16,8},{20,12},{24,0},{28,4},{1,25},{... | collective-permute-start | bytes 245768 | tf_op jit(solution)/shard_map/ppermute | solution.py:324
  20.0 0.0 collective-permute-start.3
  20.0 0.6 collective-permute-start.2
  20.6 0.7 constant_dynamic-update-slice_fusion.3
  21.3 3.3 %collective-permute-done.2 = bf16[160,256]{1,0:T(8,128)(2,1)S(1)} collective-permute-done((bf16[160,256]{1,0:T(8,128)(2,1)S(1)}, bf16[160,256]{1,0:T(8,128)(2,1)S(1)}, u32[]{:S(2)}, u32[]{:S(2)}) %collective-permute-start.2) | collective-permute-done | bytes 81952 | tf_op jit(solution)/shard_map/ppermute | solution.py:324
  24.7 1.6 %collective-permute-done.3 = bf16[160,256]{1,0:T(8,128)(2,1)S(1)} collective-permute-done((bf16[160,256]{1,0:T(8,128)(2,1)S(1)}, bf16[160,256]{1,0:T(8,128)(2,1)S(1)}, u32[]{:S(2)}, u32[]{:S(2)}) %collective-permute-start.3) | collective-permute-done | bytes 81952 | tf_op jit(solution)/shard_map/ppermute | solution.py:324
  26.3 0.0 collective-permute-done.4
  26.3 0.0 copy-start.2
  26.3 1.6 %collective-permute-start.7 = (bf16[640,256]{1,0:T(8,128)(2,1)S(1)}, bf16[640,256]{1,0:T(8,128)(2,1)S(1)}, u32[]{:S(2)}, u32[]{:S(2)}) collective-permute-start(bf16[640,256]{1,0:T(8,128)(2,1)S(1)} %constant_dynamic-update-slice_fusion.refs_0_), channel_id=1, source_target_pairs={{0,2},{1,3},{2,0},{3,1},{4,6},{5,7},{6,4},{7,5},{8,10},{9,11},{10,... | collective-permute-start | bytes 983048 | tf_op jit(solution)/shard_map/ppermute | solution.py:324
  27.9 1.5 %collective-permute-start.6 = (bf16[640,256]{1,0:T(8,128)(2,1)S(1)}, bf16[640,256]{1,0:T(8,128)(2,1)S(1)}, u32[]{:S(2)}, u32[]{:S(2)}) collective-permute-start(bf16[640,256]{1,0:T(8,128)(2,1)S(1)} %constant_dynamic-update-slice_fusion.refs_0_), channel_id=1, source_target_pairs={{0,4},{4,0},{8,12},{12,8},{16,20},{20,16},{24,28},{28,24},{1,5},{5... | collective-permute-start | bytes 983048 | tf_op jit(solution)/shard_map/ppermute | solution.py:324
  29.4 0.0 collective-permute-start.5
  29.4 6.3 %collective-permute-done.7.refs_1_.refs_3_ = bf16[640,256]{1,0:T(8,128)(2,1)S(1)} collective-permute-done((bf16[640,256]{1,0:T(8,128)(2,1)S(1)}, bf16[640,256]{1,0:T(8,128)(2,1)S(1)}, u32[]{:S(2)}, u32[]{:S(2)}) %collective-permute-start.7) | collective-permute-done | bytes 327712 | tf_op jit(solution)/shard_map/ppermute | solution.py:324
  35.7 0.0 collective-permute-start.9
  35.7 1.2 %collective-permute-done.6.refs_0_.refs_2_ = bf16[640,256]{1,0:T(8,128)(2,1)S(1)} collective-permute-done((bf16[640,256]{1,0:T(8,128)(2,1)S(1)}, bf16[640,256]{1,0:T(8,128)(2,1)S(1)}, u32[]{:S(2)}, u32[]{:S(2)}) %collective-permute-start.6) | collective-permute-done | bytes 327712 | tf_op jit(solution)/shard_map/ppermute | solution.py:324
  36.9 0.0 collective-permute-start.8
  37.0 1.6 %collective-permute-start.10 = (bf16[320,256]{1,0:T(8,128)(2,1)S(1)}, bf16[320,256]{1,0:T(8,128)(2,1)S(1)}, u32[]{:S(2)}, u32[]{:S(2)}) collective-permute-start(bf16[320,256]{1,0:T(8,128)(2,1)S(1)} %slice.8), channel_id=1, source_target_pairs={{0,4},{4,0},{8,12},{12,8},{16,20},{20,16},{24,28},{28,24},{1,5},{5... | collective-permute-start | bytes 491528 | tf_op jit(solution)/shard_map/ppermute | solution.py:324
  38.5 0.9 %collective-permute-start.11 = (bf16[320,256]{1,0:T(8,128)(2,1)S(1)}, bf16[320,256]{1,0:T(8,128)(2,1)S(1)}, u32[]{:S(2)}, u32[]{:S(2)}) collective-permute-start(bf16[320,256]{1,0:T(8,128)(2,1)S(1)} %slice.9), channel_id=1, source_target_pairs={{0,2},{1,3},{2,0},{3,1},{4,6},{5,7},{6,4},{7,5},{8,10},{9,11},{10,... | collective-permute-start | bytes 491528 | tf_op jit(solution)/shard_map/ppermute | solution.py:324
  39.4 4.2 %collective-permute-done.10.refs_6_ = bf16[320,256]{1,0:T(8,128)(2,1)S(1)} collective-permute-done((bf16[320,256]{1,0:T(8,128)(2,1)S(1)}, bf16[320,256]{1,0:T(8,128)(2,1)S(1)}, u32[]{:S(2)}, u32[]{:S(2)}) %collective-permute-start.10) | collective-permute-done | bytes 163872 | tf_op jit(solution)/shard_map/ppermute | solution.py:324
  43.6 0.0 collective-permute-start.12
  43.6 1.3 %collective-permute-done.11.refs_7_ = bf16[320,256]{1,0:T(8,128)(2,1)S(1)} collective-permute-done((bf16[320,256]{1,0:T(8,128)(2,1)S(1)}, bf16[320,256]{1,0:T(8,128)(2,1)S(1)}, u32[]{:S(2)}, u32[]{:S(2)}) %collective-permute-start.11) | collective-permute-done | bytes 163872 | tf_op jit(solution)/shard_map/ppermute | solution.py:324
  44.9 0.0 collective-permute-start.13
  44.9 2.3 %column_pieces.1.refs_10_ = bf16[2048,128]{1,0:T(8,128)(2,1)} custom-call(f32[64,4096]{1,0:T(8,128)} %bitcast.4), custom_call_target="tpu_custom_call" | custom-call | bytes 2097152 | tf_op jit(solution)/shard_map/column_pieces/pallas_call | solution.py:180
  47.2 0.0 collective-permute-done.5.refs_1_
  47.2 0.7 copy-done.3
  48.0 2.1 %sketch_gram.2.refs_4_ = f32[256,256]{1,0:T(8,128)} custom-call(bf16[640,256]{1,0:T(8,128)(2,1)} %copy-done.2, bf16[640,256]{1,0:T(8,128)(2,1)} %copy-done.3), custom_call_target="tpu_custom_call" | custom-call | flops 167772160 | bytes 1179648 | tf_op jit(solution)/shard_map/sketch_gram/pallas_call | solution.py:212
  50.1 0.0 collective-permute-done.9.refs_3_.refs_5_
  50.1 0.0 collective-permute-done.8.refs_2_.refs_4_
  50.1 0.0 copy-done
  50.1 0.0 copy-done.1
  50.1 0.7 copy-done.4
  50.8 0.7 copy-done.5
  51.5 2.5 %sketch_gram.3.refs_11_ = f32[256,256]{1,0:T(8,128)} custom-call(bf16[640,256]{1,0:T(8,128)(2,1)} %copy-done.1, bf16[640,256]{1,0:T(8,128)(2,1)} %copy-done, bf16[640,256]{1,0:T(8,128)(2,1)} %copy-done.5, bf16[640,256]{1,0:T(8,128)(2,1)} %copy-done.4, f32[256,256]{1,0:T(8,128)} %sketch_gram.2.refs_4_), custom_call_target="tpu_custom_call" | custom-call | flops 335544320 | bytes 1835008 | tf_op jit(solution)/shard_map/sketch_gram/pallas_call | solution.py:212
  54.1 0.0 copy-done.6
  54.1 0.0 collective-permute-done.12.refs_8_
  54.1 0.0 collective-permute-done.13.refs_9_
  54.1 0.6 copy-done.8
  54.7 0.7 copy-done.9
  55.4 15.2 %factor_and_project.1 = (f32[64,512]{1,0:T(8,128)}, f32[32,4096]{1,0:T(8,128)}, bf16[32,2048]{1,0:T(8,128)(2,1)}) custom-call(bf16[640,256]{1,0:T(8,128)(2,1)} %copy-done.2, bf16[640,256]{1,0:T(8,128)(2,1)} %copy-done.3, bf16[640,256]{1,0:T(8,128)(2,1)} %copy-done.1, bf16[640,256]{1,0:T(8,128)(2,1)} %copy-done, bf16[640,256]{1,0:T(8,128)(2,1)} %copy-done.5, ...), custom_call_target="tpu_custom_call" | custom-call | tf_op jit(solution)/shard_map/factor_and_project/pallas_call | solution.py:303
  70.6 0.7 collective-permute-start.14
  71.3 5.4 %collective-permute-done.14 = bf16[32,2048]{1,0:T(8,128)(2,1)S(1)} collective-permute-done((bf16[32,2048]{1,0:T(8,128)(2,1)}, bf16[32,2048]{1,0:T(8,128)(2,1)S(1)}, u32[]{:S(2)}, u32[]{:S(2)}) %collective-permute-start.14) | collective-permute-done | bytes 131104 | tf_op jit(solution)/shard_map/ppermute | solution.py:324
  76.6 0.7 convert_dynamic-update-slice_fusion
  (18 shorter events, 0.1 us)
Async XLA Ops:
  5.8 1.9 %collective-permute-start = (f32[256,256]{1,0:T(8,128)}, f32[256,256]{1,0:T(8,128)S(1)}, u32[]{:S(2)}, u32[]{:S(2)}) collective-permute-start(f32[256,256]{1,0:T(8,128)} %get-tuple-element.9), channel_id=1, source_target_pairs={{0,1},{1,0},{2,3},{3,2},{4,5},{5,4},{6,7},{7,6},{8,9},{9,8},{10,11... | collective-permute-start | bytes 786440 | tf_op jit(solution)/shard_map/ppermute | solution.py:324
  8.7 6.7 %collective-permute-start.1 = (f32[128,256]{1,0:T(8,128)S(1)}, f32[128,256]{1,0:T(8,128)S(1)}, u32[]{:S(2)}, u32[]{:S(2)}) collective-permute-start(f32[128,256]{1,0:T(8,128)S(1)} %constant_dynamic-slice_fusion), channel_id=1, source_target_pairs={{0,2},{1,3},{2,0},{3,1},{4,6},{5,7},{6,4},{7,5},{8,10},{9,11},{10,... | collective-permute-start | bytes 393224 | tf_op jit(solution)/shard_map/ppermute | solution.py:324
  16.2 10.1 %collective-permute-start.4 = (bf16[160,256]{1,0:T(8,128)(2,1)S(1)}, bf16[160,256]{1,0:T(8,128)(2,1)S(1)}, u32[]{:S(2)}, u32[]{:S(2)}) collective-permute-start(bf16[160,256]{1,0:T(8,128)(2,1)S(1)} %pad_maximum_fusion), channel_id=1, source_target_pairs={{0,24},{4,28},{8,16},{12,20},{16,8},{20,12},{24,0},{28,4},{1,25},{... | collective-permute-start | bytes 245768 | tf_op jit(solution)/shard_map/ppermute | solution.py:324
  20.0 6.3 %collective-permute-start.3 = (bf16[160,256]{1,0:T(8,128)(2,1)S(1)}, bf16[160,256]{1,0:T(8,128)(2,1)S(1)}, u32[]{:S(2)}, u32[]{:S(2)}) collective-permute-start(bf16[160,256]{1,0:T(8,128)(2,1)S(1)} %pad_maximum_fusion), channel_id=1, source_target_pairs={{0,16},{4,20},{8,24},{12,28},{16,0},{20,4},{24,8},{28,12},{1,17},{... | collective-permute-start | bytes 245768 | tf_op jit(solution)/shard_map/ppermute | solution.py:324
  20.0 4.7 %collective-permute-start.2 = (bf16[160,256]{1,0:T(8,128)(2,1)S(1)}, bf16[160,256]{1,0:T(8,128)(2,1)S(1)}, u32[]{:S(2)}, u32[]{:S(2)}) collective-permute-start(bf16[160,256]{1,0:T(8,128)(2,1)S(1)} %pad_maximum_fusion), channel_id=1, source_target_pairs={{0,8},{4,12},{8,0},{12,4},{16,24},{20,28},{24,16},{28,20},{1,9},{5... | collective-permute-start | bytes 245768 | tf_op jit(solution)/shard_map/ppermute | solution.py:324
  26.3 20.9 %copy-start.2 = (bf16[640,256]{1,0:T(8,128)(2,1)}, bf16[640,256]{1,0:T(8,128)(2,1)S(1)}, u32[]{:S(2)}) copy-start(bf16[640,256]{1,0:T(8,128)(2,1)S(1)} %constant_dynamic-update-slice_fusion.refs_0_) | copy-start | bytes 983044
  26.3 9.4 %collective-permute-start.7 = (bf16[640,256]{1,0:T(8,128)(2,1)S(1)}, bf16[640,256]{1,0:T(8,128)(2,1)S(1)}, u32[]{:S(2)}, u32[]{:S(2)}) collective-permute-start(bf16[640,256]{1,0:T(8,128)(2,1)S(1)} %constant_dynamic-update-slice_fusion.refs_0_), channel_id=1, source_target_pairs={{0,2},{1,3},{2,0},{3,1},{4,6},{5,7},{6,4},{7,5},{8,10},{9,11},{10,... | collective-permute-start | bytes 983048 | tf_op jit(solution)/shard_map/ppermute | solution.py:324
  27.9 9.0 %collective-permute-start.6 = (bf16[640,256]{1,0:T(8,128)(2,1)S(1)}, bf16[640,256]{1,0:T(8,128)(2,1)S(1)}, u32[]{:S(2)}, u32[]{:S(2)}) collective-permute-start(bf16[640,256]{1,0:T(8,128)(2,1)S(1)} %constant_dynamic-update-slice_fusion.refs_0_), channel_id=1, source_target_pairs={{0,4},{4,0},{8,12},{12,8},{16,20},{20,16},{24,28},{28,24},{1,5},{5... | collective-permute-start | bytes 983048 | tf_op jit(solution)/shard_map/ppermute | solution.py:324
  29.4 17.8 %collective-permute-start.5 = (bf16[640,256]{1,0:T(8,128)(2,1)S(1)}, bf16[640,256]{1,0:T(8,128)(2,1)S(1)}, u32[]{:S(2)}, u32[]{:S(2)}) collective-permute-start(bf16[640,256]{1,0:T(8,128)(2,1)S(1)} %constant_dynamic-update-slice_fusion.refs_0_), channel_id=1, source_target_pairs={{0,1},{1,0},{2,3},{3,2},{4,5},{5,4},{6,7},{7,6},{8,9},{9,8},{10,11... | collective-permute-start | bytes 983048 | tf_op jit(solution)/shard_map/ppermute | solution.py:324
  35.7 14.4 %copy-start = (bf16[640,256]{1,0:T(8,128)(2,1)}, bf16[640,256]{1,0:T(8,128)(2,1)S(1)}, u32[]{:S(2)}) copy-start(bf16[640,256]{1,0:T(8,128)(2,1)S(1)} %collective-permute-done.7.refs_1_.refs_3_) | copy-start | bytes 983044
  35.7 14.4 %collective-permute-start.9 = (bf16[640,256]{1,0:T(8,128)(2,1)S(1)}, bf16[640,256]{1,0:T(8,128)(2,1)S(1)}, u32[]{:S(2)}, u32[]{:S(2)}) collective-permute-start(bf16[640,256]{1,0:T(8,128)(2,1)S(1)} %collective-permute-done.7.refs_1_.refs_3_), channel_id=1, source_target_pairs={{0,1},{1,0},{2,3},{3,2},{4,5},{5,4},{6,7},{7,6},{8,9},{9,8},{10,11... | collective-permute-start | bytes 983048 | tf_op jit(solution)/shard_map/ppermute | solution.py:324
  36.9 13.2 %copy-start.1 = (bf16[640,256]{1,0:T(8,128)(2,1)}, bf16[640,256]{1,0:T(8,128)(2,1)S(1)}, u32[]{:S(2)}) copy-start(bf16[640,256]{1,0:T(8,128)(2,1)S(1)} %collective-permute-done.6.refs_0_.refs_2_) | copy-start | bytes 983044
  36.9 13.2 %collective-permute-start.8 = (bf16[640,256]{1,0:T(8,128)(2,1)S(1)}, bf16[640,256]{1,0:T(8,128)(2,1)S(1)}, u32[]{:S(2)}, u32[]{:S(2)}) collective-permute-start(bf16[640,256]{1,0:T(8,128)(2,1)S(1)} %collective-permute-done.6.refs_0_.refs_2_), channel_id=1, source_target_pairs={{0,1},{1,0},{2,3},{3,2},{4,5},{5,4},{6,7},{7,6},{8,9},{9,8},{10,11... | collective-permute-start | bytes 983048 | tf_op jit(solution)/shard_map/ppermute | solution.py:324
  37.0 6.7 %collective-permute-start.10 = (bf16[320,256]{1,0:T(8,128)(2,1)S(1)}, bf16[320,256]{1,0:T(8,128)(2,1)S(1)}, u32[]{:S(2)}, u32[]{:S(2)}) collective-permute-start(bf16[320,256]{1,0:T(8,128)(2,1)S(1)} %slice.8), channel_id=1, source_target_pairs={{0,4},{4,0},{8,12},{12,8},{16,20},{20,16},{24,28},{28,24},{1,5},{5... | collective-permute-start | bytes 491528 | tf_op jit(solution)/shard_map/ppermute | solution.py:324
  38.5 6.4 %collective-permute-start.11 = (bf16[320,256]{1,0:T(8,128)(2,1)S(1)}, bf16[320,256]{1,0:T(8,128)(2,1)S(1)}, u32[]{:S(2)}, u32[]{:S(2)}) collective-permute-start(bf16[320,256]{1,0:T(8,128)(2,1)S(1)} %slice.9), channel_id=1, source_target_pairs={{0,2},{1,3},{2,0},{3,1},{4,6},{5,7},{6,4},{7,5},{8,10},{9,11},{10,... | collective-permute-start | bytes 491528 | tf_op jit(solution)/shard_map/ppermute | solution.py:324
  43.6 10.5 %copy-start.6 = (bf16[320,256]{1,0:T(8,128)(2,1)}, bf16[320,256]{1,0:T(8,128)(2,1)S(1)}, u32[]{:S(2)}) copy-start(bf16[320,256]{1,0:T(8,128)(2,1)S(1)} %collective-permute-done.10.refs_6_) | copy-start | bytes 491524
  43.6 10.5 %collective-permute-start.12 = (bf16[320,256]{1,0:T(8,128)(2,1)S(1)}, bf16[320,256]{1,0:T(8,128)(2,1)S(1)}, u32[]{:S(2)}, u32[]{:S(2)}) collective-permute-start(bf16[320,256]{1,0:T(8,128)(2,1)S(1)} %collective-permute-done.10.refs_6_), channel_id=1, source_target_pairs={{0,1},{1,0},{2,3},{3,2},{4,5},{5,4},{6,7},{7,6},{8,9},{9,8},{10,11... | collective-permute-start | bytes 491528 | tf_op jit(solution)/shard_map/ppermute | solution.py:324
  44.9 9.2 %copy-start.7 = (bf16[320,256]{1,0:T(8,128)(2,1)}, bf16[320,256]{1,0:T(8,128)(2,1)S(1)}, u32[]{:S(2)}) copy-start(bf16[320,256]{1,0:T(8,128)(2,1)S(1)} %collective-permute-done.11.refs_7_) | copy-start | bytes 491524
  44.9 9.2 %collective-permute-start.13 = (bf16[320,256]{1,0:T(8,128)(2,1)S(1)}, bf16[320,256]{1,0:T(8,128)(2,1)S(1)}, u32[]{:S(2)}, u32[]{:S(2)}) collective-permute-start(bf16[320,256]{1,0:T(8,128)(2,1)S(1)} %collective-permute-done.11.refs_7_), channel_id=1, source_target_pairs={{0,1},{1,0},{2,3},{3,2},{4,5},{5,4},{6,7},{7,6},{8,9},{9,8},{10,11... | collective-permute-start | bytes 491528 | tf_op jit(solution)/shard_map/ppermute | solution.py:324
  47.2 0.7 copy-start.3
  50.1 0.7 copy-start.4
  50.8 0.7 copy-start.5
  54.1 0.6 copy-start.8
  54.7 0.7 copy-start.9
  70.6 6.1 %collective-permute-start.14 = (bf16[32,2048]{1,0:T(8,128)(2,1)}, bf16[32,2048]{1,0:T(8,128)(2,1)S(1)}, u32[]{:S(2)}, u32[]{:S(2)}) collective-permute-start(bf16[32,2048]{1,0:T(8,128)(2,1)} %get-tuple-element.13), channel_id=1, source_target_pairs={{0,4},{4,0},{8,12},{12,8},{16,20},{20,16},{24,28},{28,24},{1,5},{5... | collective-permute-start | bytes 393224 | tf_op jit(solution)/shard_map/ppermute | solution.py:324

commit v4 on v3

--- a/solution.py
+++ b/solution.py
@@ -61,18 +61,27 @@
         diagonal = jnp.zeros((8, n), F32)
         if jobs:
             jobs.pop(0)()
-        for t in range(8):
-            diagonal = jnp.where(sub == t, column[0][t], diagonal)
-            r = row_of(1.0 / column[0][t], t)
-            own = jnp.where(sub > t, column[0][t] * r, 0.0)
+        for t in range(0, 8, 2):
+            c0, c1 = column[0][t], column[0][t + 1]
+            a, b, d = row_of(c0, t), row_of(c1, t), row_of(c1, t + 1)
+            det = a * d - b * b
+            ra, rdet = 1.0 / a, 1.0 / det
+            ratio = b * ra
+            diagonal = jnp.where(sub == t, a, jnp.where(sub == t + 1, det * ra, diagonal))
+            own0 = jnp.where(sub > t, c0 * ra, 0.0)
+            own1 = jnp.where(sub > t + 1, (c1 * a - c0 * b) * rdet, 0.0)
             if near > 1:
-                factor[t] = column[1][t] * r
-            for k in range(t + 1, 8):
-                e = row_of(column[0][k], t)
-                column[0][k] = column[0][k] - own * e
+                n0, n1 = column[1][t], column[1][t + 1]
+                factor[t], factor[t + 1] = n0 * ra, (n1 * a - n0 * b) * rdet
+            for k in range(t + 2, 8):
+                e0 = row_of(column[0][k], t)
+                e1 = row_of(column[0][k], t + 1) - ratio * e0
+                column[0][k] = column[0][k] - own0 * e0 - own1 * e1
                 if near > 1:
-                    column[1][k] = column[1][k] - factor[t] * e
-            pivot = pivot - own * row_of(pivot, t)
+                    column[1][k] = column[1][k] - factor[t] * e0 - factor[t + 1] * e1
+            p0 = row_of(pivot, t)
+            p1 = row_of(pivot, t + 1) - ratio * p0
+            pivot = pivot - own0 * p0 - own1 * p1
         if g + 2 < blocks:
             a1, a2, a3 = three(pivot * (1.0 / diagonal))
             b1, b2, b3 = three(pivot)
@@ -104,8 +113,15 @@
     return jnp.concatenate([top, jnp.concatenate([w21, w22], axis=1)], axis=0)
 
 
-def sketch_kernel(scale, quarter, x_ref, y_ref, t_ref, mine_ref, given_ref, own_ref, x4, total):
+def sketch_kernel(scale, quarter, x_ref, y_ref, t_ref, own_ref, *refs):
+    piece_refs, (x4, total) = refs[:-2], refs[-2:]
     step = pl.program_id(0)
+    c = lax.axis_index("cols")
+
+    def first_row(bits):
+        i = c ^ bits
+        return pl.multiple_of((i % 2) * (total.shape[0] // 2) + (i // 2) * quarter, quarter)
+
 
     @pl.when(step == 0)
     def _():
@@ -113,12 +129,10 @@
         x4[...] = jnp.concatenate([pairs, pairs], axis=1)
         depth, columns = own_ref.shape
         width = x_ref.shape[0]
-        c = lax.axis_index("cols")
-        start = (c % 2) * (total.shape[0] // 2) + (c // 2) * quarter
         packed = []
         for b in range(columns // width):
             if b * depth < quarter:
-                rows = pl.ds(pl.multiple_of(start + b * depth, depth), depth)
+                rows = pl.ds(pl.multiple_of(first_row(0) + b * depth, depth), depth)
                 packed.append(x4[rows, :][:, :width])
             else:
                 packed.append(jnp.zeros((depth, width), BF16))
@@ -134,10 +148,8 @@
 
     @pl.when(step == pl.num_programs(0) - 1)
     def _():
-        half = mine_ref.shape[0]
-        core = lax.axis_index("cols") % 2
-        mine_ref[...] = total[pl.ds(pl.multiple_of(core * half, half), half), :]
-        given_ref[...] = total[pl.ds(pl.multiple_of((1 - core) * half, half), half), :]
+        for bits, piece_ref in enumerate(piece_refs):
+            piece_ref[...] = total[pl.ds(first_row(bits), quarter), :].astype(piece_ref.dtype)
 
 
 def sketch_call(x_t, y_t, test, scale, quarter, depth):
@@ -145,6 +157,8 @@
     cols, columns = test.shape
     tile = 2048
     whole = lambda shape: pl.BlockSpec(shape, lambda j: (0, 0))
+    count = rows // quarter
+    types = [F32 if bits < 2 else BF16 for bits in range(count)]
     return pl.pallas_call(
         lambda *refs: sketch_kernel(scale, quarter, *refs),
         grid=(cols // tile,),
@@ -154,15 +168,11 @@
             pl.BlockSpec((tile, columns), lambda j: (j, 0)),
         ],
         out_specs=[
-            whole((rows // 2, columns)),
-            whole((rows // 2, columns)),
             whole((depth, columns)),
-        ],
-        out_shape=[
-            jax.ShapeDtypeStruct((rows // 2, columns), F32),
-            jax.ShapeDtypeStruct((rows // 2, columns), F32),
-            jax.ShapeDtypeStruct((depth, columns), BF16),
-        ],
+        ]
+        + [whole((quarter, columns))] * count,
+        out_shape=[jax.ShapeDtypeStruct((depth, columns), BF16)]
+        + [jax.ShapeDtypeStruct((quarter, columns), t) for t in types],
         scratch_shapes=[pltpu.VMEM((rows, 4 * width), BF16), pltpu.VMEM((rows, columns), F32)],
         name="sketch_tile",
     )(x_t, y_t, test)
@@ -221,11 +231,16 @@
     )(*pieces, *(() if first else (carry,)))
 
 
-def final_kernel(places, depth, early, groups, *refs):
+def final_kernel(places, depth, early, late, groups, *refs):
     count = sum(groups)
     parts, refs = refs[:count], refs[count:]
     (y2_ref, g_ref), refs = refs[:2], refs[2:]
-    basis_ref, projected_ref, given_ref, w, s, z, x2 = refs
+    basis_ref, projected_ref, given_ref, w, s, z, x2, *landed, arrived = refs
+    copies = []
+    for i, a in enumerate(landed):
+        copies.append(pltpu.make_async_copy(parts[count - len(landed) + i], a, arrived.at[i]))
+        copies[-1].start()
+    parts = parts[: count - len(landed)] + tuple(landed)
     columns = g_ref.shape[0]
     cols = z.shape[0]
     width = y2_ref.shape[1] // 2
@@ -251,7 +266,10 @@
                     rows.append(jnp.concatenate([a, a], axis=1))
         return jnp.concatenate(rows, axis=0)
 
-    gram = gram_of([sketch(n) for n in range(early, len(groups))], g_ref[...])
+    gram = gram_of([sketch(n) for n in range(early, late)], g_ref[...])
+    for copy in copies:
+        copy.wait()
+    gram = gram_of([sketch(n) for n in range(late, len(groups))], gram)
 
     sub = 256
     work = [(i, n) for i in range(cols // sub) for n in range(len(groups))]
@@ -293,17 +311,20 @@
     basis_ref[...] = both[:own_c] + both[own_c:]
 
 
-def final_call(groups, early, y2, gram, places, quarter, depth, own_r, own_c):
+def final_call(groups, early, late, y2, gram, places, quarter, depth, own_r, own_c):
     columns = gram.shape[0]
     parts = [a for group in groups for a in group]
     counts = [len(group) for group in groups]
+    landing = parts[sum(counts[:late]) :]
     whole = lambda shape: pl.BlockSpec(shape, lambda i: (0, 0))
     height = quarter * len(places)
     cols = y2.shape[0]
     return pl.pallas_call(
-        lambda *refs: final_kernel(places, depth, early, counts, *refs),
+        lambda *refs: final_kernel(places, depth, early, late, counts, *refs),
         grid=(1,),
-        in_specs=[whole(a.shape) for a in parts] + [whole(y2.shape), whole(gram.shape)],
+        in_specs=[whole(a.shape) for a in parts[: len(parts) - len(landing)]]
+        + [pl.BlockSpec(memory_space=pltpu.HBM) for _ in landing]
+        + [whole(y2.shape), whole(gram.shape)],
         out_specs=[whole((own_c, height)), whole((own_r, 2 * cols)), whole((own_r, cols))],
         out_shape=[
             jax.ShapeDtypeStruct((own_c, height), F32),
@@ -315,7 +336,9 @@
             pltpu.VMEM((height, columns), BF16),
             pltpu.VMEM((cols, columns), F32),
             pltpu.VMEM((len(groups), sum(a.shape[0] for a in groups[0]) // (quarter + depth) * quarter, y2.shape[1]), BF16),
-        ],
+        ]
+        + [pltpu.VMEM(a.shape, BF16) for a in landing]
+        + [pltpu.SemaphoreType.DMA((len(landing),))],
         name="factor_and_project",
     )(*parts, y2, gram)
 
@@ -328,8 +351,7 @@
     cols = lax.axis_size("cols")
     rows = lax.axis_size("rows")
     chips_y, chips_z = cols // 2, rows // 2
-    ir, ic = lax.axis_index("rows"), lax.axis_index("cols")
-    iy = ic // 2
+    ir = lax.axis_index("rows")
     height, width = row_features.shape
     scale = 1.0 / math.sqrt(width)
     columns = test_block.shape[1]
@@ -338,13 +360,10 @@
 
     x_t, y_t = row_features.T, col_features.T
     depth = max(16, quarter * width // columns)
-    mine, given, x_own = sketch_call(x_t, y_t, test_block, scale, quarter, depth)
+    x_own, s_own, *given = sketch_call(x_t, y_t, test_block, scale, quarter, depth)
     y2 = columns_call(y_t)
-    mine = mine + swap(given, "cols", 1)
-    s_own = lax.dynamic_slice_in_dim(mine, iy * quarter, quarter, 0)
-    for d in range(1, chips_y):
-        given = lax.dynamic_slice_in_dim(mine, (iy ^ d) * quarter, quarter, 0)
-        s_own = s_own + swap(given, "cols", 2 * d)
+    for bits, a in list(enumerate(given, 1))[::-1]:
+        s_own = s_own + swap(a, "cols", bits).astype(F32)
     piece = jnp.concatenate([s_own.astype(BF16), x_own], axis=0)
 
     along_z = {0: piece}
@@ -383,7 +402,7 @@
 
             places.append((place, n))
     basis_t, projected, given = final_call(
-        groups, early, y2, gram, places, quarter, depth, columns // rows, columns // cols
+        groups, early, early + len(far), y2, gram, places, quarter, depth, columns // rows, columns // cols
     )
     there = swap(given, "rows", 1).astype(F32)
     projected = lax.dynamic_update_slice_in_dim(

time: 77.7 us -> 76.1 us (0.979)
  waiting for transfers between devices: 28.6 us -> 26.5 us
  Pallas kernels: 27.3 us -> 28.1 us
    ppermute x15 -> x16, waiting for transfers between devices: 28.6 us -> 26.5 us  [swap(): lax.ppermute(a, axis, [(i, i ^ bits) for i in range(lax.axis_size(axis))])]
    add x1 -> x0, other arithmetic: 0.98 us -> none  [local(): mine = mine + swap(given, 'cols', 1)]
    unnamed x1, other arithmetic: 0.02 us -> 0.94 us
    pallas_call x1, Pallas kernels: 15.2 us -> 16 us  [final_call(): pl.pallas_call(lambda *refs: final_kernel(places, depth, early, late, cou...]
    ppermute x15 -> x16, starting transfers between devices: 14.1 us -> 13.7 us  [swap(): lax.ppermute(a, axis, [(i, i ^ bits) for i in range(lax.axis_size(axis))])]
  transfers between devices with their start and end apart: 15 -> 16, of which waited for: 9 -> 10; matrix products, arithmetic and copies ran while one was open for 1% -> 1% of each run, Pallas kernels for 9% -> 9%
where the time goes in v4:
time: 76.1 us; the launch traced here: 75.7 us
  Pallas kernels  28.1 us (37%)
  waiting for transfers between devices  26.5 us (35%)
  starting transfers between devices  13.7 us (18%)
  local copies, waits for them, and re-layouts  4.26 us (6%)
  other arithmetic  2.38 us (3%)
    ppermute x16, waiting for transfers between devices, swap(): lax.ppermute(a, axis, [(i, i ^ bits) for i in range(lax.axis_size(axis))])  26.5 us
    pallas_call x1, Pallas kernels, final_call(): pl.pallas_call(lambda *refs: final_kernel(places, depth, early, late, cou...  16 us
    ppermute x16, starting transfers between devices, swap(): lax.ppermute(a, axis, [(i, i ^ bits) for i in range(lax.axis_size(axis))])  13.7 us
    pallas_call x1, Pallas kernels, sketch_call(): pl.pallas_call(lambda *refs: sketch_kernel(scale, quarter, *refs), grid=(...  5.13 us
    pallas_call x2, Pallas kernels, gram_call(): pl.pallas_call(lambda *refs: gram_kernel(quarter, depth, len(pieces), fir...  4.66 us
    unnamed x23, local copies, waits for them, and re-layouts  4.23 us
    pallas_call x1, Pallas kernels, columns_call(): pl.pallas_call(columns_kernel, out_shape=jax.ShapeDtypeStruct((cols // 2,...  2.29 us
  transfers between devices with their start and end apart: 16, of which 10 were waited for; matrix products, arithmetic and copies ran while one was open for 1% of the time, Pallas kernels for 9%

profile of v4, /device:TPU:0, one launch (start us, length us, event | category | flops | bytes accessed | tf_op | source)
XLA Modules:
  0.0 75.7 jit_solution(17053919645724133863)
XLA Ops:
  0.6 5.1 %sketch_tile.1 = (bf16[32,256]{1,0:T(8,128)(2,1)}, f32[128,256]{1,0:T(8,128)}, f32[128,256]{1,0:T(8,128)}, bf16[128,256]{1,0:T(8,128)(2,1)}, bf16[128,256]{1,0:T(8,128)(2,1)}) custom-call(f32[64,512]{1,0:T(8,128)} %bitcast.5, f32[64,4096]{1,0:T(8,128)} %bitcast.3, bf16[4096,256]{1,0:T(8,128)(2,1)} %refs_2_.1), custom_call_target="tpu_custom_call" | custom-call | tf_op jit(solution)/shard_map/sketch_tile/pallas_call | solution.py:162
  5.8 0.5 collective-permute-start.2
  6.3 2.6 %collective-permute-start = (bf16[128,256]{1,0:T(8,128)(2,1)}, bf16[128,256]{1,0:T(8,128)(2,1)S(1)}, u32[]{:S(2)}, u32[]{:S(2)}) collective-permute-start(bf16[128,256]{1,0:T(8,128)(2,1)} %get-tuple-element.11), channel_id=1, source_target_pairs={{0,3},{1,2},{2,1},{3,0},{4,7},{5,6},{6,5},{7,4},{8,11},{9,10},{10,... | collective-permute-start | bytes 196616 | tf_op jit(solution)/shard_map/ppermute | solution.py:347
  8.9 0.0 collective-permute-start.1
  8.9 2.8 %collective-permute-done = bf16[128,256]{1,0:T(8,128)(2,1)S(1)} collective-permute-done((bf16[128,256]{1,0:T(8,128)(2,1)}, bf16[128,256]{1,0:T(8,128)(2,1)S(1)}, u32[]{:S(2)}, u32[]{:S(2)}) %collective-permute-start) | collective-permute-done | bytes 65568 | tf_op jit(solution)/shard_map/ppermute | solution.py:347
  11.7 1.7 %collective-permute-done.1 = bf16[128,256]{1,0:T(8,128)(2,1)S(1)} collective-permute-done((bf16[128,256]{1,0:T(8,128)(2,1)}, bf16[128,256]{1,0:T(8,128)(2,1)S(1)}, u32[]{:S(2)}, u32[]{:S(2)}) %collective-permute-start.1) | collective-permute-done | bytes 65568 | tf_op jit(solution)/shard_map/ppermute | solution.py:347
  13.4 0.0 collective-permute-done.2
  13.4 0.9 %constant_dynamic-update-slice_fusion.4 = (bf16[640,256]{1,0:T(8,128)(2,1)S(1)}, bf16[128,256]{1,0:T(8,128)(2,1)S(1)}) fusion(f32[128,256]{1,0:T(8,128)S(1)} %collective-permute-done.2, bf16[128,256]{1,0:T(8,128)(2,1)S(1)} %collective-permute-done.1, f32[128,256]{1,0:T(8,128)} %get-tuple-element.10, bf16[128,256]{1,0:T(8,128)(2,1)S(1)} %collective-permute-done), kind=kLoop, calls=%fused_computation.7 | loop fusion | flops 196607 | bytes 524288
  14.3 0.7 pad_maximum_fusion
  15.0 1.6 %collective-permute-start.3 = (bf16[160,256]{1,0:T(8,128)(2,1)S(1)}, bf16[160,256]{1,0:T(8,128)(2,1)S(1)}, u32[]{:S(2)}, u32[]{:S(2)}) collective-permute-start(bf16[160,256]{1,0:T(8,128)(2,1)S(1)} %pad_maximum_fusion), channel_id=1, source_target_pairs={{0,8},{4,12},{8,0},{12,4},{16,24},{20,28},{24,16},{28,20},{1,9},{5... | collective-permute-start | bytes 245768 | tf_op jit(solution)/shard_map/ppermute | solution.py:347
  16.6 2.6 %collective-permute-start.4 = (bf16[160,256]{1,0:T(8,128)(2,1)S(1)}, bf16[160,256]{1,0:T(8,128)(2,1)S(1)}, u32[]{:S(2)}, u32[]{:S(2)}) collective-permute-start(bf16[160,256]{1,0:T(8,128)(2,1)S(1)} %pad_maximum_fusion), channel_id=1, source_target_pairs={{0,16},{4,20},{8,24},{12,28},{16,0},{20,4},{24,8},{28,12},{1,17},{... | collective-permute-start | bytes 245768 | tf_op jit(solution)/shard_map/ppermute | solution.py:347
  19.2 0.2 collective-permute-start.5
  19.4 0.7 constant_dynamic-update-slice_fusion.3
  20.1 0.1 collective-permute-done.3
  20.3 3.9 %collective-permute-done.4 = bf16[160,256]{1,0:T(8,128)(2,1)S(1)} collective-permute-done((bf16[160,256]{1,0:T(8,128)(2,1)S(1)}, bf16[160,256]{1,0:T(8,128)(2,1)S(1)}, u32[]{:S(2)}, u32[]{:S(2)}) %collective-permute-start.4) | collective-permute-done | bytes 81952 | tf_op jit(solution)/shard_map/ppermute | solution.py:347
  24.2 1.4 %collective-permute-done.5 = bf16[160,256]{1,0:T(8,128)(2,1)S(1)} collective-permute-done((bf16[160,256]{1,0:T(8,128)(2,1)S(1)}, bf16[160,256]{1,0:T(8,128)(2,1)S(1)}, u32[]{:S(2)}, u32[]{:S(2)}) %collective-permute-start.5) | collective-permute-done | bytes 81952 | tf_op jit(solution)/shard_map/ppermute | solution.py:347
  25.5 1.5 %collective-permute-start.8 = (bf16[640,256]{1,0:T(8,128)(2,1)S(1)}, bf16[640,256]{1,0:T(8,128)(2,1)S(1)}, u32[]{:S(2)}, u32[]{:S(2)}) collective-permute-start(bf16[640,256]{1,0:T(8,128)(2,1)S(1)} %constant_dynamic-update-slice_fusion.refs_0_), channel_id=1, source_target_pairs={{0,2},{1,3},{2,0},{3,1},{4,6},{5,7},{6,4},{7,5},{8,10},{9,11},{10,... | collective-permute-start | bytes 983048 | tf_op jit(solution)/shard_map/ppermute | solution.py:347
  27.1 1.5 %collective-permute-start.7 = (bf16[640,256]{1,0:T(8,128)(2,1)S(1)}, bf16[640,256]{1,0:T(8,128)(2,1)S(1)}, u32[]{:S(2)}, u32[]{:S(2)}) collective-permute-start(bf16[640,256]{1,0:T(8,128)(2,1)S(1)} %constant_dynamic-update-slice_fusion.refs_0_), channel_id=1, source_target_pairs={{0,4},{4,0},{8,12},{12,8},{16,20},{20,16},{24,28},{28,24},{1,5},{5... | collective-permute-start | bytes 983048 | tf_op jit(solution)/shard_map/ppermute | solution.py:347
  28.6 0.0 collective-permute-start.6
  28.6 4.3 %collective-permute-done.8.refs_1_.refs_3_ = bf16[640,256]{1,0:T(8,128)(2,1)S(1)} collective-permute-done((bf16[640,256]{1,0:T(8,128)(2,1)S(1)}, bf16[640,256]{1,0:T(8,128)(2,1)S(1)}, u32[]{:S(2)}, u32[]{:S(2)}) %collective-permute-start.8) | collective-permute-done | bytes 327712 | tf_op jit(solution)/shard_map/ppermute | solution.py:347
  32.9 0.0 collective-permute-start.10
  32.9 1.5 %collective-permute-done.7.refs_0_.refs_2_ = bf16[640,256]{1,0:T(8,128)(2,1)S(1)} collective-permute-done((bf16[640,256]{1,0:T(8,128)(2,1)S(1)}, bf16[640,256]{1,0:T(8,128)(2,1)S(1)}, u32[]{:S(2)}, u32[]{:S(2)}) %collective-permute-start.7) | collective-permute-done | bytes 327712 | tf_op jit(solution)/shard_map/ppermute | solution.py:347
  34.3 0.0 collective-permute-start.9
  34.3 1.6 %collective-permute-start.11 = (bf16[320,256]{1,0:T(8,128)(2,1)S(1)}, bf16[320,256]{1,0:T(8,128)(2,1)S(1)}, u32[]{:S(2)}, u32[]{:S(2)}) collective-permute-start(bf16[320,256]{1,0:T(8,128)(2,1)S(1)} %slice.8), channel_id=1, source_target_pairs={{0,4},{4,0},{8,12},{12,8},{16,20},{20,16},{24,28},{28,24},{1,5},{5... | collective-permute-start | bytes 491528 | tf_op jit(solution)/shard_map/ppermute | solution.py:347
  35.9 0.9 %collective-permute-start.12 = (bf16[320,256]{1,0:T(8,128)(2,1)S(1)}, bf16[320,256]{1,0:T(8,128)(2,1)S(1)}, u32[]{:S(2)}, u32[]{:S(2)}) collective-permute-start(bf16[320,256]{1,0:T(8,128)(2,1)S(1)} %slice.9), channel_id=1, source_target_pairs={{0,2},{1,3},{2,0},{3,1},{4,6},{5,7},{6,4},{7,5},{8,10},{9,11},{10,... | collective-permute-start | bytes 491528 | tf_op jit(solution)/shard_map/ppermute | solution.py:347
  36.8 4.2 %collective-permute-done.11.refs_6_ = bf16[320,256]{1,0:T(8,128)(2,1)S(1)} collective-permute-done((bf16[320,256]{1,0:T(8,128)(2,1)S(1)}, bf16[320,256]{1,0:T(8,128)(2,1)S(1)}, u32[]{:S(2)}, u32[]{:S(2)}) %collective-permute-start.11) | collective-permute-done | bytes 163872 | tf_op jit(solution)/shard_map/ppermute | solution.py:347
  41.0 0.0 collective-permute-start.13
  41.0 1.3 %collective-permute-done.12.refs_7_ = bf16[320,256]{1,0:T(8,128)(2,1)S(1)} collective-permute-done((bf16[320,256]{1,0:T(8,128)(2,1)S(1)}, bf16[320,256]{1,0:T(8,128)(2,1)S(1)}, u32[]{:S(2)}, u32[]{:S(2)}) %collective-permute-start.12) | collective-permute-done | bytes 163872 | tf_op jit(solution)/shard_map/ppermute | solution.py:347
  42.3 0.0 collective-permute-start.14
  42.3 2.3 %column_pieces.1.refs_10_ = bf16[2048,128]{1,0:T(8,128)(2,1)} custom-call(f32[64,4096]{1,0:T(8,128)} %bitcast.4), custom_call_target="tpu_custom_call" | custom-call | bytes 2097152 | tf_op jit(solution)/shard_map/column_pieces/pallas_call | solution.py:190
  44.6 0.0 collective-permute-done.6.refs_1_
  44.6 0.0 copy-done.2
  44.6 0.7 copy-done.3
  45.4 2.1 %sketch_gram.2.refs_4_ = f32[256,256]{1,0:T(8,128)} custom-call(bf16[640,256]{1,0:T(8,128)(2,1)} %copy-done.2, bf16[640,256]{1,0:T(8,128)(2,1)} %copy-done.3), custom_call_target="tpu_custom_call" | custom-call | flops 167772160 | bytes 1179648 | tf_op jit(solution)/shard_map/sketch_gram/pallas_call | solution.py:222
  47.5 0.0 collective-permute-done.10.refs_3_.refs_5_
  47.5 0.0 collective-permute-done.9.refs_2_.refs_4_
  47.5 0.0 copy-done
  47.5 0.7 copy-done.4
  48.2 0.7 copy-done.5
  48.9 2.5 %sketch_gram.3.refs_11_ = f32[256,256]{1,0:T(8,128)} custom-call(bf16[640,256]{1,0:T(8,128)(2,1)} %copy-done.1, bf16[640,256]{1,0:T(8,128)(2,1)} %copy-done, bf16[640,256]{1,0:T(8,128)(2,1)} %copy-done.5, bf16[640,256]{1,0:T(8,128)(2,1)} %copy-done.4, f32[256,256]{1,0:T(8,128)} %sketch_gram.2.refs_4_), custom_call_target="tpu_custom_call" | custom-call | flops 335544320 | bytes 1835008 | tf_op jit(solution)/shard_map/sketch_gram/pallas_call | solution.py:222
  51.5 0.0 collective-permute-done.13.refs_8_
  51.5 0.0 collective-permute-done.14.refs_9_
  51.5 0.6 copy-done.8
  52.2 0.7 copy-done.9
  52.8 16.0 %factor_and_project.1 = (f32[64,512]{1,0:T(8,128)}, f32[32,4096]{1,0:T(8,128)}, bf16[32,2048]{1,0:T(8,128)(2,1)}) custom-call(bf16[640,256]{1,0:T(8,128)(2,1)} %copy-done.2, bf16[640,256]{1,0:T(8,128)(2,1)} %copy-done.3, bf16[640,256]{1,0:T(8,128)(2,1)} %copy-done.1, bf16[640,256]{1,0:T(8,128)(2,1)} %copy-done, bf16[640,256]{1,0:T(8,128)(2,1)} %copy-done.5, ...), custom_call_target="tpu_custom_call" | custom-call | tf_op jit(solution)/shard_map/factor_and_project/pallas_call | solution.py:322
  68.9 0.7 collective-permute-start.15
  69.6 5.4 %collective-permute-done.15 = bf16[32,2048]{1,0:T(8,128)(2,1)S(1)} collective-permute-done((bf16[32,2048]{1,0:T(8,128)(2,1)}, bf16[32,2048]{1,0:T(8,128)(2,1)S(1)}, u32[]{:S(2)}, u32[]{:S(2)}) %collective-permute-start.15) | collective-permute-done | bytes 131104 | tf_op jit(solution)/shard_map/ppermute | solution.py:347
  75.0 0.7 convert_dynamic-update-slice_fusion
  (18 shorter events, 0.1 us)
Async XLA Ops:
  5.8 7.6 %collective-permute-start.2 = (f32[128,256]{1,0:T(8,128)}, f32[128,256]{1,0:T(8,128)S(1)}, u32[]{:S(2)}, u32[]{:S(2)}) collective-permute-start(f32[128,256]{1,0:T(8,128)} %get-tuple-element.13), channel_id=1, source_target_pairs={{0,1},{1,0},{2,3},{3,2},{4,5},{5,4},{6,7},{7,6},{8,9},{9,8},{10,11... | collective-permute-start | bytes 393224 | tf_op jit(solution)/shard_map/ppermute | solution.py:347
  6.3 5.4 %collective-permute-start = (bf16[128,256]{1,0:T(8,128)(2,1)}, bf16[128,256]{1,0:T(8,128)(2,1)S(1)}, u32[]{:S(2)}, u32[]{:S(2)}) collective-permute-start(bf16[128,256]{1,0:T(8,128)(2,1)} %get-tuple-element.11), channel_id=1, source_target_pairs={{0,3},{1,2},{2,1},{3,0},{4,7},{5,6},{6,5},{7,4},{8,11},{9,10},{10,... | collective-permute-start | bytes 196616 | tf_op jit(solution)/shard_map/ppermute | solution.py:347
  8.9 4.5 %collective-permute-start.1 = (bf16[128,256]{1,0:T(8,128)(2,1)}, bf16[128,256]{1,0:T(8,128)(2,1)S(1)}, u32[]{:S(2)}, u32[]{:S(2)}) collective-permute-start(bf16[128,256]{1,0:T(8,128)(2,1)} %get-tuple-element.12), channel_id=1, source_target_pairs={{0,2},{1,3},{2,0},{3,1},{4,6},{5,7},{6,4},{7,5},{8,10},{9,11},{10,... | collective-permute-start | bytes 196616 | tf_op jit(solution)/shard_map/ppermute | solution.py:347
  15.0 5.3 %collective-permute-start.3 = (bf16[160,256]{1,0:T(8,128)(2,1)S(1)}, bf16[160,256]{1,0:T(8,128)(2,1)S(1)}, u32[]{:S(2)}, u32[]{:S(2)}) collective-permute-start(bf16[160,256]{1,0:T(8,128)(2,1)S(1)} %pad_maximum_fusion), channel_id=1, source_target_pairs={{0,8},{4,12},{8,0},{12,4},{16,24},{20,28},{24,16},{28,20},{1,9},{5... | collective-permute-start | bytes 245768 | tf_op jit(solution)/shard_map/ppermute | solution.py:347
  16.6 7.6 %collective-permute-start.4 = (bf16[160,256]{1,0:T(8,128)(2,1)S(1)}, bf16[160,256]{1,0:T(8,128)(2,1)S(1)}, u32[]{:S(2)}, u32[]{:S(2)}) collective-permute-start(bf16[160,256]{1,0:T(8,128)(2,1)S(1)} %pad_maximum_fusion), channel_id=1, source_target_pairs={{0,16},{4,20},{8,24},{12,28},{16,0},{20,4},{24,8},{28,12},{1,17},{... | collective-permute-start | bytes 245768 | tf_op jit(solution)/shard_map/ppermute | solution.py:347
  19.2 6.3 %collective-permute-start.5 = (bf16[160,256]{1,0:T(8,128)(2,1)S(1)}, bf16[160,256]{1,0:T(8,128)(2,1)S(1)}, u32[]{:S(2)}, u32[]{:S(2)}) collective-permute-start(bf16[160,256]{1,0:T(8,128)(2,1)S(1)} %pad_maximum_fusion), channel_id=1, source_target_pairs={{0,24},{4,28},{8,16},{12,20},{16,8},{20,12},{24,0},{28,4},{1,25},{... | collective-permute-start | bytes 245768 | tf_op jit(solution)/shard_map/ppermute | solution.py:347
  25.5 19.1 %copy-start.2 = (bf16[640,256]{1,0:T(8,128)(2,1)}, bf16[640,256]{1,0:T(8,128)(2,1)S(1)}, u32[]{:S(2)}) copy-start(bf16[640,256]{1,0:T(8,128)(2,1)S(1)} %constant_dynamic-update-slice_fusion.refs_0_) | copy-start | bytes 983044
  25.5 7.3 %collective-permute-start.8 = (bf16[640,256]{1,0:T(8,128)(2,1)S(1)}, bf16[640,256]{1,0:T(8,128)(2,1)S(1)}, u32[]{:S(2)}, u32[]{:S(2)}) collective-permute-start(bf16[640,256]{1,0:T(8,128)(2,1)S(1)} %constant_dynamic-update-slice_fusion.refs_0_), channel_id=1, source_target_pairs={{0,2},{1,3},{2,0},{3,1},{4,6},{5,7},{6,4},{7,5},{8,10},{9,11},{10,... | collective-permute-start | bytes 983048 | tf_op jit(solution)/shard_map/ppermute | solution.py:347
  27.1 7.2 %collective-permute-start.7 = (bf16[640,256]{1,0:T(8,128)(2,1)S(1)}, bf16[640,256]{1,0:T(8,128)(2,1)S(1)}, u32[]{:S(2)}, u32[]{:S(2)}) collective-permute-start(bf16[640,256]{1,0:T(8,128)(2,1)S(1)} %constant_dynamic-update-slice_fusion.refs_0_), channel_id=1, source_target_pairs={{0,4},{4,0},{8,12},{12,8},{16,20},{20,16},{24,28},{28,24},{1,5},{5... | collective-permute-start | bytes 983048 | tf_op jit(solution)/shard_map/ppermute | solution.py:347
  28.6 16.0 %collective-permute-start.6 = (bf16[640,256]{1,0:T(8,128)(2,1)S(1)}, bf16[640,256]{1,0:T(8,128)(2,1)S(1)}, u32[]{:S(2)}, u32[]{:S(2)}) collective-permute-start(bf16[640,256]{1,0:T(8,128)(2,1)S(1)} %constant_dynamic-update-slice_fusion.refs_0_), channel_id=1, source_target_pairs={{0,1},{1,0},{2,3},{3,2},{4,5},{5,4},{6,7},{7,6},{8,9},{9,8},{10,11... | collective-permute-start | bytes 983048 | tf_op jit(solution)/shard_map/ppermute | solution.py:347
  32.9 14.6 %copy-start = (bf16[640,256]{1,0:T(8,128)(2,1)}, bf16[640,256]{1,0:T(8,128)(2,1)S(1)}, u32[]{:S(2)}) copy-start(bf16[640,256]{1,0:T(8,128)(2,1)S(1)} %collective-permute-done.8.refs_1_.refs_3_) | copy-start | bytes 983044
  32.9 14.6 %collective-permute-start.10 = (bf16[640,256]{1,0:T(8,128)(2,1)S(1)}, bf16[640,256]{1,0:T(8,128)(2,1)S(1)}, u32[]{:S(2)}, u32[]{:S(2)}) collective-permute-start(bf16[640,256]{1,0:T(8,128)(2,1)S(1)} %collective-permute-done.8.refs_1_.refs_3_), channel_id=1, source_target_pairs={{0,1},{1,0},{2,3},{3,2},{4,5},{5,4},{6,7},{7,6},{8,9},{9,8},{10,11... | collective-permute-start | bytes 983048 | tf_op jit(solution)/shard_map/ppermute | solution.py:347
  34.3 13.2 %copy-start.1 = (bf16[640,256]{1,0:T(8,128)(2,1)}, bf16[640,256]{1,0:T(8,128)(2,1)S(1)}, u32[]{:S(2)}) copy-start(bf16[640,256]{1,0:T(8,128)(2,1)S(1)} %collective-permute-done.7.refs_0_.refs_2_) | copy-start | bytes 983044
  34.3 13.2 %collective-permute-start.9 = (bf16[640,256]{1,0:T(8,128)(2,1)S(1)}, bf16[640,256]{1,0:T(8,128)(2,1)S(1)}, u32[]{:S(2)}, u32[]{:S(2)}) collective-permute-start(bf16[640,256]{1,0:T(8,128)(2,1)S(1)} %collective-permute-done.7.refs_0_.refs_2_), channel_id=1, source_target_pairs={{0,1},{1,0},{2,3},{3,2},{4,5},{5,4},{6,7},{7,6},{8,9},{9,8},{10,11... | collective-permute-start | bytes 983048 | tf_op jit(solution)/shard_map/ppermute | solution.py:347
  34.3 6.7 %collective-permute-start.11 = (bf16[320,256]{1,0:T(8,128)(2,1)S(1)}, bf16[320,256]{1,0:T(8,128)(2,1)S(1)}, u32[]{:S(2)}, u32[]{:S(2)}) collective-permute-start(bf16[320,256]{1,0:T(8,128)(2,1)S(1)} %slice.8), channel_id=1, source_target_pairs={{0,4},{4,0},{8,12},{12,8},{16,20},{20,16},{24,28},{28,24},{1,5},{5... | collective-permute-start | bytes 491528 | tf_op jit(solution)/shard_map/ppermute | solution.py:347
  35.9 6.4 %collective-permute-start.12 = (bf16[320,256]{1,0:T(8,128)(2,1)S(1)}, bf16[320,256]{1,0:T(8,128)(2,1)S(1)}, u32[]{:S(2)}, u32[]{:S(2)}) collective-permute-start(bf16[320,256]{1,0:T(8,128)(2,1)S(1)} %slice.9), channel_id=1, source_target_pairs={{0,2},{1,3},{2,0},{3,1},{4,6},{5,7},{6,4},{7,5},{8,10},{9,11},{10,... | collective-permute-start | bytes 491528 | tf_op jit(solution)/shard_map/ppermute | solution.py:347
  41.0 10.5 %copy-start.6 = (bf16[320,256]{1,0:T(8,128)(2,1)}, bf16[320,256]{1,0:T(8,128)(2,1)S(1)}, u32[]{:S(2)}) copy-start(bf16[320,256]{1,0:T(8,128)(2,1)S(1)} %collective-permute-done.11.refs_6_) | copy-start | bytes 491524
  41.0 10.5 %collective-permute-start.13 = (bf16[320,256]{1,0:T(8,128)(2,1)S(1)}, bf16[320,256]{1,0:T(8,128)(2,1)S(1)}, u32[]{:S(2)}, u32[]{:S(2)}) collective-permute-start(bf16[320,256]{1,0:T(8,128)(2,1)S(1)} %collective-permute-done.11.refs_6_), channel_id=1, source_target_pairs={{0,1},{1,0},{2,3},{3,2},{4,5},{5,4},{6,7},{7,6},{8,9},{9,8},{10,11... | collective-permute-start | bytes 491528 | tf_op jit(solution)/shard_map/ppermute | solution.py:347
  42.3 9.2 %copy-start.7 = (bf16[320,256]{1,0:T(8,128)(2,1)}, bf16[320,256]{1,0:T(8,128)(2,1)S(1)}, u32[]{:S(2)}) copy-start(bf16[320,256]{1,0:T(8,128)(2,1)S(1)} %collective-permute-done.12.refs_7_) | copy-start | bytes 491524
  42.3 9.2 %collective-permute-start.14 = (bf16[320,256]{1,0:T(8,128)(2,1)S(1)}, bf16[320,256]{1,0:T(8,128)(2,1)S(1)}, u32[]{:S(2)}, u32[]{:S(2)}) collective-permute-start(bf16[320,256]{1,0:T(8,128)(2,1)S(1)} %collective-permute-done.12.refs_7_), channel_id=1, source_target_pairs={{0,1},{1,0},{2,3},{3,2},{4,5},{5,4},{6,7},{7,6},{8,9},{9,8},{10,11... | collective-permute-start | bytes 491528 | tf_op jit(solution)/shard_map/ppermute | solution.py:347
  44.6 0.7 copy-start.3
  47.5 0.7 copy-start.4
  48.2 0.7 copy-start.5
  51.5 0.7 copy-start.8
  52.2 0.7 copy-start.9
  68.9 6.1 %collective-permute-start.15 = (bf16[32,2048]{1,0:T(8,128)(2,1)}, bf16[32,2048]{1,0:T(8,128)(2,1)S(1)}, u32[]{:S(2)}, u32[]{:S(2)}) collective-permute-start(bf16[32,2048]{1,0:T(8,128)(2,1)} %get-tuple-element.17), channel_id=1, source_target_pairs={{0,4},{4,0},{8,12},{12,8},{16,20},{20,16},{24,28},{28,24},{1,5},{5... | collective-permute-start | bytes 393224 | tf_op jit(solution)/shard_map/ppermute | solution.py:347

commit v5 on v4

--- a/solution.py
+++ b/solution.py
@@ -193,6 +193,7 @@
         cost_estimate=pl.CostEstimate(
             flops=0, bytes_accessed=4 * y_t.size + 4 * width * cols, transcendentals=0
         ),
+        compiler_params=pltpu.CompilerParams(vmem_limit_bytes=24 * 2**20),
         name="column_pieces",
     )(y_t)
 
@@ -227,20 +228,16 @@
             bytes_accessed=2 * sum(a.size for a in pieces) + 8 * columns * columns,
             transcendentals=0,
         ),
+        compiler_params=pltpu.CompilerParams(vmem_limit_bytes=24 * 2**20),
         name="sketch_gram",
     )(*pieces, *(() if first else (carry,)))
 
 
-def final_kernel(places, depth, early, late, groups, *refs):
+def final_kernel(places, depth, early, groups, *refs):
     count = sum(groups)
     parts, refs = refs[:count], refs[count:]
     (y2_ref, g_ref), refs = refs[:2], refs[2:]
-    basis_ref, projected_ref, given_ref, w, s, z, x2, *landed, arrived = refs
-    copies = []
-    for i, a in enumerate(landed):
-        copies.append(pltpu.make_async_copy(parts[count - len(landed) + i], a, arrived.at[i]))
-        copies[-1].start()
-    parts = parts[: count - len(landed)] + tuple(landed)
+    basis_ref, projected_ref, given_ref, w, s, z, x2 = refs
     columns = g_ref.shape[0]
     cols = z.shape[0]
     width = y2_ref.shape[1] // 2
@@ -266,10 +263,7 @@
                     rows.append(jnp.concatenate([a, a], axis=1))
         return jnp.concatenate(rows, axis=0)
 
-    gram = gram_of([sketch(n) for n in range(early, late)], g_ref[...])
-    for copy in copies:
-        copy.wait()
-    gram = gram_of([sketch(n) for n in range(late, len(groups))], gram)
+    gram = gram_of([sketch(n) for n in range(early, len(groups))], g_ref[...])
 
     sub = 256
     work = [(i, n) for i in range(cols // sub) for n in range(len(groups))]
@@ -311,21 +305,15 @@
     basis_ref[...] = both[:own_c] + both[own_c:]
 
 
-def final_call(groups, early, late, y2, gram, places, quarter, depth, own_r, own_c):
+def final_call(groups, early, y2, gram, places, quarter, depth, own_r, own_c):
     columns = gram.shape[0]
     parts = [a for group in groups for a in group]
     counts = [len(group) for group in groups]
-    landing = parts[sum(counts[:late]) :]
-    whole = lambda shape: pl.BlockSpec(shape, lambda i: (0, 0))
     height = quarter * len(places)
+    tall = sum(a.shape[0] for a in groups[0]) // (quarter + depth) * quarter
     cols = y2.shape[0]
     return pl.pallas_call(
-        lambda *refs: final_kernel(places, depth, early, late, counts, *refs),
-        grid=(1,),
-        in_specs=[whole(a.shape) for a in parts[: len(parts) - len(landing)]]
-        + [pl.BlockSpec(memory_space=pltpu.HBM) for _ in landing]
-        + [whole(y2.shape), whole(gram.shape)],
-        out_specs=[whole((own_c, height)), whole((own_r, 2 * cols)), whole((own_r, cols))],
+        lambda *refs: final_kernel(places, depth, early, counts, *refs),
         out_shape=[
             jax.ShapeDtypeStruct((own_c, height), F32),
             jax.ShapeDtypeStruct((own_r, 2 * cols), F32),
@@ -335,10 +323,9 @@
             pltpu.VMEM((columns, columns), F32),
             pltpu.VMEM((height, columns), BF16),
             pltpu.VMEM((cols, columns), F32),
-            pltpu.VMEM((len(groups), sum(a.shape[0] for a in groups[0]) // (quarter + depth) * quarter, y2.shape[1]), BF16),
-        ]
-        + [pltpu.VMEM(a.shape, BF16) for a in landing]
-        + [pltpu.SemaphoreType.DMA((len(landing),))],
+            pltpu.VMEM((len(groups), tall, y2.shape[1]), BF16),
+        ],
+        compiler_params=pltpu.CompilerParams(vmem_limit_bytes=40 * 2**20),
         name="factor_and_project",
     )(*parts, y2, gram)
 
@@ -402,7 +389,7 @@
 
             places.append((place, n))
     basis_t, projected, given = final_call(
-        groups, early, early + len(far), y2, gram, places, quarter, depth, columns // rows, columns // cols
+        groups, early, y2, gram, places, quarter, depth, columns // rows, columns // cols
     )
     there = swap(given, "rows", 1).astype(F32)
     projected = lax.dynamic_update_slice_in_dim(

time: 76.1 us -> 63.8 us (0.84)
  Pallas kernels: 28.1 us -> 19.5 us
  local copies, waits for them, and re-layouts: 4.26 us -> 0.76 us
    pallas_call x2, Pallas kernels: 4.66 us -> 0.82 us  [gram_call(): pl.pallas_call(lambda *refs: gram_kernel(quarter, depth, len(pieces), fir...]
    unnamed x23 -> x5, local copies, waits for them, and re-layouts: 4.23 us -> 0.74 us
    pallas_call x1, Pallas kernels: 16 us -> 13.3 us  [final_call(): pl.pallas_call(lambda *refs: final_kernel(places, depth, early, counts, *...]
    pallas_call x1, Pallas kernels: 2.29 us -> 0.19 us  [columns_call(): pl.pallas_call(columns_kernel, out_shape=jax.ShapeDtypeStruct((cols // 2,...]
  transfers between devices with their start and end apart: 16 -> 16, of which waited for: 10 -> 11; matrix products, arithmetic and copies ran while one was open for 1% -> 1% of each run, Pallas kernels for 9% -> 2%
where the time goes in v5:
time: 63.8 us; the launch traced here: 63.4 us
  waiting for transfers between devices  26.5 us (42%)
  Pallas kernels  19.5 us (31%)
  starting transfers between devices  13.5 us (21%)
  other arithmetic  2.38 us (4%)
  local copies, waits for them, and re-layouts  0.76 us (1%)
  between operations  0.72 us (1%)
    ppermute x16, waiting for transfers between devices, swap(): lax.ppermute(a, axis, [(i, i ^ bits) for i in range(lax.axis_size(axis))])  26.5 us
    ppermute x16, starting transfers between devices, swap(): lax.ppermute(a, axis, [(i, i ^ bits) for i in range(lax.axis_size(axis))])  13.5 us
    pallas_call x1, Pallas kernels, final_call(): pl.pallas_call(lambda *refs: final_kernel(places, depth, early, counts, *...  13.3 us
    pallas_call x1, Pallas kernels, sketch_call(): pl.pallas_call(lambda *refs: sketch_kernel(scale, quarter, *refs), grid=(...  5.19 us
  transfers between devices with their start and end apart: 16, of which 11 were waited for; matrix products, arithmetic and copies ran while one was open for 1% of the time, Pallas kernels for 2%

profile of v5, /device:TPU:0, one launch (start us, length us, event | category | flops | bytes accessed | tf_op | source)
XLA Modules:
  0.0 63.4 jit_solution(8923647839784915067)
XLA Ops:
  0.6 0.0 copy-start
  0.6 5.2 %sketch_tile.1 = (bf16[32,256]{1,0:T(8,128)(2,1)}, f32[128,256]{1,0:T(8,128)}, f32[128,256]{1,0:T(8,128)}, bf16[128,256]{1,0:T(8,128)(2,1)}, bf16[128,256]{1,0:T(8,128)(2,1)}) custom-call(f32[64,512]{1,0:T(8,128)} %bitcast.5, f32[64,4096]{1,0:T(8,128)} %bitcast.3, bf16[4096,256]{1,0:T(8,128)(2,1)} %refs_2_.1), custom_call_target="tpu_custom_call" | custom-call | tf_op jit(solution)/shard_map/sketch_tile/pallas_call | solution.py:162
  5.8 0.5 collective-permute-start.2
  6.3 2.6 %collective-permute-start = (bf16[128,256]{1,0:T(8,128)(2,1)}, bf16[128,256]{1,0:T(8,128)(2,1)S(1)}, u32[]{:S(2)}, u32[]{:S(2)}) collective-permute-start(bf16[128,256]{1,0:T(8,128)(2,1)} %get-tuple-element.11), channel_id=1, source_target_pairs={{0,3},{1,2},{2,1},{3,0},{4,7},{5,6},{6,5},{7,4},{8,11},{9,10},{10,... | collective-permute-start | bytes 196616 | tf_op jit(solution)/shard_map/ppermute | solution.py:334
  8.9 0.0 collective-permute-start.1
  9.0 2.8 %collective-permute-done = bf16[128,256]{1,0:T(8,128)(2,1)S(1)} collective-permute-done((bf16[128,256]{1,0:T(8,128)(2,1)}, bf16[128,256]{1,0:T(8,128)(2,1)S(1)}, u32[]{:S(2)}, u32[]{:S(2)}) %collective-permute-start) | collective-permute-done | bytes 65568 | tf_op jit(solution)/shard_map/ppermute | solution.py:334
  11.7 1.7 %collective-permute-done.1 = bf16[128,256]{1,0:T(8,128)(2,1)S(1)} collective-permute-done((bf16[128,256]{1,0:T(8,128)(2,1)}, bf16[128,256]{1,0:T(8,128)(2,1)S(1)}, u32[]{:S(2)}, u32[]{:S(2)}) %collective-permute-start.1) | collective-permute-done | bytes 65568 | tf_op jit(solution)/shard_map/ppermute | solution.py:334
  13.4 0.0 collective-permute-done.2
  13.4 0.9 %constant_dynamic-update-slice_fusion.4 = (bf16[640,256]{1,0:T(8,128)(2,1)S(1)}, bf16[128,256]{1,0:T(8,128)(2,1)S(1)}) fusion(f32[128,256]{1,0:T(8,128)S(1)} %collective-permute-done.2, bf16[128,256]{1,0:T(8,128)(2,1)S(1)} %collective-permute-done.1, f32[128,256]{1,0:T(8,128)} %get-tuple-element.10, bf16[128,256]{1,0:T(8,128)(2,1)S(1)} %collective-permute-done), kind=kLoop, calls=%fused_computation.7 | loop fusion | flops 196607 | bytes 524288
  14.4 0.7 %pad_maximum_fusion = bf16[160,256]{1,0:T(8,128)(2,1)S(1)} fusion(bf16[32,256]{1,0:T(8,128)(2,1)} %get-tuple-element.14, bf16[128,256]{1,0:T(8,128)(2,1)S(1)} %get-tuple-element.19), kind=kLoop, calls=%fused_computation.2 | loop fusion | flops 163840 | bytes 163840 | tf_op jit(solution)/shard_map/concatenate | solution.py:354
  15.1 1.6 %collective-permute-start.3 = (bf16[160,256]{1,0:T(8,128)(2,1)S(1)}, bf16[160,256]{1,0:T(8,128)(2,1)S(1)}, u32[]{:S(2)}, u32[]{:S(2)}) collective-permute-start(bf16[160,256]{1,0:T(8,128)(2,1)S(1)} %pad_maximum_fusion), channel_id=1, source_target_pairs={{0,8},{4,12},{8,0},{12,4},{16,24},{20,28},{24,16},{28,20},{1,9},{5... | collective-permute-start | bytes 245768 | tf_op jit(solution)/shard_map/ppermute | solution.py:334
  16.7 2.6 %collective-permute-start.4 = (bf16[160,256]{1,0:T(8,128)(2,1)S(1)}, bf16[160,256]{1,0:T(8,128)(2,1)S(1)}, u32[]{:S(2)}, u32[]{:S(2)}) collective-permute-start(bf16[160,256]{1,0:T(8,128)(2,1)S(1)} %pad_maximum_fusion), channel_id=1, source_target_pairs={{0,16},{4,20},{8,24},{12,28},{16,0},{20,4},{24,8},{28,12},{1,17},{... | collective-permute-start | bytes 245768 | tf_op jit(solution)/shard_map/ppermute | solution.py:334
  19.3 0.2 collective-permute-start.5
  19.5 0.7 %constant_dynamic-update-slice_fusion.3 = bf16[640,256]{1,0:T(8,128)(2,1)S(1)} fusion(bf16[640,256]{1,0:T(8,128)(2,1)S(1)} %get-tuple-element.18, bf16[32,256]{1,0:T(8,128)(2,1)} %get-tuple-element.14), kind=kLoop, calls=%fused_computation.6 | loop fusion | bytes 32768
  20.2 0.1 collective-permute-done.3
  20.3 3.9 %collective-permute-done.4 = bf16[160,256]{1,0:T(8,128)(2,1)S(1)} collective-permute-done((bf16[160,256]{1,0:T(8,128)(2,1)S(1)}, bf16[160,256]{1,0:T(8,128)(2,1)S(1)}, u32[]{:S(2)}, u32[]{:S(2)}) %collective-permute-start.4) | collective-permute-done | bytes 81952 | tf_op jit(solution)/shard_map/ppermute | solution.py:334
  24.2 1.4 %collective-permute-done.5 = bf16[160,256]{1,0:T(8,128)(2,1)S(1)} collective-permute-done((bf16[160,256]{1,0:T(8,128)(2,1)S(1)}, bf16[160,256]{1,0:T(8,128)(2,1)S(1)}, u32[]{:S(2)}, u32[]{:S(2)}) %collective-permute-start.5) | collective-permute-done | bytes 81952 | tf_op jit(solution)/shard_map/ppermute | solution.py:334
  25.6 1.5 %collective-permute-start.8 = (bf16[640,256]{1,0:T(8,128)(2,1)S(1)}, bf16[640,256]{1,0:T(8,128)(2,1)S(1)}, u32[]{:S(2)}, u32[]{:S(2)}) collective-permute-start(bf16[640,256]{1,0:T(8,128)(2,1)S(1)} %constant_dynamic-update-slice_fusion.refs_0_), channel_id=1, source_target_pairs={{0,2},{1,3},{2,0},{3,1},{4,6},{5,7},{6,4},{7,5},{8,10},{9,11},{10,... | collective-permute-start | bytes 983048 | tf_op jit(solution)/shard_map/ppermute | solution.py:334
  27.1 1.5 %collective-permute-start.7 = (bf16[640,256]{1,0:T(8,128)(2,1)S(1)}, bf16[640,256]{1,0:T(8,128)(2,1)S(1)}, u32[]{:S(2)}, u32[]{:S(2)}) collective-permute-start(bf16[640,256]{1,0:T(8,128)(2,1)S(1)} %constant_dynamic-update-slice_fusion.refs_0_), channel_id=1, source_target_pairs={{0,4},{4,0},{8,12},{12,8},{16,20},{20,16},{24,28},{28,24},{1,5},{5... | collective-permute-start | bytes 983048 | tf_op jit(solution)/shard_map/ppermute | solution.py:334
  28.6 0.0 collective-permute-start.6
  28.6 4.3 %collective-permute-done.8.refs_1_.refs_3_ = bf16[640,256]{1,0:T(8,128)(2,1)S(1)} collective-permute-done((bf16[640,256]{1,0:T(8,128)(2,1)S(1)}, bf16[640,256]{1,0:T(8,128)(2,1)S(1)}, u32[]{:S(2)}, u32[]{:S(2)}) %collective-permute-start.8) | collective-permute-done | bytes 327712 | tf_op jit(solution)/shard_map/ppermute | solution.py:334
  32.9 0.0 collective-permute-start.10
  32.9 1.5 %collective-permute-done.7.refs_0_.refs_2_ = bf16[640,256]{1,0:T(8,128)(2,1)S(1)} collective-permute-done((bf16[640,256]{1,0:T(8,128)(2,1)S(1)}, bf16[640,256]{1,0:T(8,128)(2,1)S(1)}, u32[]{:S(2)}, u32[]{:S(2)}) %collective-permute-start.7) | collective-permute-done | bytes 327712 | tf_op jit(solution)/shard_map/ppermute | solution.py:334
  34.4 0.0 collective-permute-start.9
  34.4 1.6 %collective-permute-start.11 = (bf16[320,256]{1,0:T(8,128)(2,1)S(1)}, bf16[320,256]{1,0:T(8,128)(2,1)S(1)}, u32[]{:S(2)}, u32[]{:S(2)}) collective-permute-start(bf16[320,256]{1,0:T(8,128)(2,1)S(1)} %slice.8), channel_id=1, source_target_pairs={{0,4},{4,0},{8,12},{12,8},{16,20},{20,16},{24,28},{28,24},{1,5},{5... | collective-permute-start | bytes 491528 | tf_op jit(solution)/shard_map/ppermute | solution.py:334
  35.9 0.9 %collective-permute-start.12 = (bf16[320,256]{1,0:T(8,128)(2,1)S(1)}, bf16[320,256]{1,0:T(8,128)(2,1)S(1)}, u32[]{:S(2)}, u32[]{:S(2)}) collective-permute-start(bf16[320,256]{1,0:T(8,128)(2,1)S(1)} %slice.9), channel_id=1, source_target_pairs={{0,2},{1,3},{2,0},{3,1},{4,6},{5,7},{6,4},{7,5},{8,10},{9,11},{10,... | collective-permute-start | bytes 491528 | tf_op jit(solution)/shard_map/ppermute | solution.py:334
  36.8 4.2 %collective-permute-done.11.refs_6_ = bf16[320,256]{1,0:T(8,128)(2,1)S(1)} collective-permute-done((bf16[320,256]{1,0:T(8,128)(2,1)S(1)}, bf16[320,256]{1,0:T(8,128)(2,1)S(1)}, u32[]{:S(2)}, u32[]{:S(2)}) %collective-permute-start.11) | collective-permute-done | bytes 163872 | tf_op jit(solution)/shard_map/ppermute | solution.py:334
  41.0 0.0 collective-permute-start.13
  41.1 1.3 %collective-permute-done.12.refs_7_ = bf16[320,256]{1,0:T(8,128)(2,1)S(1)} collective-permute-done((bf16[320,256]{1,0:T(8,128)(2,1)S(1)}, bf16[320,256]{1,0:T(8,128)(2,1)S(1)}, u32[]{:S(2)}, u32[]{:S(2)}) %collective-permute-start.12) | collective-permute-done | bytes 163872 | tf_op jit(solution)/shard_map/ppermute | solution.py:334
  42.3 0.0 collective-permute-start.14
  42.3 0.0 copy-done
  42.4 0.2 column_pieces.1.refs_10_
  42.5 0.0 collective-permute-done.6.refs_1_
  42.6 0.3 sketch_gram.2.refs_4_
  42.9 0.0 collective-permute-done.10.refs_3_.refs_5_
  42.9 0.0 collective-permute-done.9.refs_2_.refs_4_
  42.9 0.5 sketch_gram.3.refs_11_
  43.4 0.0 collective-permute-done.13.refs_8_
  43.4 0.3 collective-permute-done.14.refs_9_
  43.7 13.3 %factor_and_project.1 = (f32[64,512]{1,0:T(8,128)}, f32[32,4096]{1,0:T(8,128)}, bf16[32,2048]{1,0:T(8,128)(2,1)S(1)}) custom-call(bf16[640,256]{1,0:T(8,128)(2,1)S(1)} %constant_dynamic-update-slice_fusion.refs_0_, bf16[640,256]{1,0:T(8,128)(2,1)S(1)} %collective-permute-done.6.refs_1_, bf16[640,256]{1,0:T(8,128)(2,1)S(1)} %collective-permute-done.7.refs_0_.refs_2_, ...), custom_call_target="tpu_custom_call" | custom-call | tf_op jit(solution)/shard_map/factor_and_project/pallas_call | solution.py:315
  57.1 0.5 collective-permute-start.15
  57.6 5.1 %collective-permute-done.15 = bf16[32,2048]{1,0:T(8,128)(2,1)S(1)} collective-permute-done((bf16[32,2048]{1,0:T(8,128)(2,1)S(1)}, bf16[32,2048]{1,0:T(8,128)(2,1)S(1)}, u32[]{:S(2)}, u32[]{:S(2)}) %collective-permute-start.15) | collective-permute-done | bytes 131104 | tf_op jit(solution)/shard_map/ppermute | solution.py:334
  62.7 0.7 %convert_dynamic-update-slice_fusion = f32[32,4096]{1,0:T(8,128)} fusion(f32[32,4096]{1,0:T(8,128)} %get-tuple-element.16, s32[]{:T(128)S(6)} %select_n.11, bf16[32,2048]{1,0:T(8,128)(2,1)S(1)} %collective-permute-done.15), kind=kLoop, calls=%fused_computation | loop fusion | flops 65536 | bytes 393220 | tf_op jit(solution)/shard_map/dynamic_update_slice | solution.py:395
  (5 shorter events, 0.0 us)
Async XLA Ops:
  0.6 41.7 %copy-start = (f32[4096,64]{0,1:T(8,128)S(1)}, f32[4096,64]{0,1:T(8,128)}, u32[]{:S(2)}) copy-start(f32[4096,64]{0,1:T(8,128)} %param.4) | copy-start | bytes 3145732
  5.8 7.6 %collective-permute-start.2 = (f32[128,256]{1,0:T(8,128)}, f32[128,256]{1,0:T(8,128)S(1)}, u32[]{:S(2)}, u32[]{:S(2)}) collective-permute-start(f32[128,256]{1,0:T(8,128)} %get-tuple-element.13), channel_id=1, source_target_pairs={{0,1},{1,0},{2,3},{3,2},{4,5},{5,4},{6,7},{7,6},{8,9},{9,8},{10,11... | collective-permute-start | bytes 393224 | tf_op jit(solution)/shard_map/ppermute | solution.py:334
  6.3 5.4 %collective-permute-start = (bf16[128,256]{1,0:T(8,128)(2,1)}, bf16[128,256]{1,0:T(8,128)(2,1)S(1)}, u32[]{:S(2)}, u32[]{:S(2)}) collective-permute-start(bf16[128,256]{1,0:T(8,128)(2,1)} %get-tuple-element.11), channel_id=1, source_target_pairs={{0,3},{1,2},{2,1},{3,0},{4,7},{5,6},{6,5},{7,4},{8,11},{9,10},{10,... | collective-permute-start | bytes 196616 | tf_op jit(solution)/shard_map/ppermute | solution.py:334
  8.9 4.5 %collective-permute-start.1 = (bf16[128,256]{1,0:T(8,128)(2,1)}, bf16[128,256]{1,0:T(8,128)(2,1)S(1)}, u32[]{:S(2)}, u32[]{:S(2)}) collective-permute-start(bf16[128,256]{1,0:T(8,128)(2,1)} %get-tuple-element.12), channel_id=1, source_target_pairs={{0,2},{1,3},{2,0},{3,1},{4,6},{5,7},{6,4},{7,5},{8,10},{9,11},{10,... | collective-permute-start | bytes 196616 | tf_op jit(solution)/shard_map/ppermute | solution.py:334
  15.1 5.3 %collective-permute-start.3 = (bf16[160,256]{1,0:T(8,128)(2,1)S(1)}, bf16[160,256]{1,0:T(8,128)(2,1)S(1)}, u32[]{:S(2)}, u32[]{:S(2)}) collective-permute-start(bf16[160,256]{1,0:T(8,128)(2,1)S(1)} %pad_maximum_fusion), channel_id=1, source_target_pairs={{0,8},{4,12},{8,0},{12,4},{16,24},{20,28},{24,16},{28,20},{1,9},{5... | collective-permute-start | bytes 245768 | tf_op jit(solution)/shard_map/ppermute | solution.py:334
  16.7 7.6 %collective-permute-start.4 = (bf16[160,256]{1,0:T(8,128)(2,1)S(1)}, bf16[160,256]{1,0:T(8,128)(2,1)S(1)}, u32[]{:S(2)}, u32[]{:S(2)}) collective-permute-start(bf16[160,256]{1,0:T(8,128)(2,1)S(1)} %pad_maximum_fusion), channel_id=1, source_target_pairs={{0,16},{4,20},{8,24},{12,28},{16,0},{20,4},{24,8},{28,12},{1,17},{... | collective-permute-start | bytes 245768 | tf_op jit(solution)/shard_map/ppermute | solution.py:334
  19.3 6.3 %collective-permute-start.5 = (bf16[160,256]{1,0:T(8,128)(2,1)S(1)}, bf16[160,256]{1,0:T(8,128)(2,1)S(1)}, u32[]{:S(2)}, u32[]{:S(2)}) collective-permute-start(bf16[160,256]{1,0:T(8,128)(2,1)S(1)} %pad_maximum_fusion), channel_id=1, source_target_pairs={{0,24},{4,28},{8,16},{12,20},{16,8},{20,12},{24,0},{28,4},{1,25},{... | collective-permute-start | bytes 245768 | tf_op jit(solution)/shard_map/ppermute | solution.py:334
  25.6 7.3 %collective-permute-start.8 = (bf16[640,256]{1,0:T(8,128)(2,1)S(1)}, bf16[640,256]{1,0:T(8,128)(2,1)S(1)}, u32[]{:S(2)}, u32[]{:S(2)}) collective-permute-start(bf16[640,256]{1,0:T(8,128)(2,1)S(1)} %constant_dynamic-update-slice_fusion.refs_0_), channel_id=1, source_target_pairs={{0,2},{1,3},{2,0},{3,1},{4,6},{5,7},{6,4},{7,5},{8,10},{9,11},{10,... | collective-permute-start | bytes 983048 | tf_op jit(solution)/shard_map/ppermute | solution.py:334
  27.1 7.3 %collective-permute-start.7 = (bf16[640,256]{1,0:T(8,128)(2,1)S(1)}, bf16[640,256]{1,0:T(8,128)(2,1)S(1)}, u32[]{:S(2)}, u32[]{:S(2)}) collective-permute-start(bf16[640,256]{1,0:T(8,128)(2,1)S(1)} %constant_dynamic-update-slice_fusion.refs_0_), channel_id=1, source_target_pairs={{0,4},{4,0},{8,12},{12,8},{16,20},{20,16},{24,28},{28,24},{1,5},{5... | collective-permute-start | bytes 983048 | tf_op jit(solution)/shard_map/ppermute | solution.py:334
  28.6 14.0 %collective-permute-start.6 = (bf16[640,256]{1,0:T(8,128)(2,1)S(1)}, bf16[640,256]{1,0:T(8,128)(2,1)S(1)}, u32[]{:S(2)}, u32[]{:S(2)}) collective-permute-start(bf16[640,256]{1,0:T(8,128)(2,1)S(1)} %constant_dynamic-update-slice_fusion.refs_0_), channel_id=1, source_target_pairs={{0,1},{1,0},{2,3},{3,2},{4,5},{5,4},{6,7},{7,6},{8,9},{9,8},{10,11... | collective-permute-start | bytes 983048 | tf_op jit(solution)/shard_map/ppermute | solution.py:334
  32.9 10.0 %collective-permute-start.10 = (bf16[640,256]{1,0:T(8,128)(2,1)S(1)}, bf16[640,256]{1,0:T(8,128)(2,1)S(1)}, u32[]{:S(2)}, u32[]{:S(2)}) collective-permute-start(bf16[640,256]{1,0:T(8,128)(2,1)S(1)} %collective-permute-done.8.refs_1_.refs_3_), channel_id=1, source_target_pairs={{0,1},{1,0},{2,3},{3,2},{4,5},{5,4},{6,7},{7,6},{8,9},{9,8},{10,11... | collective-permute-start | bytes 983048 | tf_op jit(solution)/shard_map/ppermute | solution.py:334
  34.4 8.6 %collective-permute-start.9 = (bf16[640,256]{1,0:T(8,128)(2,1)S(1)}, bf16[640,256]{1,0:T(8,128)(2,1)S(1)}, u32[]{:S(2)}, u32[]{:S(2)}) collective-permute-start(bf16[640,256]{1,0:T(8,128)(2,1)S(1)} %collective-permute-done.7.refs_0_.refs_2_), channel_id=1, source_target_pairs={{0,1},{1,0},{2,3},{3,2},{4,5},{5,4},{6,7},{7,6},{8,9},{9,8},{10,11... | collective-permute-start | bytes 983048 | tf_op jit(solution)/shard_map/ppermute | solution.py:334
  34.4 6.7 %collective-permute-start.11 = (bf16[320,256]{1,0:T(8,128)(2,1)S(1)}, bf16[320,256]{1,0:T(8,128)(2,1)S(1)}, u32[]{:S(2)}, u32[]{:S(2)}) collective-permute-start(bf16[320,256]{1,0:T(8,128)(2,1)S(1)} %slice.8), channel_id=1, source_target_pairs={{0,4},{4,0},{8,12},{12,8},{16,20},{20,16},{24,28},{28,24},{1,5},{5... | collective-permute-start | bytes 491528 | tf_op jit(solution)/shard_map/ppermute | solution.py:334
  35.9 6.4 %collective-permute-start.12 = (bf16[320,256]{1,0:T(8,128)(2,1)S(1)}, bf16[320,256]{1,0:T(8,128)(2,1)S(1)}, u32[]{:S(2)}, u32[]{:S(2)}) collective-permute-start(bf16[320,256]{1,0:T(8,128)(2,1)S(1)} %slice.9), channel_id=1, source_target_pairs={{0,2},{1,3},{2,0},{3,1},{4,6},{5,7},{6,4},{7,5},{8,10},{9,11},{10,... | collective-permute-start | bytes 491528 | tf_op jit(solution)/shard_map/ppermute | solution.py:334
  41.0 2.4 %collective-permute-start.13 = (bf16[320,256]{1,0:T(8,128)(2,1)S(1)}, bf16[320,256]{1,0:T(8,128)(2,1)S(1)}, u32[]{:S(2)}, u32[]{:S(2)}) collective-permute-start(bf16[320,256]{1,0:T(8,128)(2,1)S(1)} %collective-permute-done.11.refs_6_), channel_id=1, source_target_pairs={{0,1},{1,0},{2,3},{3,2},{4,5},{5,4},{6,7},{7,6},{8,9},{9,8},{10,11... | collective-permute-start | bytes 491528 | tf_op jit(solution)/shard_map/ppermute | solution.py:334
  42.3 1.4 %collective-permute-start.14 = (bf16[320,256]{1,0:T(8,128)(2,1)S(1)}, bf16[320,256]{1,0:T(8,128)(2,1)S(1)}, u32[]{:S(2)}, u32[]{:S(2)}) collective-permute-start(bf16[320,256]{1,0:T(8,128)(2,1)S(1)} %collective-permute-done.12.refs_7_), channel_id=1, source_target_pairs={{0,1},{1,0},{2,3},{3,2},{4,5},{5,4},{6,7},{7,6},{8,9},{9,8},{10,11... | collective-permute-start | bytes 491528 | tf_op jit(solution)/shard_map/ppermute | solution.py:334
  57.1 5.6 %collective-permute-start.15 = (bf16[32,2048]{1,0:T(8,128)(2,1)S(1)}, bf16[32,2048]{1,0:T(8,128)(2,1)S(1)}, u32[]{:S(2)}, u32[]{:S(2)}) collective-permute-start(bf16[32,2048]{1,0:T(8,128)(2,1)S(1)} %get-tuple-element.17), channel_id=1, source_target_pairs={{0,4},{4,0},{8,12},{12,8},{16,20},{20,16},{24,28},{28,24},{1,5},{5... | collective-permute-start | bytes 393224 | tf_op jit(solution)/shard_map/ppermute | solution.py:334
